TPU v7x, 32 devices: a whole 2x2x4 slice. The times are simulated.
32 devices in a mesh: grp: 4 (over y, x), mem: 8 (over z, core).
Axes of the slice: x: 2, y: 2, z: 4, core: 2. Of those that a mesh axis runs over, the one named last changes fastest.
Arguments:
- user_rows: bfloat16 [4096, 2048], P(('grp', 'mem')), may hold values from -6 to 6
- projection: bfloat16 [2048, 2048], replicated, may hold values from -0.125 to 0.125
- item_table: bfloat16 [8192, 2048], P(('grp', 'mem')), may hold values from -8 to 8
- positive: int32 [4096], P(('grp', 'mem')), may hold values from 0 to 8191, as said below
- negatives: int32 [4, 1024], P(None, ('grp', 'mem')), may hold values from 0 to 8191, as said below
Outputs:
- user_grad: bfloat16 [4096, 2048], P(('grp', 'mem'))
- item_grad: float32 [8192, 2048], P(('grp', 'mem'))
Inputs may be any that keep to these rules, and one draw needn't show every extreme that they name: `positive`: owner o (grp-major order over grp and mem) holds item rows o * 256 to (o + 1) * 256 - 1. Among the 128 rows of any one device, at most 16 positives lie with any one owner, and one owner receives exactly 16 from every device. `negatives`: in every group, negative j is one of the item rows of owner j // 32.
All inputs are finite; a program needn't handle non-finite values.
Results may differ from a plain program's by a relative error of at most 0.0075.
Values may be sent and summed in bfloat16 or wider, within the bound.
No kernel may reach another device: no remote copies, remote signals or barrier semaphores. Data moves between devices by JAX's collectives and lax.ppermute only.
A program may use at most 64 MiB of HBM per device.

v0:
```python
import functools
import math

import jax
import jax.numpy as jnp
from jax import lax
from jax.experimental import pallas as pl
from jax.experimental.pallas import tpu as pltpu
from jax.sharding import PartitionSpec as P


F32 = jnp.float32
BF16 = jnp.bfloat16
VMEM_LIMIT = 60 * 1024 * 1024
SPARE = 6 * 1024 * 1024
VM = pl.BlockSpec(memory_space=pltpu.VMEM)
SM = pl.BlockSpec(memory_space=pltpu.SMEM)


def dot(a, b, ca=1, cb=0):
    return lax.dot_general(a, b, (((ca,), (cb,)), ((), ())), preferred_element_type=F32)


def chunk_of(width):
    return width if width < 512 else 512


def cost(flops, nbytes):
    return pl.CostEstimate(flops=int(flops), bytes_accessed=int(nbytes), transcendentals=0)


def size_of(shape, dtype):
    return math.prod(shape) * jnp.dtype(dtype).itemsize


def call(kernel, outs, n_smem, args, flops):
    nbytes = sum(size_of(x.shape, x.dtype) for x in args[n_smem:])
    nbytes += sum(size_of(s, t) for s, t in outs)
    return pl.pallas_call(
        kernel,
        out_shape=[jax.ShapeDtypeStruct(s, t) for s, t in outs],
        in_specs=[SM] * n_smem + [VM] * (len(args) - n_smem),
        out_specs=[VM] * len(outs),
        compiler_params=pltpu.CompilerParams(
            vmem_limit_bytes=min(VMEM_LIMIT, nbytes * 3 // 2 + SPARE)
        ),
        cost_estimate=cost(flops, nbytes),
    )(*args)


def project_kernel(x_ref, w_ref, up_ref, down_ref, hidden_ref):
    hidden = dot(x_ref[...], w_ref[...])
    hidden_ref[...] = hidden
    z = (hidden * jax.nn.sigmoid(hidden)).astype(BF16)
    half = up_ref.shape[0]
    up_ref[...] = z[:half]
    down_ref[...] = z[half:]


def project(x, w):
    rows, width = x.shape
    half = rows // 2
    tile = min(width, 1024)
    col = lambda n: pl.BlockSpec((n, tile), lambda i: (0, i))
    return pl.pallas_call(
    project_kernel,
    grid=(width // tile,),
    out_shape=[
        jax.ShapeDtypeStruct((half, width), BF16),
        jax.ShapeDtypeStruct((half, width), BF16),
        jax.ShapeDtypeStruct((rows, width), F32),
    ],
    in_specs=[pl.BlockSpec((rows, width), lambda i: (0, 0)), col(width)],
    out_specs=[col(half), col(half), col(rows)],
    compiler_params=pltpu.CompilerParams(vmem_limit_bytes=VMEM_LIMIT // 3),
    cost_estimate=cost(2 * rows * width * width, 2 * width * width),
    name="project",
    )(x, w)


def hits(ids, first, block):
    lane = lax.broadcasted_iota(jnp.int32, (ids.shape[0], block.shape[0]), 1)
    return ((ids - first) == lane).astype(BF16)


def pick_kernel(n, based, first_ref, ids_ref, neg_ref, *refs):
    blocks = refs[:n]
    base_ref = refs[n] if based else None
    pos_ref, rows_ref = refs[n + based :]
    pick_rows(first_ref, ids_ref, neg_ref, blocks, 1, base_ref, [pos_ref], [rows_ref], [0])


def pick_rows(first_ref, ids_ref, neg_ref, blocks, run, base_ref, pos_refs, row_refs, row_at):
    ids, neg = ids_ref[...], neg_ref[...]
    picks = [hits(ids, first_ref[n], block) for n, block in enumerate(blocks)]
    owners = len(blocks) // run
    each = neg.shape[0] // owners
    neg_picks = [
        hits(neg[n // run * each : (n // run + 1) * each], first_ref[n], block)
        for n, block in enumerate(blocks)
    ]
    width = blocks[0].shape[1]
    step = chunk_of(width)
    cut = ids.shape[0] // len(pos_refs)
    for c in range(0, width, step):
        cols = slice(c, c + step)
        rows = sum(dot(p, block[:, cols]) for p, block in zip(picks, blocks))
        if base_ref is not None:
            rows = rows + base_ref[:, cols].astype(F32)
        rows = rows.astype(BF16)
        for k, pos_ref in enumerate(pos_refs):
            pos_ref[:, cols] = rows[k * cut : (k + 1) * cut]
        for o in range(owners):
            mine = range(o * run, (o + 1) * run)
            got = sum(dot(neg_picks[n], blocks[n][:, cols]) for n in mine)
            at = row_at[0] + o * each
            row_refs[0][at : at + each, cols] = got.astype(BF16)


def scores(scale, z_of, neg_ref, pos_refs, here, logit_ref, pos_out):
    width = neg_ref.shape[1]
    step = chunk_of(width)
    lanes = min(width, 128)
    slot = pos_refs[0].shape[0]
    logits = 0.0
    pos = [jnp.zeros((slot, lanes), F32) for _ in pos_refs]
    for c in range(0, width, step):
        cols = slice(c, c + step)
        z = z_of(cols)
        logits = logits + dot(neg_ref[:, cols], z, 1, 1)
        for k, ref in enumerate(pos_refs):
            prod = z[k * slot : (k + 1) * slot].astype(F32) * ref[:, cols].astype(F32)
            for d in range(0, step, lanes):
                pos[k] = pos[k] + prod[:, d : d + lanes]
    logits = logits * scale
    pos = [scale * jnp.sum(jnp.transpose(p), axis=0, keepdims=True) for p in pos]
    pos = pos[0] if len(pos) == 1 else jnp.concatenate(pos, axis=1)
    top = jnp.max(logits, axis=0, keepdims=True)
    top = jnp.where(here, jnp.maximum(top, pos), top)
    total = jnp.sum(jnp.exp(logits - top), axis=0, keepdims=True)
    total = total + jnp.where(here, jnp.exp(pos - top), 0.0)
    logit_ref[...] = logits
    pos_out[...] = pos
    return top, total


def main_kernel(n, slots, run, scale, first_ref, ids_ref, neg_ref, here_ref, base_ref, *refs):
    early = refs[:2]
    blocks = refs[2 : 2 + n]
    zs = refs[2 + n : 2 + n + 2 * slots]
    rest = refs[2 + n + 2 * slots :]
    pos_refs, (neg_out, logit_ref, pos_out, stat_ref) = rest[: slots + 1], rest[slots + 1 :]
    at = 0
    for e in early:
        neg_out[at : at + e.shape[0]] = e[...]
        at += e.shape[0]
    pick_rows(first_ref, ids_ref, neg_ref, blocks, run, base_ref, pos_refs, [neg_out], [at])

    def z_of(cols):
        return jnp.concatenate([z[:, cols] for z in zs], axis=0)

    users = slots * pos_refs[0].shape[0]
    here = here_ref[:, :users] > 0
    top, total = scores(scale, z_of, neg_out, pos_refs[:slots], here, logit_ref, pos_out)
    stat_ref[0:1] = top
    stat_ref[1:2] = total


def tail_kernel(scale, here_ref, neg_ref, pos_ref, up_ref, down_ref, stat_in, *refs):
    logit_ref, pos_out, stat_ref = refs

    def z_of(cols):
        return jnp.concatenate([up_ref[:, cols], down_ref[:, cols]], axis=0)

    slot = pos_ref.shape[0]
    users = here_ref.shape[1]
    here = here_ref[:, users - slot :] > 0
    top, total = scores(scale, z_of, neg_ref, [pos_ref], here, logit_ref, pos_out)
    stat_ref[:, : users - slot] = stat_in[...]
    stat_ref[0:1, users - slot :] = top
    stat_ref[1:2, users - slot :] = total


def join_kernel(*refs):
    out = refs[-1]
    at = 0
    for r in refs[:-1]:
        out[at : at + r.shape[0]] = r[...]
        at += r.shape[0]


def slot_total(stats, chips, k, slot):
    half = slot // 2
    tops, totals = [], []
    for s in range(chips):
        up = (k - s) % chips * slot
        down = (k + s) % chips * slot + half
        stat = jnp.concatenate(
            [stats[s][:, up : up + half], stats[s][:, down : down + half]], axis=1
        )
        tops.append(stat[0:1])
        totals.append(stat[1:2])
    peak = functools.reduce(jnp.maximum, tops)
    return peak + jnp.log(sum(t * jnp.exp(m - peak) for m, t in zip(tops, totals)))


def slot_weights(stats, chips, k, slot, logit, pos, here):
    log_total = slot_total(stats, chips, k, slot)
    prob = jnp.exp(logit - log_total).astype(BF16)
    weight = jnp.where(here > 0, jnp.exp(pos - log_total) - 1.0, 0.0)
    return prob, weight


def slot_grad(scale, prob, weight, neg_ref, pos_ref, up_ref, down_ref):
    slot, width = pos_ref.shape
    half = slot // 2
    column = jnp.transpose(jnp.broadcast_to(weight, (128, slot)))[:, 0:1]
    prob = jnp.transpose(prob.astype(F32)).astype(BF16)
    step = chunk_of(width)
    for c in range(0, width, step):
        cols = slice(c, c + step)
        grad = dot(prob, neg_ref[:, cols]) + column * pos_ref[:, cols].astype(F32)
        grad = scale * grad
        up_ref[:, cols] = grad[:half].astype(up_ref.dtype)
        down_ref[:, cols] = grad[half:].astype(down_ref.dtype)


def lead_kernel(chips, scale, here_ref, logit_ref, pos_ref, neg_ref, rows_ref, *refs):
    stats, (up_ref, down_ref) = refs[:chips], refs[chips:]
    slot = rows_ref.shape[0]
    lanes = slice(slot, 2 * slot)
    prob, weight = slot_weights(
        stats, chips, 1, slot, logit_ref[:, lanes], pos_ref[:, lanes], here_ref[:, lanes]
    )
    slot_grad(scale, prob, weight, neg_ref, rows_ref, up_ref, down_ref)


def rest_kernel(chips, scale, order, each, here_ref, logit_ref, pos_ref, logit_t, pos_t, *refs):
    neg_ref, refs = refs[0], refs[1:]
    rows, refs = refs[: chips - 1], refs[chips - 1 :]
    stats, refs = refs[:chips], refs[chips:]
    own_ref, other_ref, weight_ref = refs[:3]
    parts = refs[3:]
    slot = rows[0].shape[0]
    at = 0
    for k in range(chips):
        lanes = slice(k * slot, (k + 1) * slot)
        last = k == chips - 1
        logit = logit_t[...] if last else logit_ref[:, lanes]
        pos = pos_t[...] if last else pos_ref[:, lanes]
        prob, weight = slot_weights(stats, chips, k, slot, logit, pos, here_ref[:, lanes])
        weight_ref[:, lanes] = weight
        for n, (side, owner) in enumerate(order):
            to = other_ref if side else own_ref
            to[owner * each : (owner + 1) * each, lanes] = prob[n * each : (n + 1) * each]
        if k != 1:
            slot_grad(scale, prob, weight, neg_ref, rows[at], parts[2 * at], parts[2 * at + 1])
            at += 1


def item_kernel(scale, first_ref, neg_ref, *refs):
    sides = [refs[4 * s : 4 * s + 4] for s in range(2)]
    outs = refs[8:]
    own_rows = sum(o.shape[0] for o in outs)
    width = outs[0].shape[1]
    first = first_ref[0]
    neg = neg_ref[...] - first
    pick = lax.broadcasted_iota(jnp.int32, (own_rows, neg.shape[1]), 0) == neg
    pick = pick.astype(F32).astype(BF16)
    weights = []
    for ids_ref, prob_ref, weight_ref, _ in sides:
        ids = ids_ref[...] - first
        row = lax.broadcasted_iota(jnp.int32, (own_rows, ids.shape[1]), 0)
        w = dot(pick, prob_ref[...]) + jnp.where(row == ids, weight_ref[...], 0.0)
        weights.append(w.astype(BF16))
    step = chunk_of(width)
    for c in range(0, width, step):
        cols = slice(c, c + step)
        grad = scale * sum(dot(w, side[3][:, cols]) for w, side in zip(weights, sides))
        at = 0
        for o in outs:
            o[:, cols] = grad[at : at + o.shape[0]].astype(o.dtype)
            at += o.shape[0]


def finish_kernel(up_ref, up_in_ref, down_ref, down_in_ref, hidden_ref, w_ref, out_ref, gh_ref):
    @pl.when(pl.program_id(0) == 0)
    def _():
        half = up_ref.shape[0]
        for at, a, b in ((0, up_ref, up_in_ref), (half, down_ref, down_in_ref)):
            hidden = hidden_ref[at : at + half]
            s = jax.nn.sigmoid(hidden)
            slope = s * (1.0 + hidden * (1.0 - s))
            gh_ref[at : at + half] = ((a[...] + b[...].astype(F32)) * slope).astype(BF16)

    out_ref[...] = dot(gh_ref[...], w_ref[...], 1, 1).astype(BF16)


def finish(up, up_in, down, down_in, hidden, w):
    rows, width = hidden.shape
    tile = min(width, 1024)
    whole = lambda n: pl.BlockSpec((n, width), lambda i: (0, 0))
    return pl.pallas_call(
        finish_kernel,
        grid=(width // tile,),
        out_shape=jax.ShapeDtypeStruct((rows, width), BF16),
        in_specs=[whole(rows // 2)] * 4
        + [whole(rows), pl.BlockSpec((tile, width), lambda i: (i, 0))],
        out_specs=pl.BlockSpec((rows, tile), lambda i: (0, i)),
        scratch_shapes=[pltpu.VMEM((rows, width), BF16)],
        compiler_params=pltpu.CompilerParams(vmem_limit_bytes=VMEM_LIMIT // 3),
        cost_estimate=cost(2 * rows * width * width, 2 * width * width),
        name="finish",
    )(up, up_in, down, down_in, hidden, w)


def ring_shift(x, step, chips):
    perm = [
        (chip * 2 + core, (chip + step) % chips * 2 + core)
        for chip in range(chips)
        for core in range(2)
    ]
    return lax.ppermute(x, "mem", perm)


def core_swap(x, members):
    return lax.ppermute(x, "mem", [(m, m ^ 1) for m in range(members)])


def group_swap(x, bits, groups):
    return lax.ppermute(x, "grp", [(g, g ^ bits) for g in range(groups)])


def low_bit(k):
    return k & -k


def on_device(user_rows, projection, item_table, positive, negatives):
    groups = lax.axis_size("grp")
    members = lax.axis_size("mem")
    chips = members // 2
    rows_here, width = user_rows.shape
    half = rows_here // 2
    users = chips * rows_here
    own_rows = item_table.shape[0]
    mid = own_rows // 2
    neg_rows = negatives.shape[1]
    scale = 4.0 / math.sqrt(width)
    g = lax.axis_index("grp")
    m = lax.axis_index("mem")
    single = [k for k in range(1, groups) if low_bit(k) == k]
    double = [k for k in range(1, groups) if low_bit(k) != k]

    block = {0: [(0, item_table)]}
    for k in single:
        block[k] = [(0, group_swap(item_table, k, groups))]
    z_up, z_down, hidden = project(user_rows, projection)
    z_ups, z_downs = [z_up], [z_down]
    for _ in range(1, chips):
        z_ups.append(ring_shift(z_ups[-1], 1, chips))
        z_downs.append(ring_shift(z_downs[-1], -1, chips))
    z_slots = [z for pair in zip(z_ups, z_downs) for z in pair]
    ids_in = [positive] + [ring_shift(positive, k, chips) for k in range(1, chips)]
    ids = jnp.concatenate(
        [x for k in range(chips) for x in (ids_in[k][:half], ids_in[-k % chips][half:])]
    )
    neg_own = [jnp.take(negatives, g, axis=0)]
    for k in range(1, groups):
        neg_own.append(group_swap(jnp.take(negatives, g ^ k, axis=0), k, groups))
    id_sib = core_swap(jnp.concatenate([ids] + neg_own), members)
    ids_other = id_sib[:users]
    neg_other = [id_sib[users + k * neg_rows : users + (k + 1) * neg_rows] for k in range(groups)]
    for k in double:
        low = low_bit(k)
        rest = k ^ low
        block[k] = [
            (0, group_swap(block[rest][0][1][:mid], low, groups)),
            (mid, group_swap(block[low][0][1][mid:], rest, groups)),
        ]

    def first_of(k, member):
        return ((g ^ k) * members + member) * own_rows

    order = []

    def stage(ks):
        firsts, rows, negs = [], [], []
        for side in range(2):
            for k in ks:
                order.append((side, k))
                negs.append(neg_other[k] if side else neg_own[k])
                for at, piece in block[k]:
                    firsts.append(first_of(k, m ^ 1 if side else m) + at)
                    rows.append(core_swap(piece, members) if side else piece)
        return jnp.stack(firsts).astype(jnp.int32), jnp.concatenate(negs)[:, None], rows

    sel = ids[:, None]
    here = ((ids // (2 * own_rows)) % chips == m // 2).astype(jnp.int32)[None]
    slots = chips - 1
    base, early = None, []
    for ks in ([0], single):
        firsts, neg_ids, rows = stage(ks)
        base, got_rows = call(
            functools.partial(pick_kernel, len(rows), int(base is not None)),
            [((users, width), BF16), ((neg_ids.shape[0], width), BF16)],
            1,
            [firsts, sel, neg_ids] + rows + ([] if base is None else [base]),
            2 * users * width * own_rows * len(rows),
        )
        early.append(got_rows)
    firsts, neg_ids, rows = stage(double)
    negs = 2 * groups * neg_rows
    out = call(
        functools.partial(main_kernel, len(rows), slots, 2, scale),
        [((rows_here, width), BF16)] * chips
        + [
            ((negs, width), BF16),
            ((negs, slots * rows_here), F32),
            ((1, slots * rows_here), F32),
            ((2, slots * rows_here), F32),
        ],
        1,
        [firsts, sel, neg_ids, here, base] + early + rows + z_slots[: 2 * slots],
        2 * users * width * mid * len(rows) + 2 * users * negs * width,
    )
    pos_rows, (neg_all, logits, pos, stat) = out[:chips], out[chips:]
    logits_t, pos_t, stat = call(
        functools.partial(tail_kernel, scale),
        [((negs, rows_here), F32), ((1, rows_here), F32), ((2, users), F32)],
        0,
        [here, neg_all, pos_rows[-1]] + z_slots[2 * slots :] + [stat],
        2 * rows_here * negs * width,
    )
    stats = [stat] + [ring_shift(stat, k, chips) for k in range(1, chips)]
    (z_all,) = call(join_kernel, [((users, width), BF16)], 0, z_slots, users * width)
    z_other = core_swap(z_all, members)
    mine = groups * neg_rows
    part = [None] * chips
    part[1] = call(
        functools.partial(lead_kernel, chips, scale),
        [((half, width), BF16)] * 2,
        0,
        [here, logits, pos, neg_all, pos_rows[1]] + stats,
        2 * rows_here * negs * width,
    )
    others = [k for k in range(chips) if k != 1]
    out = call(
        functools.partial(rest_kernel, chips, scale, tuple(order), neg_rows),
        [((mine, users), BF16), ((mine, users), BF16), ((1, users), F32)]
        + [((half, width), BF16 if k else F32) for k in others for _ in range(2)],
        0,
        [here, logits, pos, logits_t, pos_t, neg_all] + [pos_rows[k] for k in others] + stats,
        2 * users * negs * width,
    )
    prob, prob_out, weight = out[:3]
    for n, k in enumerate(others):
        part[k] = out[3 + 2 * n : 5 + 2 * n]
    prob_in = core_swap(prob_out, members)
    weight_in = core_swap(weight, members)

    def item_part(k, kinds):
        args = [
            first_of(k, m).reshape(1).astype(jnp.int32),
            neg_own[k][None],
            ids[None],
            prob[k * neg_rows : (k + 1) * neg_rows],
            weight,
            z_all,
            ids_other[None],
            prob_in[k * neg_rows : (k + 1) * neg_rows],
            weight_in,
            z_other,
        ]
        return call(
            functools.partial(item_kernel, scale),
            [((n, width), t) for n, t in kinds],
            1,
            args,
            4 * own_rows * users * width,
        )

    def ring_sum(side, step):
        moving = part[1][side]
        for k in range(2, chips):
            moving = ring_shift(moving, step, chips)
            moving = (part[k][side].astype(F32) + moving.astype(F32)).astype(BF16)
        return ring_shift(moving, step, chips)

    up_in = ring_sum(0, 1)
    down_in = ring_sum(1, -1)

    sums = {}
    for k in double + single:
        sums[k] = item_part(k, [(mid, BF16), (mid, BF16)])
    (total,) = item_part(0, [(own_rows, F32)])
    for k in double:
        low = low_bit(k)
        rest = k ^ low
        a = group_swap(sums[k][0], low, groups)
        b = group_swap(sums[k][1], rest, groups)
        sums[rest] = [(sums[rest][0].astype(F32) + a.astype(F32)).astype(BF16), sums[rest][1]]
        sums[low] = [sums[low][0], (sums[low][1].astype(F32) + b.astype(F32)).astype(BF16)]
    got = {}
    for k in single:
        got[k] = [group_swap(piece, k, groups) for piece in sums[k]]
    item_grad = total + sum(jnp.concatenate(got[k]).astype(F32) for k in single)
    user_grad = finish(part[0][0], up_in, part[0][1], down_in, hidden, projection)
    return (user_grad, item_grad)


def solution(mesh):
    owners = ("grp", "mem")

    return jax.shard_map(
        on_device,
        mesh=mesh,
        in_specs=(P(owners, None), P(), P(owners, None), P(owners), P(None, owners)),
        out_specs=(P(owners, None), P(owners, None)),
        check_vma=False,
    )
```

profile of v0, /device:TPU:0, one launch (start us, length us, event | category | flops | bytes accessed | tf_op | source)
XLA Modules:
  0.0 176.6 jit_solution(3884094848948334625)
XLA Ops:
  0.6 3.0 %collective-permute-start.7 = (bf16[256,2048]{1,0:T(8,128)(2,1)}, bf16[256,2048]{1,0:T(8,128)(2,1)}, u32[]{:S(2)}, u32[]{:S(2)}) collective-permute-start(bf16[256,2048]{1,0:T(8,128)(2,1)} %refs_0_.1), channel_id=1, source_target_pairs={{0,8},{8,0},{16,24},{24,16},{1,9},{9,1},{17,25},{25,17},{2,10},{10... | collective-permute-start | bytes 3145736 | tf_op jit(solution)/shard_map/ppermute | solution.py:331
  3.7 1.5 collective-permute-start.8
  5.2 3.4 %copy-done = bf16[2048,2048]{1,0:T(8,128)(2,1)S(1)} copy-done((bf16[2048,2048]{1,0:T(8,128)(2,1)S(1)}, bf16[2048,2048]{1,0:T(8,128)(2,1)}, u32[]{:S(2)}) %copy-start) | copy-done | bytes 8388632
  8.6 1.0 copy-done.14
  9.6 2.2 %project.1 = (bf16[64,2048]{1,0:T(8,128)(2,1)S(1)}, bf16[64,2048]{1,0:T(8,128)(2,1)S(1)}, f32[128,2048]{1,0:T(8,128)S(1)}) custom-call(bf16[128,2048]{1,0:T(8,128)(2,1)S(1)} %copy-done.14, bf16[2048,2048]{1,0:T(8,128)(2,1)S(1)} %copy-done), custom_call_target="tpu_custom_call" | custom-call | flops 1073741824 | bytes 8388608 | tf_op jit(solution)/shard_map/project/pallas_call | solution.py:65
  12.7 1.6 collective-permute-start.16
  14.3 2.2 %collective-permute-start.17 = (bf16[64,2048]{1,0:T(8,128)(2,1)S(1)}, bf16[64,2048]{1,0:T(8,128)(2,1)S(1)}, u32[]{:S(2)}, u32[]{:S(2)}) collective-permute-start(bf16[64,2048]{1,0:T(8,128)(2,1)S(1)} %get-tuple-element.43.refs_7_.refs_1_), channel_id=1, source_target_pairs={{0,6},{1,7},{2,0},{3,1},{4,2},{5,3},{6,4},{7,5},{8,14},{9,15},{10,... | collective-permute-start | bytes 786440 | tf_op jit(solution)/shard_map/ppermute | solution.py:323
  17.2 9.9 %collective-permute-done.4 = s32[32]{0:T(128)S(1)} collective-permute-done((s32[32]{0:T(128)S(1)}, s32[32]{0:T(128)S(1)}, u32[]{:S(2)}, u32[]{:S(2)}) %collective-permute-start.4) | collective-permute-done | bytes 160 | tf_op jit(solution)/shard_map/ppermute | solution.py:331
  27.1 1.8 collective-permute-start.5
  28.9 1.8 %collective-permute-done.5 = s32[32]{0:T(128)S(1)} collective-permute-done((s32[32]{0:T(128)S(1)}, s32[32]{0:T(128)S(1)}, u32[]{:S(2)}, u32[]{:S(2)}) %collective-permute-start.5) | collective-permute-done | bytes 160 | tf_op jit(solution)/shard_map/ppermute | solution.py:331
  30.7 2.7 %collective-permute-start.3 = (s32[32]{0:T(128)S(1)}, s32[32]{0:T(128)S(1)}, u32[]{:S(2)}, u32[]{:S(2)}) collective-permute-start(s32[32]{0:T(128)S(1)} %get-tuple-element.94), channel_id=1, source_target_pairs={{0,24},{8,16},{16,8},{24,0},{1,25},{9,17},{17,9},{25,1},{2,26},{10... | collective-permute-start | bytes 392 | tf_op jit(solution)/shard_map/ppermute | solution.py:331
  33.4 1.8 %collective-permute-done.3 = s32[32]{0:T(128)S(1)} collective-permute-done((s32[32]{0:T(128)S(1)}, s32[32]{0:T(128)S(1)}, u32[]{:S(2)}, u32[]{:S(2)}) %collective-permute-start.3) | collective-permute-done | bytes 160 | tf_op jit(solution)/shard_map/ppermute | solution.py:331
  35.2 1.8 %collective-permute-start = (s32[128]{0:T(128)S(1)}, s32[128]{0:T(128)S(1)}, u32[]{:S(2)}, u32[]{:S(2)}) collective-permute-start(s32[128]{0:T(128)S(1)} %copy-done.22), channel_id=1, source_target_pairs={{0,2},{1,3},{2,4},{3,5},{4,6},{5,7},{6,0},{7,1},{8,10},{9,11},{10,... | collective-permute-start | bytes 1544 | tf_op jit(solution)/shard_map/ppermute | solution.py:323
  37.0 3.6 %collective-permute-done = s32[128]{0:T(128)S(1)} collective-permute-done((s32[128]{0:T(128)S(1)}, s32[128]{0:T(128)S(1)}, u32[]{:S(2)}, u32[]{:S(2)}) %collective-permute-start) | collective-permute-done | bytes 544 | tf_op jit(solution)/shard_map/ppermute | solution.py:323
  40.6 2.0 %collective-permute-start.1 = (s32[128]{0:T(128)S(1)}, s32[128]{0:T(128)S(1)}, u32[]{:S(2)}, u32[]{:S(2)}) collective-permute-start(s32[128]{0:T(128)S(1)} %copy-done.22), channel_id=1, source_target_pairs={{0,6},{1,7},{2,0},{3,1},{4,2},{5,3},{6,4},{7,5},{8,14},{9,15},{10,... | collective-permute-start | bytes 1544 | tf_op jit(solution)/shard_map/ppermute | solution.py:323
  42.7 1.5 collective-permute-done.1
  45.2 3.4 %collective-permute-start.18 = (bf16[64,2048]{1,0:T(8,128)(2,1)S(1)}, bf16[64,2048]{1,0:T(8,128)(2,1)S(1)}, u32[]{:S(2)}, u32[]{:S(2)}) collective-permute-start(bf16[64,2048]{1,0:T(8,128)(2,1)S(1)} %collective-permute-done.16.refs_8_.refs_2_), channel_id=1, source_target_pairs={{0,2},{1,3},{2,4},{3,5},{4,6},{5,7},{6,0},{7,1},{8,10},{9,11},{10,... | collective-permute-start | bytes 786440 | tf_op jit(solution)/shard_map/ppermute | solution.py:323
  49.2 1.2 collective-permute-done.6
  50.5 3.0 %collective-permute-done.18.refs_10_.refs_4_ = bf16[64,2048]{1,0:T(8,128)(2,1)S(1)} collective-permute-done((bf16[64,2048]{1,0:T(8,128)(2,1)S(1)}, bf16[64,2048]{1,0:T(8,128)(2,1)S(1)}, u32[]{:S(2)}, u32[]{:S(2)}) %collective-permute-start.18) | collective-permute-done | bytes 262176 | tf_op jit(solution)/shard_map/ppermute | solution.py:323
  53.5 1.4 collective-permute-start.20
  54.9 7.2 %collective-permute-done.19.refs_11_.refs_5_ = bf16[64,2048]{1,0:T(8,128)(2,1)S(1)} collective-permute-done((bf16[64,2048]{1,0:T(8,128)(2,1)S(1)}, bf16[64,2048]{1,0:T(8,128)(2,1)S(1)}, u32[]{:S(2)}, u32[]{:S(2)}) %collective-permute-start.19) | collective-permute-done | bytes 262176 | tf_op jit(solution)/shard_map/ppermute | solution.py:323
  65.7 1.9 %slice.89 = bf16[128,2048]{1,0:T(8,128)(2,1)} slice(bf16[256,2048]{1,0:T(8,128)(2,1)} %collective-permute-done.8.refs_1_), slice={[0:128], [0:2048]} | slice | bytes 1048576 | tf_op jit(solution)/shard_map/slice | solution.py:377
  67.6 1.9 %slice.90 = bf16[128,2048]{1,0:T(8,128)(2,1)} slice(bf16[256,2048]{1,0:T(8,128)(2,1)} %collective-permute-done.7.refs_0_), slice={[128:256], [0:2048]} | slice | bytes 1048576 | tf_op jit(solution)/shard_map/slice | solution.py:378
  70.2 1.5 collective-permute-start.12
  72.4 1.5 collective-permute-start.13
  77.4 7.0 %collective-permute-done.12.refs_2_ = bf16[128,2048]{1,0:T(8,128)(2,1)} collective-permute-done((bf16[128,2048]{1,0:T(8,128)(2,1)}, bf16[128,2048]{1,0:T(8,128)(2,1)}, u32[]{:S(2)}, u32[]{:S(2)}) %collective-permute-start.12) | collective-permute-done | bytes 524320 | tf_op jit(solution)/shard_map/ppermute | solution.py:331
  84.4 1.9 %collective-permute-done.13.refs_3_ = bf16[128,2048]{1,0:T(8,128)(2,1)} collective-permute-done((bf16[128,2048]{1,0:T(8,128)(2,1)}, bf16[128,2048]{1,0:T(8,128)(2,1)}, u32[]{:S(2)}, u32[]{:S(2)}) %collective-permute-start.13) | collective-permute-done | bytes 524320 | tf_op jit(solution)/shard_map/ppermute | solution.py:331
  89.5 3.3 %shard_map.68 = (bf16[512,2048]{1,0:T(8,128)(2,1)S(1)}, bf16[64,2048]{1,0:T(8,128)(2,1)S(1)}) custom-call(s32[2]{0:T(128)S(1)} %copy-done.21, s32[512,1]{1,0:T(8,128)S(1)} %copy-done.4, s32[64,1]{1,0:T(8,128)S(1)} %copy.11.neg_ref, bf16[256,2048]{1,0:T(8,128)(2,1)} %refs_0_.1, bf16[256,2048]{1,0:T(8,128)(2,1)} %collective-permute-done.11.refs_1_), custom_call_target="tpu_custom_call" | custom-call | flops 1073741824 | bytes 4458752 | tf_op jit(solution)/shard_map/pallas_call | solution.py:39
  93.5 5.4 %shard_map.69 = (bf16[512,2048]{1,0:T(8,128)(2,1)S(1)}, bf16[128,2048]{1,0:T(8,128)(2,1)S(1)}) custom-call(s32[4]{0:T(128)S(1)} %copy-done.20, s32[512,1]{1,0:T(8,128)S(1)} %copy-done.5, s32[128,1]{1,0:T(8,128)S(1)} %copy.13.neg_ref, bf16[256,2048]{1,0:T(8,128)(2,1)} %collective-permute-done.7.refs_0_, bf16[256,2048]{1,0:T(8,128)(2,1)} %collective-permute-done.8.refs_1_, ...), custom_call_target="tpu_custom_call" | custom-call | flops 2147483648 | bytes 8915456 | tf_op jit(solution)/shard_map/pallas_call | solution.py:39
  98.9 5.1 %shard_map.70 = (bf16[128,2048]{1,0:T(8,128)(2,1)S(1)}, bf16[128,2048]{1,0:T(8,128)(2,1)S(1)}, bf16[128,2048]{1,0:T(8,128)(2,1)S(1)}, bf16[128,2048]{1,0:T(8,128...) custom-call(s32[4]{0:T(128)S(1)} %copy-done.19, ...), custom_call_target="tpu_custom_call" | custom-call | flops 1610612736 | bytes 10101504 | tf_op jit(solution)/shard_map/pallas_call | solution.py:39
  104.6 1.9 %collective-permute-start.22 = (f32[2,512]{1,0:T(2,128)S(1)}, f32[2,512]{1,0:T(2,128)S(1)}, u32[]{:S(2)}, u32[]{:S(2)}) collective-permute-start(f32[2,512]{1,0:T(2,128)S(1)} %get-tuple-element.53.refs_4_.refs_0_), channel_id=1, source_target_pairs={{0,2},{1,3},{2,4},{3,5},{4,6},{5,7},{6,0},{7,1},{8,10},{9,11},{10,... | collective-permute-start | bytes 12296 | tf_op jit(solution)/shard_map/ppermute | solution.py:323
  106.5 2.4 %collective-permute-start.24 = (f32[2,512]{1,0:T(2,128)S(1)}, f32[2,512]{1,0:T(2,128)S(1)}, u32[]{:S(2)}, u32[]{:S(2)}) collective-permute-start(f32[2,512]{1,0:T(2,128)S(1)} %get-tuple-element.53.refs_4_.refs_0_), channel_id=1, source_target_pairs={{0,6},{1,7},{2,0},{3,1},{4,2},{5,3},{6,4},{7,5},{8,14},{9,15},{10,... | collective-permute-start | bytes 12296 | tf_op jit(solution)/shard_map/ppermute | solution.py:323
  109.0 1.1 collective-permute-done.22.refs_5_.refs_1_
  111.4 1.7 collective-permute-start.25
  113.1 2.2 %collective-permute-start.28 = (bf16[64,2048]{1,0:T(8,128)(2,1)S(1)}, bf16[64,2048]{1,0:T(8,128)(2,1)S(1)}, u32[]{:S(2)}, u32[]{:S(2)}) collective-permute-start(bf16[64,2048]{1,0:T(8,128)(2,1)S(1)} %get-tuple-element.62), channel_id=1, source_target_pairs={{0,6},{1,7},{2,0},{3,1},{4,2},{5,3},{6,4},{7,5},{8,14},{9,15},{10,... | collective-permute-start | bytes 786440 | tf_op jit(solution)/shard_map/ppermute | solution.py:323
  117.6 4.8 %collective-permute-done.25 = bf16[64,2048]{1,0:T(8,128)(2,1)S(1)} collective-permute-done((bf16[64,2048]{1,0:T(8,128)(2,1)S(1)}, bf16[64,2048]{1,0:T(8,128)(2,1)S(1)}, u32[]{:S(2)}, u32[]{:S(2)}) %collective-permute-start.25) | collective-permute-done | bytes 262176 | tf_op jit(solution)/shard_map/ppermute | solution.py:323
  122.6 3.7 %collective-permute-done.28 = bf16[64,2048]{1,0:T(8,128)(2,1)S(1)} collective-permute-done((bf16[64,2048]{1,0:T(8,128)(2,1)S(1)}, bf16[64,2048]{1,0:T(8,128)(2,1)S(1)}, u32[]{:S(2)}, u32[]{:S(2)}) %collective-permute-start.28) | collective-permute-done | bytes 262176 | tf_op jit(solution)/shard_map/ppermute | solution.py:323
  126.4 3.5 %collective-permute-start.29 = (bf16[64,2048]{1,0:T(8,128)(2,1)S(1)}, bf16[64,2048]{1,0:T(8,128)(2,1)S(1)}, u32[]{:S(2)}, u32[]{:S(2)}) collective-permute-start(bf16[64,2048]{1,0:T(8,128)(2,1)S(1)} %add_convert_fusion.3), channel_id=1, source_target_pairs={{0,6},{1,7},{2,0},{3,1},{4,2},{5,3},{6,4},{7,5},{8,14},{9,15},{10,... | collective-permute-start | bytes 786440 | tf_op jit(solution)/shard_map/ppermute | solution.py:323
  129.9 3.0 %shard_map.77 = (bf16[128,2048]{1,0:T(8,128)(2,1)S(1)}, bf16[128,2048]{1,0:T(8,128)(2,1)S(1)}) custom-call(s32[1]{0:T(128)} %bitcast.6.first_ref, s32[1,32]{1,0:T(1,128)S(1)} %bitcast.54, s32[1,512]{1,0:T(1,128)S(1)} %bitcast.42, bf16[32,512]{1,0:T(8,128)(2,1)S(1)} %get-tuple-element.89.refs_1_, f32[1,512]{1,0:T(1,128)S(1)} %get-tuple-element.65.refs_2_, ...), custom_call_target="tpu_custom_call" | custom-call | flops 1073741824 | bytes 5316736 | tf_op jit(solution)/shard_map/pallas_call | solution.py:39
  132.9 1.6 collective-permute-start.35
  134.7 3.2 %shard_map.76 = (bf16[128,2048]{1,0:T(8,128)(2,1)S(1)}, bf16[128,2048]{1,0:T(8,128)(2,1)S(1)}) custom-call(s32[1]{0:T(128)} %bitcast.16.first_ref, s32[1,32]{1,0:T(1,128)S(1)} %bitcast.51, s32[1,512]{1,0:T(1,128)S(1)} %bitcast.43, bf16[32,512]{1,0:T(8,128)(2,1)S(1)} %get-tuple-element.90.refs_1_, f32[1,512]{1,0:T(1,128)S(1)} %get-tuple-element.65.refs_2_, ...), custom_call_target="tpu_custom_call" | custom-call | flops 1073741824 | bytes 5316736 | tf_op jit(solution)/shard_map/pallas_call | solution.py:39
  138.5 1.5 collective-permute-start.37
  140.0 3.0 %shard_map.78 = (bf16[128,2048]{1,0:T(8,128)(2,1)S(1)}, bf16[128,2048]{1,0:T(8,128)(2,1)S(1)}) custom-call(s32[1]{0:T(128)} %bitcast.17.first_ref, s32[1,32]{1,0:T(1,128)S(1)} %bitcast.50, s32[1,512]{1,0:T(1,128)S(1)} %bitcast.44, bf16[32,512]{1,0:T(8,128)(2,1)S(1)} %get-tuple-element.88.refs_1_, f32[1,512]{1,0:T(1,128)S(1)} %get-tuple-element.65.refs_2_, ...), custom_call_target="tpu_custom_call" | custom-call | flops 1073741824 | bytes 5316736 | tf_op jit(solution)/shard_map/pallas_call | solution.py:39
  144.1 17.1 %collective-permute-done.37 = bf16[128,2048]{1,0:T(8,128)(2,1)S(1)} collective-permute-done((bf16[128,2048]{1,0:T(8,128)(2,1)S(1)}, bf16[128,2048]{1,0:T(8,128)(2,1)S(1)}, u32[]{:S(2)}, u32[]{:S(2)}) %collective-permute-start.37) | collective-permute-done | bytes 524320 | tf_op jit(solution)/shard_map/ppermute | solution.py:331
  163.0 3.8 %collective-permute-start.30 = (bf16[64,2048]{1,0:T(8,128)(2,1)S(1)}, bf16[64,2048]{1,0:T(8,128)(2,1)S(1)}, u32[]{:S(2)}, u32[]{:S(2)}) collective-permute-start(bf16[64,2048]{1,0:T(8,128)(2,1)S(1)} %add_convert_fusion.2), channel_id=1, source_target_pairs={{0,6},{1,7},{2,0},{3,1},{4,2},{5,3},{6,4},{7,5},{8,14},{9,15},{10,... | collective-permute-start | bytes 786440 | tf_op jit(solution)/shard_map/ppermute | solution.py:323
  166.9 3.1 %shard_map.75 = f32[256,2048]{1,0:T(8,128)S(1)} custom-call(s32[1]{0:T(128)} %bitcast.21.first_ref, s32[1,32]{1,0:T(1,128)S(1)} %copy-done.16, s32[1,512]{1,0:T(1,128)S(1)} %bitcast.45, bf16[32,512]{1,0:T(8,128)(2,1)S(1)} %get-tuple-element.91.refs_1_, f32[1,512]{1,0:T(1,128)S(1)} %get-tuple-element.65.refs_2_, bf16[512,2048]{1,0:T(8,128)(2,1)S(1)} %shard_map.74.refs_3_, ...), custom_call_target="tpu_custom_call" | custom-call | flops 1073741824 | bytes 6365312 | tf_op jit(solution)/shard_map/pallas_call | solution.py:39
  170.7 4.1 %finish.1 = bf16[128,2048]{1,0:T(8,128)(2,1)} custom-call(f32[64,2048]{1,0:T(8,128)S(1)} %get-tuple-element.54.up_ref, bf16[64,2048]{1,0:T(8,128)(2,1)S(1)} %collective-permute-done.27.up_in_ref, f32[64,2048]{1,0:T(8,128)S(1)} %get-tuple-element.59.down_ref, bf16[64,2048]{1,0:T(8,128)(2,1)S(1)} %collective-permute-done.30.down_in_ref, ...), custom_call_target="tpu_custom_call" | custom-call | flops 1073741824 | bytes 8388608 | tf_op jit(solution)/shard_map/finish/pallas_call | solution.py:303
  174.8 1.8 add_add_fusion
  (133 shorter events, 24.4 us)
Async XLA Ops:
  0.6 62.3 %collective-permute-start.7 = (bf16[256,2048]{1,0:T(8,128)(2,1)}, bf16[256,2048]{1,0:T(8,128)(2,1)}, u32[]{:S(2)}, u32[]{:S(2)}) collective-permute-start(bf16[256,2048]{1,0:T(8,128)(2,1)} %refs_0_.1), channel_id=1, source_target_pairs={{0,8},{8,0},{16,24},{24,16},{1,9},{9,1},{17,25},{25,17},{2,10},{10... | collective-permute-start | bytes 3145736 | tf_op jit(solution)/shard_map/ppermute | solution.py:331
  3.7 59.3 %collective-permute-start.8 = (bf16[256,2048]{1,0:T(8,128)(2,1)}, bf16[256,2048]{1,0:T(8,128)(2,1)}, u32[]{:S(2)}, u32[]{:S(2)}) collective-permute-start(bf16[256,2048]{1,0:T(8,128)(2,1)} %refs_0_.1), channel_id=1, source_target_pairs={{0,16},{8,24},{16,0},{24,8},{1,17},{9,25},{17,1},{25,9},{2,18},{10... | collective-permute-start | bytes 3145736 | tf_op jit(solution)/shard_map/ppermute | solution.py:331
  9.6 25.6 %copy-start.22 = (s32[128]{0:T(128)S(1)}, s32[128]{0:T(128)}, u32[]{:S(2)}) copy-start(s32[128]{0:T(128)} %param.10) | copy-start | bytes 1540
  12.7 32.4 %collective-permute-start.16 = (bf16[64,2048]{1,0:T(8,128)(2,1)S(1)}, bf16[64,2048]{1,0:T(8,128)(2,1)S(1)}, u32[]{:S(2)}, u32[]{:S(2)}) collective-permute-start(bf16[64,2048]{1,0:T(8,128)(2,1)S(1)} %get-tuple-element.42.refs_6_.refs_0_), channel_id=1, source_target_pairs={{0,2},{1,3},{2,4},{3,5},{4,6},{5,7},{6,0},{7,1},{8,10},{9,11},{10,... | collective-permute-start | bytes 786440 | tf_op jit(solution)/shard_map/ppermute | solution.py:323
  14.3 34.2 %collective-permute-start.17 = (bf16[64,2048]{1,0:T(8,128)(2,1)S(1)}, bf16[64,2048]{1,0:T(8,128)(2,1)S(1)}, u32[]{:S(2)}, u32[]{:S(2)}) collective-permute-start(bf16[64,2048]{1,0:T(8,128)(2,1)S(1)} %get-tuple-element.43.refs_7_.refs_1_), channel_id=1, source_target_pairs={{0,6},{1,7},{2,0},{3,1},{4,2},{5,3},{6,4},{7,5},{8,14},{9,15},{10,... | collective-permute-start | bytes 786440 | tf_op jit(solution)/shard_map/ppermute | solution.py:323
  16.6 70.0 %copy-start.15 = (s32[1,32]{1,0:T(1,128)}, s32[1,32]{1,0:T(1,128)S(1)}, u32[]{:S(2)}) copy-start(s32[1,32]{1,0:T(1,128)S(1)} %get-tuple-element.95.neg_ref) | copy-start | bytes 388
  16.6 10.5 %collective-permute-start.4 = (s32[32]{0:T(128)S(1)}, s32[32]{0:T(128)S(1)}, u32[]{:S(2)}, u32[]{:S(2)}) collective-permute-start(s32[32]{0:T(128)S(1)} %get-tuple-element.97), channel_id=1, source_target_pairs={{0,8},{8,0},{16,24},{24,16},{1,9},{9,1},{17,25},{25,17},{2,10},{10... | collective-permute-start | bytes 392 | tf_op jit(solution)/shard_map/ppermute | solution.py:331
  27.1 3.6 %collective-permute-start.5 = (s32[32]{0:T(128)S(1)}, s32[32]{0:T(128)S(1)}, u32[]{:S(2)}, u32[]{:S(2)}) collective-permute-start(s32[32]{0:T(128)S(1)} %get-tuple-element.96), channel_id=1, source_target_pairs={{0,16},{8,24},{16,0},{24,8},{1,17},{9,25},{17,1},{25,9},{2,18},{10... | collective-permute-start | bytes 392 | tf_op jit(solution)/shard_map/ppermute | solution.py:331
  30.7 4.5 %collective-permute-start.3 = (s32[32]{0:T(128)S(1)}, s32[32]{0:T(128)S(1)}, u32[]{:S(2)}, u32[]{:S(2)}) collective-permute-start(s32[32]{0:T(128)S(1)} %get-tuple-element.94), channel_id=1, source_target_pairs={{0,24},{8,16},{16,8},{24,0},{1,25},{9,17},{17,9},{25,1},{2,26},{10... | collective-permute-start | bytes 392 | tf_op jit(solution)/shard_map/ppermute | solution.py:331
  35.2 42.1 %copy-start.17 = (s32[32]{0:T(128)}, s32[32]{0:T(128)S(1)}, u32[]{:S(2)}) copy-start(s32[32]{0:T(128)S(1)} %collective-permute-done.3) | copy-start | bytes 388
  35.2 5.4 %collective-permute-start = (s32[128]{0:T(128)S(1)}, s32[128]{0:T(128)S(1)}, u32[]{:S(2)}, u32[]{:S(2)}) collective-permute-start(s32[128]{0:T(128)S(1)} %copy-done.22), channel_id=1, source_target_pairs={{0,2},{1,3},{2,4},{3,5},{4,6},{5,7},{6,0},{7,1},{8,10},{9,11},{10,... | collective-permute-start | bytes 1544 | tf_op jit(solution)/shard_map/ppermute | solution.py:323
  40.6 3.6 %collective-permute-start.1 = (s32[128]{0:T(128)S(1)}, s32[128]{0:T(128)S(1)}, u32[]{:S(2)}, u32[]{:S(2)}) collective-permute-start(s32[128]{0:T(128)S(1)} %copy-done.22), channel_id=1, source_target_pairs={{0,6},{1,7},{2,0},{3,1},{4,2},{5,3},{6,4},{7,5},{8,14},{9,15},{10,... | collective-permute-start | bytes 1544 | tf_op jit(solution)/shard_map/ppermute | solution.py:323
  44.2 4.9 %collective-permute-start.2 = (s32[128]{0:T(128)S(1)}, s32[128]{0:T(128)S(1)}, u32[]{:S(2)}, u32[]{:S(2)}) collective-permute-start(s32[128]{0:T(128)S(1)} %copy-done.22), channel_id=1, source_target_pairs={{0,4},{1,5},{2,6},{3,7},{4,0},{5,1},{6,2},{7,3},{8,12},{9,13},{10,... | collective-permute-start | bytes 1544 | tf_op jit(solution)/shard_map/ppermute | solution.py:323
  45.2 8.3 %collective-permute-start.18 = (bf16[64,2048]{1,0:T(8,128)(2,1)S(1)}, bf16[64,2048]{1,0:T(8,128)(2,1)S(1)}, u32[]{:S(2)}, u32[]{:S(2)}) collective-permute-start(bf16[64,2048]{1,0:T(8,128)(2,1)S(1)} %collective-permute-done.16.refs_8_.refs_2_), channel_id=1, source_target_pairs={{0,2},{1,3},{2,4},{3,5},{4,6},{5,7},{6,0},{7,1},{8,10},{9,11},{10,... | collective-permute-start | bytes 786440 | tf_op jit(solution)/shard_map/ppermute | solution.py:323
  48.5 13.5 %collective-permute-start.19 = (bf16[64,2048]{1,0:T(8,128)(2,1)S(1)}, bf16[64,2048]{1,0:T(8,128)(2,1)S(1)}, u32[]{:S(2)}, u32[]{:S(2)}) collective-permute-start(bf16[64,2048]{1,0:T(8,128)(2,1)S(1)} %collective-permute-done.17.refs_9_.refs_3_), channel_id=1, source_target_pairs={{0,6},{1,7},{2,0},{3,1},{4,2},{5,3},{6,4},{7,5},{8,14},{9,15},{10,... | collective-permute-start | bytes 786440 | tf_op jit(solution)/shard_map/ppermute | solution.py:323
  49.2 1.2 collective-permute-start.6
  50.3 27.0 %copy-start.23 = (s32[640]{0:T(1024)}, s32[640]{0:T(1024)S(1)}, u32[]{:S(2)}) copy-start(s32[640]{0:T(1024)S(1)} %collective-permute-done.6) | copy-start | bytes 7684
  50.3 27.0 %collective-permute-start.11 = (bf16[256,2048]{1,0:T(8,128)(2,1)}, bf16[256,2048]{1,0:T(8,128)(2,1)}, u32[]{:S(2)}, u32[]{:S(2)}) collective-permute-start(bf16[256,2048]{1,0:T(8,128)(2,1)} %refs_0_.1), channel_id=1, source_target_pairs={{0,1},{1,0},{2,3},{3,2},{4,5},{5,4},{6,7},{7,6},{8,9},{9,8},{10,11... | collective-permute-start | bytes 3145736 | tf_op jit(solution)/shard_map/ppermute | solution.py:327
  53.5 16.0 %collective-permute-start.20 = (bf16[64,2048]{1,0:T(8,128)(2,1)S(1)}, bf16[64,2048]{1,0:T(8,128)(2,1)S(1)}, u32[]{:S(2)}, u32[]{:S(2)}) collective-permute-start(bf16[64,2048]{1,0:T(8,128)(2,1)S(1)} %collective-permute-done.18.refs_10_.refs_4_), channel_id=1, source_target_pairs={{0,2},{1,3},{2,4},{3,5},{4,6},{5,7},{6,0},{7,1},{8,10},{9,11},{10,... | collective-permute-start | bytes 786440 | tf_op jit(solution)/shard_map/ppermute | solution.py:323
  62.1 9.6 %collective-permute-start.21 = (bf16[64,2048]{1,0:T(8,128)(2,1)S(1)}, bf16[64,2048]{1,0:T(8,128)(2,1)S(1)}, u32[]{:S(2)}, u32[]{:S(2)}) collective-permute-start(bf16[64,2048]{1,0:T(8,128)(2,1)S(1)} %collective-permute-done.19.refs_11_.refs_5_), channel_id=1, source_target_pairs={{0,6},{1,7},{2,0},{3,1},{4,2},{5,3},{6,4},{7,5},{8,14},{9,15},{10,... | collective-permute-start | bytes 786440 | tf_op jit(solution)/shard_map/ppermute | solution.py:323
  62.9 29.9 %collective-permute-start.9 = (bf16[256,2048]{1,0:T(8,128)(2,1)}, bf16[256,2048]{1,0:T(8,128)(2,1)}, u32[]{:S(2)}, u32[]{:S(2)}) collective-permute-start(bf16[256,2048]{1,0:T(8,128)(2,1)} %collective-permute-done.7.refs_0_), channel_id=1, source_target_pairs={{0,1},{1,0},{2,3},{3,2},{4,5},{5,4},{6,7},{7,6},{8,9},{9,8},{10,11... | collective-permute-start | bytes 3145736 | tf_op jit(solution)/shard_map/ppermute | solution.py:327
  62.9 29.9 %collective-permute-start.10 = (bf16[256,2048]{1,0:T(8,128)(2,1)}, bf16[256,2048]{1,0:T(8,128)(2,1)}, u32[]{:S(2)}, u32[]{:S(2)}) collective-permute-start(bf16[256,2048]{1,0:T(8,128)(2,1)} %collective-permute-done.8.refs_1_), channel_id=1, source_target_pairs={{0,1},{1,0},{2,3},{3,2},{4,5},{5,4},{6,7},{7,6},{8,9},{9,8},{10,11... | collective-permute-start | bytes 3145736 | tf_op jit(solution)/shard_map/ppermute | solution.py:327
  70.2 14.2 %collective-permute-start.12 = (bf16[128,2048]{1,0:T(8,128)(2,1)}, bf16[128,2048]{1,0:T(8,128)(2,1)}, u32[]{:S(2)}, u32[]{:S(2)}) collective-permute-start(bf16[128,2048]{1,0:T(8,128)(2,1)} %slice.89), channel_id=1, source_target_pairs={{0,8},{8,0},{16,24},{24,16},{1,9},{9,1},{17,25},{25,17},{2,10},{10... | collective-permute-start | bytes 1572872 | tf_op jit(solution)/shard_map/ppermute | solution.py:331
  72.4 13.9 %collective-permute-start.13 = (bf16[128,2048]{1,0:T(8,128)(2,1)}, bf16[128,2048]{1,0:T(8,128)(2,1)}, u32[]{:S(2)}, u32[]{:S(2)}) collective-permute-start(bf16[128,2048]{1,0:T(8,128)(2,1)} %slice.90), channel_id=1, source_target_pairs={{0,16},{8,24},{16,0},{24,8},{1,17},{9,25},{17,1},{25,9},{2,18},{10... | collective-permute-start | bytes 1572872 | tf_op jit(solution)/shard_map/ppermute | solution.py:331
  77.3 52.6 %collective-permute-start.33 = (bf16[512,2048]{1,0:T(8,128)(2,1)S(1)}, bf16[512,2048]{1,0:T(8,128)(2,1)}, u32[]{:S(2)}, u32[]{:S(2)}) collective-permute-start(bf16[512,2048]{1,0:T(8,128)(2,1)S(1)} %shard_map.74.refs_3_), channel_id=1, source_target_pairs={{0,1},{1,0},{2,3},{3,2},{4,5},{5,4},{6,7},{7,6},{8,9},{9,8},{10,11... | collective-permute-start | bytes 6291464 | tf_op jit(solution)/shard_map/ppermute | solution.py:327
  84.4 14.4 %collective-permute-start.14 = (bf16[128,2048]{1,0:T(8,128)(2,1)}, bf16[128,2048]{1,0:T(8,128)(2,1)}, u32[]{:S(2)}, u32[]{:S(2)}) collective-permute-start(bf16[128,2048]{1,0:T(8,128)(2,1)} %collective-permute-done.12.refs_2_), channel_id=1, source_target_pairs={{0,1},{1,0},{2,3},{3,2},{4,5},{5,4},{6,7},{7,6},{8,9},{9,8},{10,11... | collective-permute-start | bytes 1572872 | tf_op jit(solution)/shard_map/ppermute | solution.py:327
  86.4 12.5 %collective-permute-start.15 = (bf16[128,2048]{1,0:T(8,128)(2,1)}, bf16[128,2048]{1,0:T(8,128)(2,1)}, u32[]{:S(2)}, u32[]{:S(2)}) collective-permute-start(bf16[128,2048]{1,0:T(8,128)(2,1)} %collective-permute-done.13.refs_3_), channel_id=1, source_target_pairs={{0,1},{1,0},{2,3},{3,2},{4,5},{5,4},{6,7},{7,6},{8,9},{9,8},{10,11... | collective-permute-start | bytes 1572872 | tf_op jit(solution)/shard_map/ppermute | solution.py:327
  104.6 5.5 %collective-permute-start.22 = (f32[2,512]{1,0:T(2,128)S(1)}, f32[2,512]{1,0:T(2,128)S(1)}, u32[]{:S(2)}, u32[]{:S(2)}) collective-permute-start(f32[2,512]{1,0:T(2,128)S(1)} %get-tuple-element.53.refs_4_.refs_0_), channel_id=1, source_target_pairs={{0,2},{1,3},{2,4},{3,5},{4,6},{5,7},{6,0},{7,1},{8,10},{9,11},{10,... | collective-permute-start | bytes 12296 | tf_op jit(solution)/shard_map/ppermute | solution.py:323
  106.5 4.5 %collective-permute-start.23 = (f32[2,512]{1,0:T(2,128)S(1)}, f32[2,512]{1,0:T(2,128)S(1)}, u32[]{:S(2)}, u32[]{:S(2)}) collective-permute-start(f32[2,512]{1,0:T(2,128)S(1)} %get-tuple-element.53.refs_4_.refs_0_), channel_id=1, source_target_pairs={{0,4},{1,5},{2,6},{3,7},{4,0},{5,1},{6,2},{7,3},{8,12},{9,13},{10,... | collective-permute-start | bytes 12296 | tf_op jit(solution)/shard_map/ppermute | solution.py:323
  106.5 4.5 %collective-permute-start.24 = (f32[2,512]{1,0:T(2,128)S(1)}, f32[2,512]{1,0:T(2,128)S(1)}, u32[]{:S(2)}, u32[]{:S(2)}) collective-permute-start(f32[2,512]{1,0:T(2,128)S(1)} %get-tuple-element.53.refs_4_.refs_0_), channel_id=1, source_target_pairs={{0,6},{1,7},{2,0},{3,1},{4,2},{5,3},{6,4},{7,5},{8,14},{9,15},{10,... | collective-permute-start | bytes 12296 | tf_op jit(solution)/shard_map/ppermute | solution.py:323
  111.4 11.0 %collective-permute-start.25 = (bf16[64,2048]{1,0:T(8,128)(2,1)S(1)}, bf16[64,2048]{1,0:T(8,128)(2,1)S(1)}, u32[]{:S(2)}, u32[]{:S(2)}) collective-permute-start(bf16[64,2048]{1,0:T(8,128)(2,1)S(1)} %get-tuple-element.58), channel_id=1, source_target_pairs={{0,2},{1,3},{2,4},{3,5},{4,6},{5,7},{6,0},{7,1},{8,10},{9,11},{10,... | collective-permute-start | bytes 786440 | tf_op jit(solution)/shard_map/ppermute | solution.py:323
  113.1 13.2 %collective-permute-start.28 = (bf16[64,2048]{1,0:T(8,128)(2,1)S(1)}, bf16[64,2048]{1,0:T(8,128)(2,1)S(1)}, u32[]{:S(2)}, u32[]{:S(2)}) collective-permute-start(bf16[64,2048]{1,0:T(8,128)(2,1)S(1)} %get-tuple-element.62), channel_id=1, source_target_pairs={{0,6},{1,7},{2,0},{3,1},{4,2},{5,3},{6,4},{7,5},{8,14},{9,15},{10,... | collective-permute-start | bytes 786440 | tf_op jit(solution)/shard_map/ppermute | solution.py:323
  115.3 14.6 %copy-start.18 = (s32[32]{0:T(128)S(1)}, s32[32]{0:T(128)}, u32[]{:S(2)}) copy-start(s32[32]{0:T(128)} %copy-done.17) | copy-start | bytes 388
  116.2 1.4 collective-permute-start.31
  116.3 13.6 %collective-permute-start.32 = (f32[1,512]{1,0:T(1,128)S(1)}, f32[1,512]{1,0:T(1,128)S(1)}, u32[]{:S(2)}, u32[]{:S(2)}) collective-permute-start(f32[1,512]{1,0:T(1,128)S(1)} %get-tuple-element.65.refs_2_), channel_id=1, source_target_pairs={{0,1},{1,0},{2,3},{3,2},{4,5},{5,4},{6,7},{7,6},{8,9},{9,8},{10,11... | collective-permute-start | bytes 6152 | tf_op jit(solution)/shard_map/ppermute | solution.py:327
  122.5 12.0 %collective-permute-start.26 = (bf16[64,2048]{1,0:T(8,128)(2,1)S(1)}, bf16[64,2048]{1,0:T(8,128)(2,1)S(1)}, u32[]{:S(2)}, u32[]{:S(2)}) collective-permute-start(bf16[64,2048]{1,0:T(8,128)(2,1)S(1)} %add_convert_fusion.5), channel_id=1, source_target_pairs={{0,2},{1,3},{2,4},{3,5},{4,6},{5,7},{6,0},{7,1},{8,10},{9,11},{10,... | collective-permute-start | bytes 786440 | tf_op jit(solution)/shard_map/ppermute | solution.py:323
  126.4 35.5 %collective-permute-start.29 = (bf16[64,2048]{1,0:T(8,128)(2,1)S(1)}, bf16[64,2048]{1,0:T(8,128)(2,1)S(1)}, u32[]{:S(2)}, u32[]{:S(2)}) collective-permute-start(bf16[64,2048]{1,0:T(8,128)(2,1)S(1)} %add_convert_fusion.3), channel_id=1, source_target_pairs={{0,6},{1,7},{2,0},{3,1},{4,2},{5,3},{6,4},{7,5},{8,14},{9,15},{10,... | collective-permute-start | bytes 786440 | tf_op jit(solution)/shard_map/ppermute | solution.py:323
  132.9 10.1 %collective-permute-start.35 = (bf16[128,2048]{1,0:T(8,128)(2,1)S(1)}, bf16[128,2048]{1,0:T(8,128)(2,1)S(1)}, u32[]{:S(2)}, u32[]{:S(2)}) collective-permute-start(bf16[128,2048]{1,0:T(8,128)(2,1)S(1)} %get-tuple-element.69), channel_id=1, source_target_pairs={{0,16},{8,24},{16,0},{24,8},{1,17},{9,25},{17,1},{25,9},{2,18},{10... | collective-permute-start | bytes 1572872 | tf_op jit(solution)/shard_map/ppermute | solution.py:331
  134.6 28.4 %collective-permute-start.27 = (bf16[64,2048]{1,0:T(8,128)(2,1)S(1)}, bf16[64,2048]{1,0:T(8,128)(2,1)S(1)}, u32[]{:S(2)}, u32[]{:S(2)}) collective-permute-start(bf16[64,2048]{1,0:T(8,128)(2,1)S(1)} %add_convert_fusion.4), channel_id=1, source_target_pairs={{0,2},{1,3},{2,4},{3,5},{4,6},{5,7},{6,0},{7,1},{8,10},{9,11},{10,... | collective-permute-start | bytes 786440 | tf_op jit(solution)/shard_map/ppermute | solution.py:323
  134.7 36.1 %slice-start = ((s8[8388608]{0:T(1024)(128)(4,1)}), s8[4194304]{0:T(1024)(128)(4,1)S(1)}, s32[]{:S(2)}) async-start(s8[8388608]{0:T(1024)(128)(4,1)} %bitcast.39), calls=%async_computation | async-start | bytes 8388608
  137.9 36.9 %collective-permute-start.34 = (bf16[128,2048]{1,0:T(8,128)(2,1)S(1)}, bf16[128,2048]{1,0:T(8,128)(2,1)S(1)}, u32[]{:S(2)}, u32[]{:S(2)}) collective-permute-start(bf16[128,2048]{1,0:T(8,128)(2,1)S(1)} %get-tuple-element.67), channel_id=1, source_target_pairs={{0,8},{8,0},{16,24},{24,16},{1,9},{9,1},{17,25},{25,17},{2,10},{10... | collective-permute-start | bytes 1572872 | tf_op jit(solution)/shard_map/ppermute | solution.py:331
  138.5 22.8 %collective-permute-start.37 = (bf16[128,2048]{1,0:T(8,128)(2,1)S(1)}, bf16[128,2048]{1,0:T(8,128)(2,1)S(1)}, u32[]{:S(2)}, u32[]{:S(2)}) collective-permute-start(bf16[128,2048]{1,0:T(8,128)(2,1)S(1)} %get-tuple-element.71), channel_id=1, source_target_pairs={{0,8},{8,0},{16,24},{24,16},{1,9},{9,1},{17,25},{25,17},{2,10},{10... | collective-permute-start | bytes 1572872 | tf_op jit(solution)/shard_map/ppermute | solution.py:331
  143.0 23.8 %copy-start.16 = (s32[1,32]{1,0:T(1,128)S(1)}, s32[1,32]{1,0:T(1,128)}, u32[]{:S(2)}) copy-start(s32[1,32]{1,0:T(1,128)} %copy-done.15) | copy-start | bytes 388
  143.0 31.8 %collective-permute-start.39 = (bf16[128,2048]{1,0:T(8,128)(2,1)S(1)}, bf16[128,2048]{1,0:T(8,128)(2,1)S(1)}, u32[]{:S(2)}, u32[]{:S(2)}) collective-permute-start(bf16[128,2048]{1,0:T(8,128)(2,1)S(1)} %get-tuple-element.72), channel_id=1, source_target_pairs={{0,16},{8,24},{16,0},{24,8},{1,17},{9,25},{17,1},{25,9},{2,18},{10... | collective-permute-start | bytes 1572872 | tf_op jit(solution)/shard_map/ppermute | solution.py:331
  144.0 26.7 %slice-start.1 = ((s8[8388608]{0:T(1024)(128)(4,1)}), s8[4194304]{0:T(1024)(128)(4,1)S(1)}, s32[]{:S(2)}) async-start(s8[8388608]{0:T(1024)(128)(4,1)} %bitcast.39), calls=%async_computation.1 | async-start | bytes 8388608
  161.3 13.6 %collective-permute-start.36 = (bf16[128,2048]{1,0:T(8,128)(2,1)S(1)}, bf16[128,2048]{1,0:T(8,128)(2,1)S(1)}, u32[]{:S(2)}, u32[]{:S(2)}) collective-permute-start(bf16[128,2048]{1,0:T(8,128)(2,1)S(1)} %add_convert_fusion.1), channel_id=1, source_target_pairs={{0,8},{8,0},{16,24},{24,16},{1,9},{9,1},{17,25},{25,17},{2,10},{10... | collective-permute-start | bytes 1572872 | tf_op jit(solution)/shard_map/ppermute | solution.py:331
  161.9 12.9 %collective-permute-start.38 = (bf16[128,2048]{1,0:T(8,128)(2,1)S(1)}, bf16[128,2048]{1,0:T(8,128)(2,1)S(1)}, u32[]{:S(2)}, u32[]{:S(2)}) collective-permute-start(bf16[128,2048]{1,0:T(8,128)(2,1)S(1)} %add_convert_fusion), channel_id=1, source_target_pairs={{0,16},{8,24},{16,0},{24,8},{1,17},{9,25},{17,1},{25,9},{2,18},{10... | collective-permute-start | bytes 1572872 | tf_op jit(solution)/shard_map/ppermute | solution.py:331
  163.0 7.7 %collective-permute-start.30 = (bf16[64,2048]{1,0:T(8,128)(2,1)S(1)}, bf16[64,2048]{1,0:T(8,128)(2,1)S(1)}, u32[]{:S(2)}, u32[]{:S(2)}) collective-permute-start(bf16[64,2048]{1,0:T(8,128)(2,1)S(1)} %add_convert_fusion.2), channel_id=1, source_target_pairs={{0,6},{1,7},{2,0},{3,1},{4,2},{5,3},{6,4},{7,5},{8,14},{9,15},{10,... | collective-permute-start | bytes 786440 | tf_op jit(solution)/shard_map/ppermute | solution.py:323
  (20 other events, 64.3 us)
where the time goes:
time: 177 us
  waiting for transfers between devices  68.2 us (39%)
  starting transfers between devices  49.9 us (28%)
  Pallas kernels  34.3 us (19%)
  local copies, waits for them, and re-layouts  18.2 us (10%)
  other arithmetic  4.97 us (3%)
    ppermute x13, waiting for transfers between devices, group_swap(): return lax.ppermute(x, 'grp', [(g, g ^ bits) for g in range(groups)])  39.6 us
    ppermute x18, starting transfers between devices, ring_shift(): return lax.ppermute(x, 'mem', perm)  29.7 us
    pallas_call x11, Pallas kernels, call(): pl.pallas_call(kernel, out_shape=[jax.ShapeDtypeStruct(s, t) for s, t in...  28.1 us
    ppermute x18, waiting for transfers between devices, ring_shift(): return lax.ppermute(x, 'mem', perm)  26.6 us
    ppermute x13, starting transfers between devices, group_swap(): return lax.ppermute(x, 'grp', [(g, g ^ bits) for g in range(groups)])  18.8 us
    unnamed x56, local copies, waits for them, and re-layouts  12 us
    pallas_call x1, Pallas kernels, finish(): pl.pallas_call(finish_kernel, grid=(width // tile,), out_shape=jax.ShapeD...  4.07 us
  transfers between devices with their start and end apart: 40, of which 17 were waited for; matrix products, arithmetic and copies ran while one was open for 5% of the time, Pallas kernels for 19%

commit v1 on v0

v1 whole, which is shorter than its diff:
```python
import functools
import math

import jax
import jax.numpy as jnp
from jax import lax
from jax.experimental import pallas as pl
from jax.experimental.pallas import tpu as pltpu
from jax.sharding import PartitionSpec as P


F32 = jnp.float32
BF16 = jnp.bfloat16
VMEM_LIMIT = 60 * 1024 * 1024
SPARE = 6 * 1024 * 1024
VM = pl.BlockSpec(memory_space=pltpu.VMEM)
SM = pl.BlockSpec(memory_space=pltpu.SMEM)


def dot(a, b, ca=1, cb=0):
    return lax.dot_general(a, b, (((ca,), (cb,)), ((), ())), preferred_element_type=F32)


def chunk_of(width):
    return width if width < 512 else 512


def cost(flops, nbytes):
    return pl.CostEstimate(flops=int(flops), bytes_accessed=int(nbytes), transcendentals=0)


def size_of(shape, dtype):
    return math.prod(shape) * jnp.dtype(dtype).itemsize


def call(kernel, outs, n_smem, args, flops):
    nbytes = sum(size_of(x.shape, x.dtype) for x in args[n_smem:])
    nbytes += sum(size_of(s, t) for s, t in outs)
    return pl.pallas_call(
        kernel,
        out_shape=[jax.ShapeDtypeStruct(s, t) for s, t in outs],
        in_specs=[SM] * n_smem + [VM] * (len(args) - n_smem),
        out_specs=[VM] * len(outs),
        compiler_params=pltpu.CompilerParams(
            vmem_limit_bytes=min(VMEM_LIMIT, nbytes * 3 // 2 + SPARE)
        ),
        cost_estimate=cost(flops, nbytes),
    )(*args)


def project_kernel(x_up, x_down, w_ref, z_ref, *hidden_ref):
    x = jnp.concatenate([x_up[...], x_down[...]], axis=0)
    width = w_ref.shape[1]
    step = chunk_of(width)
    for c in range(0, width, step):
        cols = slice(c, c + step)
        hidden = dot(x, w_ref[:, cols])
        if hidden_ref:
            hidden_ref[0][:, cols] = hidden
        z_ref[:, cols] = (hidden * jax.nn.sigmoid(hidden)).astype(BF16)


def first_of(k, side, own_rows):
    g, m = lax.axis_index("grp"), lax.axis_index("mem")
    return ((g ^ k) * lax.axis_size("mem") + (m ^ side)) * own_rows


def column(row):
    tall = jnp.broadcast_to(row.astype(F32), (128, row.shape[1]))
    return jnp.transpose(tall)[:, 0:1].astype(jnp.int32)


def ids_kernel(chips, *refs):
    pos, neg, out = refs[:chips], refs[chips:-1], refs[-1]
    half = pos[0].shape[1] // 2
    row = []
    for k in range(chips):
        row += [pos[k][:, :half], pos[-k % chips][:, half:]]
    out[0:1] = jnp.concatenate(row, axis=1)
    g = lax.axis_index("grp")
    row = jnp.concatenate([n[pl.ds(g, 1)] for n in neg], axis=1)
    out[1:2, : row.shape[1]] = row


def is_here(ids, own_rows):
    here = None
    for k in range(lax.axis_size("grp")):
        low = jnp.minimum(first_of(k, 0, own_rows), first_of(k, 1, own_rows))
        hit = (ids >= low) & (ids < low + 2 * own_rows)
        here = hit if here is None else here | hit
    return here


def hits(ids, first, block):
    lane = lax.broadcasted_iota(jnp.int32, (ids.shape[0], block.shape[0]), 1)
    return ((ids - first) == lane).astype(BF16)


def pick_kernel(plan, own_rows, each, own_ref, other_ref, *refs):
    n = len(plan)
    blocks = refs[:n]
    base_ref = refs[n] if len(refs) > n + 2 else None
    pick_rows(plan, own_rows, each, own_ref, other_ref, blocks, base_ref, [refs[-2]], refs[-1], 0)


def pick_rows(plan, own_rows, each, own_ref, other_ref, blocks, base_ref, pos_refs, row_ref, at):
    users = own_ref.shape[1]
    ids = column(own_ref[0:1])
    many = each * lax.axis_size("grp")
    neg = [column(r[1:2, :many]) for r in (own_ref, other_ref)]
    firsts = [first_of(k, side, own_rows) + row for side, k, row in plan]
    picks = [hits(ids, f, block) for f, block in zip(firsts, blocks)]
    owners = list(dict.fromkeys((side, k) for side, k, _ in plan))
    neg_picks = [
        hits(neg[side][k * each : (k + 1) * each], f, block)
        for (side, k, _), f, block in zip(plan, firsts, blocks)
    ]
    width = blocks[0].shape[1]
    step = chunk_of(width)
    cut = users // len(pos_refs)
    for c in range(0, width, step):
        cols = slice(c, c + step)
        rows = sum(dot(p, block[:, cols]) for p, block in zip(picks, blocks))
        if base_ref is not None:
            rows = rows + base_ref[:, cols].astype(F32)
        rows = rows.astype(BF16)
        for k, pos_ref in enumerate(pos_refs):
            pos_ref[:, cols] = rows[k * cut : (k + 1) * cut]
        for o, owner in enumerate(owners):
            mine = [n for n, (side, k, _) in enumerate(plan) if (side, k) == owner]
            got = sum(dot(neg_picks[n], blocks[n][:, cols]) for n in mine)
            row_ref[at + o * each : at + (o + 1) * each, cols] = got.astype(BF16)


def scores(scale, z_of, neg_ref, pos_refs, here, logit_ref, pos_out):
    width = neg_ref.shape[1]
    step = chunk_of(width)
    lanes = min(width, 128)
    slot = pos_refs[0].shape[0]
    logits = 0.0
    pos = [jnp.zeros((slot, lanes), F32) for _ in pos_refs]
    for c in range(0, width, step):
        cols = slice(c, c + step)
        z = z_of(cols)
        logits = logits + dot(neg_ref[:, cols], z, 1, 1)
        for k, ref in enumerate(pos_refs):
            prod = z[k * slot : (k + 1) * slot].astype(F32) * ref[:, cols].astype(F32)
            for d in range(0, step, lanes):
                pos[k] = pos[k] + prod[:, d : d + lanes]
    logits = logits * scale
    pos = [scale * jnp.sum(jnp.transpose(p), axis=0, keepdims=True) for p in pos]
    pos = pos[0] if len(pos) == 1 else jnp.concatenate(pos, axis=1)
    top = jnp.max(logits, axis=0, keepdims=True)
    top = jnp.where(here, jnp.maximum(top, pos), top)
    total = jnp.sum(jnp.exp(logits - top), axis=0, keepdims=True)
    total = total + jnp.where(here, jnp.exp(pos - top), 0.0)
    logit_ref[...] = logits
    pos_out[...] = pos
    return top, total


def main_kernel(plan, own_rows, each, slots, scale, own_ref, other_ref, base_ref, *refs):
    n = len(plan)
    early = refs[:2]
    blocks = refs[2 : 2 + n]
    zs = refs[2 + n : 2 + n + slots]
    rest = refs[2 + n + slots :]
    pos_refs, (neg_out, logit_ref, pos_out, stat_ref) = rest[: slots + 1], rest[slots + 1 :]
    at = 0
    for e in early:
        neg_out[at : at + e.shape[0]] = e[...]
        at += e.shape[0]
    pick_rows(plan, own_rows, each, own_ref, other_ref, blocks, base_ref, pos_refs, neg_out, at)

    def z_of(cols):
        return jnp.concatenate([z[:, cols] for z in zs], axis=0)

    users = slots * pos_refs[0].shape[0]
    here = is_here(own_ref[0:1, :users], own_rows)
    top, total = scores(scale, z_of, neg_out, pos_refs[:slots], here, logit_ref, pos_out)
    stat_ref[0:1] = top
    stat_ref[1:2] = total


def tail_kernel(own_rows, scale, own_ref, neg_ref, pos_ref, z_ref, stat_in, *refs):
    logit_ref, pos_out, stat_ref = refs

    def z_of(cols):
        return z_ref[:, cols]

    slot = pos_ref.shape[0]
    users = own_ref.shape[1]
    here = is_here(own_ref[0:1, users - slot :], own_rows)
    top, total = scores(scale, z_of, neg_ref, [pos_ref], here, logit_ref, pos_out)
    stat_ref[:, : users - slot] = stat_in[...]
    stat_ref[0:1, users - slot :] = top
    stat_ref[1:2, users - slot :] = total


def join_kernel(*refs):
    out = refs[-1]
    at = 0
    for r in refs[:-1]:
        out[at : at + r.shape[0]] = r[...]
        at += r.shape[0]


def slot_total(stats, chips, k, slot):
    half = slot // 2
    tops, totals = [], []
    for s in range(chips):
        up = (k - s) % chips * slot
        down = (k + s) % chips * slot + half
        stat = jnp.concatenate(
            [stats[s][:, up : up + half], stats[s][:, down : down + half]], axis=1
        )
        tops.append(stat[0:1])
        totals.append(stat[1:2])
    peak = functools.reduce(jnp.maximum, tops)
    return peak + jnp.log(sum(t * jnp.exp(m - peak) for m, t in zip(tops, totals)))


def slot_weights(stats, chips, k, slot, logit, pos, here):
    log_total = slot_total(stats, chips, k, slot)
    prob = jnp.exp(logit - log_total).astype(BF16)
    weight = jnp.where(here, jnp.exp(pos - log_total) - 1.0, 0.0)
    return prob, weight


def slot_grad(scale, prob, weight, neg_ref, pos_ref, up_ref, down_ref):
    slot, width = pos_ref.shape
    half = slot // 2
    tall = jnp.transpose(jnp.broadcast_to(weight, (128, slot)))[:, 0:1]
    prob = jnp.transpose(prob.astype(F32)).astype(BF16)
    step = chunk_of(width)
    for c in range(0, width, step):
        cols = slice(c, c + step)
        grad = dot(prob, neg_ref[:, cols]) + tall * pos_ref[:, cols].astype(F32)
        grad = scale * grad
        up_ref[:, cols] = grad[:half].astype(up_ref.dtype)
        down_ref[:, cols] = grad[half:].astype(down_ref.dtype)


def lead_kernel(chips, own_rows, scale, own_ref, logit_ref, pos_ref, neg_ref, rows_ref, *refs):
    stats, (up_ref, down_ref) = refs[:chips], refs[chips:]
    slot = rows_ref.shape[0]
    lanes = slice(slot, 2 * slot)
    here = is_here(own_ref[0:1, lanes], own_rows)
    prob, weight = slot_weights(
        stats, chips, 1, slot, logit_ref[:, lanes], pos_ref[:, lanes], here
    )
    slot_grad(scale, prob, weight, neg_ref, rows_ref, up_ref, down_ref)


def rest_kernel(chips, own_rows, scale, order, each, own_in, logit_ref, pos_ref, logit_t, pos_t, *refs):
    neg_ref, refs = refs[0], refs[1:]
    rows, refs = refs[: chips - 1], refs[chips - 1 :]
    stats, refs = refs[:chips], refs[chips:]
    own_ref, other_ref, weight_ref = refs[:3]
    parts = refs[3:]
    slot = rows[0].shape[0]
    at = 0
    for k in range(chips):
        lanes = slice(k * slot, (k + 1) * slot)
        last = k == chips - 1
        logit = logit_t[...] if last else logit_ref[:, lanes]
        pos = pos_t[...] if last else pos_ref[:, lanes]
        here = is_here(own_in[0:1, lanes], own_rows)
        prob, weight = slot_weights(stats, chips, k, slot, logit, pos, here)
        weight_ref[:, lanes] = weight
        for n, (side, owner) in enumerate(order):
            to = other_ref if side else own_ref
            to[owner * each : (owner + 1) * each, lanes] = prob[n * each : (n + 1) * each]
        if k != 1:
            slot_grad(scale, prob, weight, neg_ref, rows[at], parts[2 * at], parts[2 * at + 1])
            at += 1


def item_kernel(scale, k, each, *refs):
    sides = [refs[4 * s : 4 * s + 4] for s in range(2)]
    outs = refs[8:]
    own_rows = sum(o.shape[0] for o in outs)
    width = outs[0].shape[1]
    first = first_of(k, 0, own_rows)
    owner = slice(k * each, (k + 1) * each)
    neg = sides[0][0][1:2, owner] - first
    pick = lax.broadcasted_iota(jnp.int32, (own_rows, each), 0) == neg
    pick = pick.astype(F32).astype(BF16)
    weights = []
    for ids_ref, prob_ref, weight_ref, _ in sides:
        ids = ids_ref[0:1] - first
        row = lax.broadcasted_iota(jnp.int32, (own_rows, ids.shape[1]), 0)
        w = dot(pick, prob_ref[owner]) + jnp.where(row == ids, weight_ref[...], 0.0)
        weights.append(w.astype(BF16))
    step = chunk_of(width)
    for c in range(0, width, step):
        cols = slice(c, c + step)
        grad = scale * sum(dot(w, side[3][:, cols]) for w, side in zip(weights, sides))
        at = 0
        for o in outs:
            o[:, cols] = grad[at : at + o.shape[0]].astype(o.dtype)
            at += o.shape[0]


def finish_kernel(up_ref, up_in_ref, down_ref, down_in_ref, hidden_ref, w_ref, out_ref):
    grad = [a[...] + b[...].astype(F32) for a, b in ((up_ref, up_in_ref), (down_ref, down_in_ref))]
    hidden = hidden_ref[...]
    s = jax.nn.sigmoid(hidden)
    slope = s * (1.0 + hidden * (1.0 - s))
    grad = (jnp.concatenate(grad, axis=0) * slope).astype(BF16)
    step = chunk_of(w_ref.shape[0])
    for c in range(0, w_ref.shape[0], step):
        cols = slice(c, c + step)
        out_ref[:, cols] = dot(grad, w_ref[cols], 1, 1).astype(BF16)


def ring_shift(x, step, chips):
    perm = [
        (chip * 2 + core, (chip + step) % chips * 2 + core)
        for chip in range(chips)
        for core in range(2)
    ]
    return lax.ppermute(x, "mem", perm)


def core_swap(x, members):
    return lax.ppermute(x, "mem", [(m, m ^ 1) for m in range(members)])


def group_swap(x, bits, groups):
    return lax.ppermute(x, "grp", [(g, g ^ bits) for g in range(groups)])


def low_bit(k):
    return k & -k


def on_device(user_rows, projection, item_table, positive, negatives):
    groups = lax.axis_size("grp")
    members = lax.axis_size("mem")
    chips = members // 2
    rows_here, width = user_rows.shape
    half = rows_here // 2
    users = chips * rows_here
    own_rows = item_table.shape[0]
    mid = own_rows // 2
    neg_rows = negatives.shape[1]
    scale = 4.0 / math.sqrt(width)
    single = [k for k in range(1, groups) if low_bit(k) == k]
    double = [k for k in range(1, groups) if low_bit(k) != k]

    block = {0: [(0, item_table)]}
    for k in single:
        block[k] = [(0, group_swap(item_table, k, groups))]
    x_up, x_down = user_rows[:half], user_rows[half:]
    z_slots = []
    for k in range(chips):
        if k:
            x_up = ring_shift(x_up, 1, chips)
            x_down = ring_shift(x_down, -1, chips)
        got = call(
            project_kernel,
            [((rows_here, width), BF16)] + ([] if k else [((rows_here, width), F32)]),
            0,
            [x_up, x_down, projection],
            2 * rows_here * width * width,
        )
        z_slots.append(got[0])
        if not k:
            hidden = got[1]
    row = positive[None]
    ids_in = [row] + [ring_shift(row, k, chips) for k in range(1, chips)]
    neg_in = [negatives] + [group_swap(negatives, k, groups) for k in range(1, groups)]
    (own,) = call(
        functools.partial(ids_kernel, chips), [((2, users), jnp.int32)], 0, ids_in + neg_in, users
    )
    other = core_swap(own, members)
    for k in double:
        low = low_bit(k)
        rest = k ^ low
        block[k] = [
            (0, group_swap(block[rest][0][1][:mid], low, groups)),
            (mid, group_swap(block[low][0][1][mid:], rest, groups)),
        ]

    def stage(ks):
        plan, rows = [], []
        for side in range(2):
            for k in ks:
                for at, piece in block[k]:
                    plan.append((side, k, at))
                    rows.append(core_swap(piece, members) if side else piece)
        return tuple(plan), rows

    order = []
    slots = chips - 1
    base, early = [], []
    for ks in ([0], single):
        plan, rows = stage(ks)
        order += [(side, k) for side, k, _ in plan]
        pos_base, got_rows = call(
            functools.partial(pick_kernel, plan, own_rows, neg_rows),
            [((users, width), BF16), ((len(plan) * neg_rows, width), BF16)],
            0,
            [own, other] + rows + base,
            2 * users * width * own_rows * len(rows),
        )
        base = [pos_base]
        early.append(got_rows)
    plan, rows = stage(double)
    order += list(dict.fromkeys((side, k) for side, k, _ in plan))
    negs = 2 * groups * neg_rows
    out = call(
        functools.partial(main_kernel, plan, own_rows, neg_rows, slots, scale),
        [((rows_here, width), BF16)] * chips
        + [
            ((negs, width), BF16),
            ((negs, slots * rows_here), F32),
            ((1, slots * rows_here), F32),
            ((2, slots * rows_here), F32),
        ],
        0,
        [own, other] + base + early + rows + z_slots[:slots],
        2 * users * width * mid * len(rows) + 2 * users * negs * width,
    )
    pos_rows, (neg_all, logits, pos, stat) = out[:chips], out[chips:]
    logits_t, pos_t, stat = call(
        functools.partial(tail_kernel, own_rows, scale),
        [((negs, rows_here), F32), ((1, rows_here), F32), ((2, users), F32)],
        0,
        [own, neg_all, pos_rows[-1], z_slots[-1], stat],
        2 * rows_here * negs * width,
    )
    stats = [stat] + [ring_shift(stat, k, chips) for k in range(1, chips)]
    (z_all,) = call(join_kernel, [((users, width), BF16)], 0, z_slots, users * width)
    z_other = core_swap(z_all, members)
    mine = groups * neg_rows
    part = [None] * chips
    part[1] = call(
        functools.partial(lead_kernel, chips, own_rows, scale),
        [((half, width), BF16)] * 2,
        0,
        [own, logits, pos, neg_all, pos_rows[1]] + stats,
        2 * rows_here * negs * width,
    )
    others = [k for k in range(chips) if k != 1]
    out = call(
        functools.partial(rest_kernel, chips, own_rows, scale, tuple(order), neg_rows),
        [((mine, users), BF16), ((mine, users), BF16), ((1, users), F32)]
        + [((half, width), BF16 if k else F32) for k in others for _ in range(2)],
        0,
        [own, logits, pos, logits_t, pos_t, neg_all] + [pos_rows[k] for k in others] + stats,
        2 * users * negs * width,
    )
    prob, prob_out, weight = out[:3]
    for n, k in enumerate(others):
        part[k] = out[3 + 2 * n : 5 + 2 * n]
    prob_in = core_swap(prob_out, members)
    weight_in = core_swap(weight, members)

    def item_part(k, kinds):
        return call(
            functools.partial(item_kernel, scale, k, neg_rows),
            [((n, width), t) for n, t in kinds],
            0,
            [own, prob, weight, z_all, other, prob_in, weight_in, z_other],
            4 * own_rows * users * width,
        )

    def ring_sum(side, step):
        moving = part[1][side]
        for k in range(2, chips):
            moving = ring_shift(moving, step, chips)
            moving = (part[k][side].astype(F32) + moving.astype(F32)).astype(BF16)
        return ring_shift(moving, step, chips)

    up_in = ring_sum(0, 1)
    down_in = ring_sum(1, -1)

    sums = {}
    for k in double + single:
        sums[k] = item_part(k, [(mid, BF16), (mid, BF16)])
    (total,) = item_part(0, [(own_rows, F32)])
    for k in double:
        low = low_bit(k)
        rest = k ^ low
        a = group_swap(sums[k][0], low, groups)
        b = group_swap(sums[k][1], rest, groups)
        sums[rest] = [(sums[rest][0].astype(F32) + a.astype(F32)).astype(BF16), sums[rest][1]]
        sums[low] = [sums[low][0], (sums[low][1].astype(F32) + b.astype(F32)).astype(BF16)]
    got = {}
    for k in single:
        got[k] = [group_swap(piece, k, groups) for piece in sums[k]]
    item_grad = total + sum(jnp.concatenate(got[k]).astype(F32) for k in single)
    (user_grad,) = call(
        finish_kernel,
        [((rows_here, width), BF16)],
        0,
        [part[0][0], up_in, part[0][1], down_in, hidden, projection],
        2 * rows_here * width * width,
    )
    return (user_grad, item_grad)


def solution(mesh):
    owners = ("grp", "mem")

    return jax.shard_map(
        on_device,
        mesh=mesh,
        in_specs=(P(owners, None), P(), P(owners, None), P(owners), P(None, owners)),
        out_specs=(P(owners, None), P(owners, None)),
        check_vma=False,
    )
```

time: 177 us -> 167 us (0.944)
  waiting for transfers between devices: 68.2 us -> 84.9 us
  local copies, waits for them, and re-layouts: 18.2 us -> 7.95 us
  Pallas kernels: 34.3 us -> 26.4 us
  starting transfers between devices: 49.9 us -> 44.6 us
  other arithmetic: 4.97 us -> 2.29 us
    ppermute x18, waiting for transfers between devices: 26.6 us -> 52.6 us  [ring_shift(): return lax.ppermute(x, 'mem', perm)]
    ppermute x13, waiting for transfers between devices: 39.6 us -> 31.2 us  [group_swap(): return lax.ppermute(x, 'grp', [(g, g ^ bits) for g in range(groups)])]
    pallas_call x2 -> x0, Pallas kernels: 6.22 us -> none  [the longest x1 4.07 us: finish(): pl.pallas_call(finish_kernel, grid=(width // tile,), out_shape=jax.ShapeD...]
    ppermute x13, starting transfers between devices: 18.8 us -> 12.6 us  [group_swap(): return lax.ppermute(x, 'grp', [(g, g ^ bits) for g in range(groups)])]
    unnamed x56 -> x10, local copies, waits for them, and re-layouts: 12 us -> 6.8 us
    another operation x3 -> x0, other arithmetic: 1.93 us -> none  [stage(): jnp.stack(firsts).astype(jnp.int32)]
    slice x1, local copies, waits for them, and re-layouts: 1.9 us -> 0.04 us  [on_device(): block[low][0][1][mid:]]
    slice x1, local copies, waits for them, and re-layouts: 1.88 us -> 0.04 us  [on_device(): block[rest][0][1][:mid]]
  transfers between devices with their start and end apart: 40 -> 40, of which waited for: 17 -> 20; matrix products, arithmetic and copies ran while one was open for 5% -> 1% of each run, Pallas kernels for 19% -> 16%
where the time goes in v1:
time: 167 us
  waiting for transfers between devices  84.9 us (51%)
  starting transfers between devices  44.6 us (27%)
  Pallas kernels  26.4 us (16%)
  local copies, waits for them, and re-layouts  7.95 us (5%)
  other arithmetic  2.29 us (1%)
    ppermute x18, waiting for transfers between devices, ring_shift(): return lax.ppermute(x, 'mem', perm)  52.6 us
    ppermute x13, waiting for transfers between devices, group_swap(): return lax.ppermute(x, 'grp', [(g, g ^ bits) for g in range(groups)])  31.2 us
    ppermute x18, starting transfers between devices, ring_shift(): return lax.ppermute(x, 'mem', perm)  30.2 us
    pallas_call x17, Pallas kernels, call(): pl.pallas_call(kernel, out_shape=[jax.ShapeDtypeStruct(s, t) for s, t in...  26.4 us
    ppermute x13, starting transfers between devices, group_swap(): return lax.ppermute(x, 'grp', [(g, g ^ bits) for g in range(groups)])  12.6 us
    unnamed x10, local copies, waits for them, and re-layouts  6.8 us
  transfers between devices with their start and end apart: 40, of which 20 were waited for; matrix products, arithmetic and copies ran while one was open for 1% of the time, Pallas kernels for 16%

profile of v1, /device:TPU:0, one launch (start us, length us, event | category | flops | bytes accessed | tf_op | source)
XLA Modules:
  0.0 167.2 jit_solution(8081125530936349472)
XLA Ops:
  0.6 3.0 %collective-permute-start.7 = (bf16[256,2048]{1,0:T(8,128)(2,1)}, bf16[256,2048]{1,0:T(8,128)(2,1)S(1)}, u32[]{:S(2)}, u32[]{:S(2)}) collective-permute-start(bf16[256,2048]{1,0:T(8,128)(2,1)} %refs_0_.1), channel_id=1, source_target_pairs={{0,8},{8,0},{16,24},{24,16},{1,9},{9,1},{17,25},{25,17},{2,10},{10... | collective-permute-start | bytes 3145736 | tf_op jit(solution)/shard_map/ppermute | solution.py:331
  3.7 1.5 collective-permute-start.8
  6.3 1.6 collective-permute-start.16
  7.9 2.2 %collective-permute-start.17 = (bf16[64,2048]{1,0:T(8,128)(2,1)S(1)}, bf16[64,2048]{1,0:T(8,128)(2,1)S(1)}, u32[]{:S(2)}, u32[]{:S(2)}) collective-permute-start(bf16[64,2048]{1,0:T(8,128)(2,1)S(1)} %get-tuple-element.70.x_down), channel_id=1, source_target_pairs={{0,6},{1,7},{2,0},{3,1},{4,2},{5,3},{6,4},{7,5},{8,14},{9,15},{10,... | collective-permute-start | bytes 786440 | tf_op jit(solution)/shard_map/ppermute | solution.py:323
  10.1 11.2 %collective-permute-done.refs_1_ = s32[1,128]{1,0:T(1,128)S(1)} collective-permute-done((s32[1,128]{1,0:T(1,128)}, s32[1,128]{1,0:T(1,128)S(1)}, u32[]{:S(2)}, u32[]{:S(2)}) %collective-permute-start) | collective-permute-done | bytes 544 | tf_op jit(solution)/shard_map/ppermute | solution.py:323
  22.1 3.8 %collective-permute-done.1.refs_2_ = s32[1,128]{1,0:T(1,128)S(1)} collective-permute-done((s32[1,128]{1,0:T(1,128)}, s32[1,128]{1,0:T(1,128)S(1)}, u32[]{:S(2)}, u32[]{:S(2)}) %collective-permute-start.1) | collective-permute-done | bytes 544 | tf_op jit(solution)/shard_map/ppermute | solution.py:323
  25.9 1.8 %collective-permute-start.2 = (s32[1,128]{1,0:T(1,128)}, s32[1,128]{1,0:T(1,128)S(1)}, u32[]{:S(2)}, u32[]{:S(2)}) collective-permute-start(s32[1,128]{1,0:T(1,128)} %bitcast.3), channel_id=1, source_target_pairs={{0,6},{1,7},{2,0},{3,1},{4,2},{5,3},{6,4},{7,5},{8,14},{9,15},{10,... | collective-permute-start | bytes 1544 | tf_op jit(solution)/shard_map/ppermute | solution.py:323
  27.7 1.9 %collective-permute-done.2.refs_3_ = s32[1,128]{1,0:T(1,128)S(1)} collective-permute-done((s32[1,128]{1,0:T(1,128)}, s32[1,128]{1,0:T(1,128)S(1)}, u32[]{:S(2)}, u32[]{:S(2)}) %collective-permute-start.2) | collective-permute-done | bytes 544 | tf_op jit(solution)/shard_map/ppermute | solution.py:323
  30.2 3.3 %collective-permute-done.3.refs_5_ = s32[4,32]{1,0:T(4,128)S(1)} collective-permute-done((s32[4,32]{1,0:T(4,128)}, s32[4,32]{1,0:T(4,128)S(1)}, u32[]{:S(2)}, u32[]{:S(2)}) %collective-permute-start.3) | collective-permute-done | bytes 544 | tf_op jit(solution)/shard_map/ppermute | solution.py:331
  33.9 3.3 %collective-permute-done.4.refs_6_ = s32[4,32]{1,0:T(4,128)S(1)} collective-permute-done((s32[4,32]{1,0:T(4,128)}, s32[4,32]{1,0:T(4,128)S(1)}, u32[]{:S(2)}, u32[]{:S(2)}) %collective-permute-start.4) | collective-permute-done | bytes 544 | tf_op jit(solution)/shard_map/ppermute | solution.py:331
  37.7 4.2 %collective-permute-done.5.refs_7_ = s32[4,32]{1,0:T(4,128)S(1)} collective-permute-done((s32[4,32]{1,0:T(4,128)}, s32[4,32]{1,0:T(4,128)S(1)}, u32[]{:S(2)}, u32[]{:S(2)}) %collective-permute-start.5) | collective-permute-done | bytes 544 | tf_op jit(solution)/shard_map/ppermute | solution.py:331
  44.7 3.8 %collective-permute-start.19 = (bf16[64,2048]{1,0:T(8,128)(2,1)S(1)}, bf16[64,2048]{1,0:T(8,128)(2,1)S(1)}, u32[]{:S(2)}, u32[]{:S(2)}) collective-permute-start(bf16[64,2048]{1,0:T(8,128)(2,1)S(1)} %collective-permute-done.17.x_down), channel_id=1, source_target_pairs={{0,6},{1,7},{2,0},{3,1},{4,2},{5,3},{6,4},{7,5},{8,14},{9,15},{10,... | collective-permute-start | bytes 786440 | tf_op jit(solution)/shard_map/ppermute | solution.py:323
  48.5 7.2 %collective-permute-done.18.x_up = bf16[64,2048]{1,0:T(8,128)(2,1)S(1)} collective-permute-done((bf16[64,2048]{1,0:T(8,128)(2,1)S(1)}, bf16[64,2048]{1,0:T(8,128)(2,1)S(1)}, u32[]{:S(2)}, u32[]{:S(2)}) %collective-permute-start.18) | collective-permute-done | bytes 262176 | tf_op jit(solution)/shard_map/ppermute | solution.py:323
  55.7 3.2 %collective-permute-done.19.x_down = bf16[64,2048]{1,0:T(8,128)(2,1)S(1)} collective-permute-done((bf16[64,2048]{1,0:T(8,128)(2,1)S(1)}, bf16[64,2048]{1,0:T(8,128)(2,1)S(1)}, u32[]{:S(2)}, u32[]{:S(2)}) %collective-permute-start.19) | collective-permute-done | bytes 262176 | tf_op jit(solution)/shard_map/ppermute | solution.py:323
  58.9 3.5 %collective-permute-start.21 = (bf16[64,2048]{1,0:T(8,128)(2,1)S(1)}, bf16[64,2048]{1,0:T(8,128)(2,1)S(1)}, u32[]{:S(2)}, u32[]{:S(2)}) collective-permute-start(bf16[64,2048]{1,0:T(8,128)(2,1)S(1)} %collective-permute-done.19.x_down), channel_id=1, source_target_pairs={{0,6},{1,7},{2,0},{3,1},{4,2},{5,3},{6,4},{7,5},{8,14},{9,15},{10,... | collective-permute-start | bytes 786440 | tf_op jit(solution)/shard_map/ppermute | solution.py:323
  63.1 6.6 %collective-permute-done.20.x_up = bf16[64,2048]{1,0:T(8,128)(2,1)S(1)} collective-permute-done((bf16[64,2048]{1,0:T(8,128)(2,1)S(1)}, bf16[64,2048]{1,0:T(8,128)(2,1)S(1)}, u32[]{:S(2)}, u32[]{:S(2)}) %collective-permute-start.20) | collective-permute-done | bytes 262176 | tf_op jit(solution)/shard_map/ppermute | solution.py:323
  70.2 3.2 %collective-permute-done.21.x_down = bf16[64,2048]{1,0:T(8,128)(2,1)S(1)} collective-permute-done((bf16[64,2048]{1,0:T(8,128)(2,1)S(1)}, bf16[64,2048]{1,0:T(8,128)(2,1)S(1)}, u32[]{:S(2)}, u32[]{:S(2)}) %collective-permute-start.21) | collective-permute-done | bytes 262176 | tf_op jit(solution)/shard_map/ppermute | solution.py:323
  73.9 3.4 %copy-done = bf16[2048,2048]{1,0:T(8,128)(2,1)S(1)} copy-done((bf16[2048,2048]{1,0:T(8,128)(2,1)S(1)}, bf16[2048,2048]{1,0:T(8,128)(2,1)}, u32[]{:S(2)}) %copy-start) | copy-done | bytes 8388632
  77.3 1.3 shard_map.71
  78.6 2.1 %copy-done.1 = bf16[2048,2048]{1,0:T(8,128)(2,1)S(1)} copy-done((bf16[2048,2048]{1,0:T(8,128)(2,1)S(1)}, bf16[2048,2048]{1,0:T(8,128)(2,1)}, u32[]{:S(2)}) %copy-start.1) | copy-done | bytes 8388632
  80.7 1.3 shard_map.72.refs_7_.refs_1_
  82.0 1.3 shard_map.73.refs_8_.refs_2_
  83.3 1.3 shard_map.75.z_ref.refs_3_
  85.3 1.4 collective-permute-done.13.refs_3_
  86.7 2.0 %shard_map.69 = (bf16[512,2048]{1,0:T(8,128)(2,1)S(1)}, bf16[64,2048]{1,0:T(8,128)(2,1)S(1)}) custom-call(s32[2,512]{1,0:T(2,128)S(1)} %shard_map.68.own_ref.own_in.refs_0_, s32[2,512]{1,0:T(2,128)S(1)} %collective-permute-done.6.other_ref.refs_4_, bf16[256,2048]{1,0:T(8,128)(2,1)S(1)} %copy-done.4, bf16[256,2048]{1,0:T(8,128)(2,1)S(1)} %collective-permute-done.11.refs_1_), custom_call_target="tpu_custom_call" | custom-call | flops 1073741824 | bytes 4464640 | tf_op jit(solution)/shard_map/pallas_call | solution.py:39
  88.7 3.4 %shard_map.70 = (bf16[512,2048]{1,0:T(8,128)(2,1)S(1)}, bf16[128,2048]{1,0:T(8,128)(2,1)S(1)}) custom-call(s32[2,512]{1,0:T(2,128)S(1)} %shard_map.68.own_ref.own_in.refs_0_, s32[2,512]{1,0:T(2,128)S(1)} %collective-permute-done.6.other_ref.refs_4_, bf16[256,2048]{1,0:T(8,128)(2,1)S(1)} %collective-permute-done.7.refs_0_, ...), custom_call_target="tpu_custom_call" | custom-call | flops 2147483648 | bytes 8921088 | tf_op jit(solution)/shard_map/pallas_call | solution.py:39
  92.1 3.8 %shard_map.74 = (bf16[128,2048]{1,0:T(8,128)(2,1)S(1)}, bf16[128,2048]{1,0:T(8,128)(2,1)S(1)}, bf16[128,2048]{1,0:T(8,128)(2,1)S(1)}, bf16[128,2048]{1,0:T(8,128...) custom-call(s32[2,512]{1,0:T(2,128)S(1)} %shard_map.68.own_ref.own_i, ...), custom_call_target="tpu_custom_call" | custom-call | flops 1610612736 | bytes 10105344 | tf_op jit(solution)/shard_map/pallas_call | solution.py:39
  96.7 1.8 %collective-permute-start.22 = (f32[2,512]{1,0:T(2,128)S(1)}, f32[2,512]{1,0:T(2,128)S(1)}, u32[]{:S(2)}, u32[]{:S(2)}) collective-permute-start(f32[2,512]{1,0:T(2,128)S(1)} %get-tuple-element.50.refs_4_.refs_0_), channel_id=1, source_target_pairs={{0,2},{1,3},{2,4},{3,5},{4,6},{5,7},{6,0},{7,1},{8,10},{9,11},{10,... | collective-permute-start | bytes 12296 | tf_op jit(solution)/shard_map/ppermute | solution.py:323
  99.3 1.6 collective-permute-start.24
  100.8 1.3 collective-permute-done.22.refs_5_.refs_1_
  103.3 1.8 %collective-permute-start.25 = (bf16[64,2048]{1,0:T(8,128)(2,1)S(1)}, bf16[64,2048]{1,0:T(8,128)(2,1)S(1)}, u32[]{:S(2)}, u32[]{:S(2)}) collective-permute-start(bf16[64,2048]{1,0:T(8,128)(2,1)S(1)} %get-tuple-element.55), channel_id=1, source_target_pairs={{0,2},{1,3},{2,4},{3,5},{4,6},{5,7},{6,0},{7,1},{8,10},{9,11},{10,... | collective-permute-start | bytes 786440 | tf_op jit(solution)/shard_map/ppermute | solution.py:323
  105.2 2.1 %collective-permute-start.28 = (bf16[64,2048]{1,0:T(8,128)(2,1)S(1)}, bf16[64,2048]{1,0:T(8,128)(2,1)S(1)}, u32[]{:S(2)}, u32[]{:S(2)}) collective-permute-start(bf16[64,2048]{1,0:T(8,128)(2,1)S(1)} %get-tuple-element.59), channel_id=1, source_target_pairs={{0,6},{1,7},{2,0},{3,1},{4,2},{5,3},{6,4},{7,5},{8,14},{9,15},{10,... | collective-permute-start | bytes 786440 | tf_op jit(solution)/shard_map/ppermute | solution.py:323
  108.7 5.6 %collective-permute-done.25 = bf16[64,2048]{1,0:T(8,128)(2,1)S(1)} collective-permute-done((bf16[64,2048]{1,0:T(8,128)(2,1)S(1)}, bf16[64,2048]{1,0:T(8,128)(2,1)S(1)}, u32[]{:S(2)}, u32[]{:S(2)}) %collective-permute-start.25) | collective-permute-done | bytes 262176 | tf_op jit(solution)/shard_map/ppermute | solution.py:323
  114.5 3.7 %collective-permute-done.28 = bf16[64,2048]{1,0:T(8,128)(2,1)S(1)} collective-permute-done((bf16[64,2048]{1,0:T(8,128)(2,1)S(1)}, bf16[64,2048]{1,0:T(8,128)(2,1)S(1)}, u32[]{:S(2)}, u32[]{:S(2)}) %collective-permute-start.28) | collective-permute-done | bytes 262176 | tf_op jit(solution)/shard_map/ppermute | solution.py:323
  118.3 3.6 %collective-permute-start.29 = (bf16[64,2048]{1,0:T(8,128)(2,1)S(1)}, bf16[64,2048]{1,0:T(8,128)(2,1)S(1)}, u32[]{:S(2)}, u32[]{:S(2)}) collective-permute-start(bf16[64,2048]{1,0:T(8,128)(2,1)S(1)} %add_convert_fusion.3), channel_id=1, source_target_pairs={{0,6},{1,7},{2,0},{3,1},{4,2},{5,3},{6,4},{7,5},{8,14},{9,15},{10,... | collective-permute-start | bytes 786440 | tf_op jit(solution)/shard_map/ppermute | solution.py:323
  121.9 1.5 shard_map.83
  124.1 1.5 collective-permute-done.26
  125.8 1.6 shard_map.82
  127.4 1.4 collective-permute-start.34
  129.5 1.5 shard_map.84
  131.0 4.6 %collective-permute-done.35 = bf16[128,2048]{1,0:T(8,128)(2,1)S(1)} collective-permute-done((bf16[128,2048]{1,0:T(8,128)(2,1)S(1)}, bf16[128,2048]{1,0:T(8,128)(2,1)S(1)}, u32[]{:S(2)}, u32[]{:S(2)}) %collective-permute-start.35) | collective-permute-done | bytes 524320 | tf_op jit(solution)/shard_map/ppermute | solution.py:331
  136.4 14.4 %collective-permute-done.37 = bf16[128,2048]{1,0:T(8,128)(2,1)S(1)} collective-permute-done((bf16[128,2048]{1,0:T(8,128)(2,1)S(1)}, bf16[128,2048]{1,0:T(8,128)(2,1)S(1)}, u32[]{:S(2)}, u32[]{:S(2)}) %collective-permute-start.37) | collective-permute-done | bytes 524320 | tf_op jit(solution)/shard_map/ppermute | solution.py:331
  151.9 1.2 collective-permute-start.38
  153.2 4.6 %collective-permute-start.30 = (bf16[64,2048]{1,0:T(8,128)(2,1)S(1)}, bf16[64,2048]{1,0:T(8,128)(2,1)S(1)}, u32[]{:S(2)}, u32[]{:S(2)}) collective-permute-start(bf16[64,2048]{1,0:T(8,128)(2,1)S(1)} %add_convert_fusion.2), channel_id=1, source_target_pairs={{0,6},{1,7},{2,0},{3,1},{4,2},{5,3},{6,4},{7,5},{8,14},{9,15},{10,... | collective-permute-start | bytes 786440 | tf_op jit(solution)/shard_map/ppermute | solution.py:323
  157.8 1.5 shard_map.81
  159.2 2.4 %collective-permute-done.30.down_in_ref = bf16[64,2048]{1,0:T(8,128)(2,1)S(1)} collective-permute-done((bf16[64,2048]{1,0:T(8,128)(2,1)S(1)}, bf16[64,2048]{1,0:T(8,128)(2,1)S(1)}, u32[]{:S(2)}, u32[]{:S(2)}) %collective-permute-start.30) | collective-permute-done | bytes 262176 | tf_op jit(solution)/shard_map/ppermute | solution.py:323
  161.6 3.7 %shard_map.79 = bf16[128,2048]{1,0:T(8,128)(2,1)} custom-call(f32[64,2048]{1,0:T(8,128)S(1)} %get-tuple-element.51.up_ref, bf16[64,2048]{1,0:T(8,128)(2,1)S(1)} %collective-permute-done.27.up_in_ref, f32[64,2048]{1,0:T(8,128)S(1)} %get-tuple-element.56.down_ref, bf16[64,2048]{1,0:T(8,128)(2,1)S(1)} %collective-permute-done.30.down_in_ref, ...), custom_call_target="tpu_custom_call" | custom-call | flops 1073741824 | bytes 11534336 | tf_op jit(solution)/shard_map/pallas_call | solution.py:39
  165.4 1.8 %add_add_fusion = f32[256,2048]{1,0:T(8,128)} fusion(f32[256,2048]{1,0:T(8,128)S(1)} %shard_map.81, bf16[128,2048]{1,0:T(8,128)(2,1)S(1)} %collective-permute-done.36, bf16[128,2048]{1,0:T(8,128)(2,1)S(1)} %collective-permute-done.34, bf16[128,2048]{1,0:T(8,128)(2,1)S(1)} %collective-permute-done.39, bf16[128,2048]{1,0:T(8,128)(2,1)S(1)} %collective-permute-done.38), kind=kLoop, calls=%fused_computation | loop fusion | flops 5242880 | bytes 6291456 | tf_op jit(solution)/shard_map/add | solution.py:494
  (69 shorter events, 16.4 us)
Async XLA Ops:
  0.6 61.8 %collective-permute-start.7 = (bf16[256,2048]{1,0:T(8,128)(2,1)}, bf16[256,2048]{1,0:T(8,128)(2,1)S(1)}, u32[]{:S(2)}, u32[]{:S(2)}) collective-permute-start(bf16[256,2048]{1,0:T(8,128)(2,1)} %refs_0_.1), channel_id=1, source_target_pairs={{0,8},{8,0},{16,24},{24,16},{1,9},{9,1},{17,25},{25,17},{2,10},{10... | collective-permute-start | bytes 3145736 | tf_op jit(solution)/shard_map/ppermute | solution.py:331
  3.7 58.8 %collective-permute-start.8 = (bf16[256,2048]{1,0:T(8,128)(2,1)}, bf16[256,2048]{1,0:T(8,128)(2,1)S(1)}, u32[]{:S(2)}, u32[]{:S(2)}) collective-permute-start(bf16[256,2048]{1,0:T(8,128)(2,1)} %refs_0_.1), channel_id=1, source_target_pairs={{0,16},{8,24},{16,0},{24,8},{1,17},{9,25},{17,1},{25,9},{2,18},{10... | collective-permute-start | bytes 3145736 | tf_op jit(solution)/shard_map/ppermute | solution.py:331
  6.3 38.4 %collective-permute-start.16 = (bf16[64,2048]{1,0:T(8,128)(2,1)S(1)}, bf16[64,2048]{1,0:T(8,128)(2,1)S(1)}, u32[]{:S(2)}, u32[]{:S(2)}) collective-permute-start(bf16[64,2048]{1,0:T(8,128)(2,1)S(1)} %get-tuple-element.71.x_up), channel_id=1, source_target_pairs={{0,2},{1,3},{2,4},{3,5},{4,6},{5,7},{6,0},{7,1},{8,10},{9,11},{10,... | collective-permute-start | bytes 786440 | tf_op jit(solution)/shard_map/ppermute | solution.py:323
  7.9 36.8 %collective-permute-start.17 = (bf16[64,2048]{1,0:T(8,128)(2,1)S(1)}, bf16[64,2048]{1,0:T(8,128)(2,1)S(1)}, u32[]{:S(2)}, u32[]{:S(2)}) collective-permute-start(bf16[64,2048]{1,0:T(8,128)(2,1)S(1)} %get-tuple-element.70.x_down), channel_id=1, source_target_pairs={{0,6},{1,7},{2,0},{3,1},{4,2},{5,3},{6,4},{7,5},{8,14},{9,15},{10,... | collective-permute-start | bytes 786440 | tf_op jit(solution)/shard_map/ppermute | solution.py:323
  10.1 11.2 %collective-permute-start = (s32[1,128]{1,0:T(1,128)}, s32[1,128]{1,0:T(1,128)S(1)}, u32[]{:S(2)}, u32[]{:S(2)}) collective-permute-start(s32[1,128]{1,0:T(1,128)} %bitcast.1), channel_id=1, source_target_pairs={{0,2},{1,3},{2,4},{3,5},{4,6},{5,7},{6,0},{7,1},{8,10},{9,11},{10,... | collective-permute-start | bytes 1544 | tf_op jit(solution)/shard_map/ppermute | solution.py:323
  21.3 4.6 %collective-permute-start.1 = (s32[1,128]{1,0:T(1,128)}, s32[1,128]{1,0:T(1,128)S(1)}, u32[]{:S(2)}, u32[]{:S(2)}) collective-permute-start(s32[1,128]{1,0:T(1,128)} %bitcast.2), channel_id=1, source_target_pairs={{0,4},{1,5},{2,6},{3,7},{4,0},{5,1},{6,2},{7,3},{8,12},{9,13},{10,... | collective-permute-start | bytes 1544 | tf_op jit(solution)/shard_map/ppermute | solution.py:323
  25.9 3.7 %collective-permute-start.2 = (s32[1,128]{1,0:T(1,128)}, s32[1,128]{1,0:T(1,128)S(1)}, u32[]{:S(2)}, u32[]{:S(2)}) collective-permute-start(s32[1,128]{1,0:T(1,128)} %bitcast.3), channel_id=1, source_target_pairs={{0,6},{1,7},{2,0},{3,1},{4,2},{5,3},{6,4},{7,5},{8,14},{9,15},{10,... | collective-permute-start | bytes 1544 | tf_op jit(solution)/shard_map/ppermute | solution.py:323
  29.6 3.8 %collective-permute-start.3 = (s32[4,32]{1,0:T(4,128)}, s32[4,32]{1,0:T(4,128)S(1)}, u32[]{:S(2)}, u32[]{:S(2)}) collective-permute-start(s32[4,32]{1,0:T(4,128)} %refs_4_.1), channel_id=1, source_target_pairs={{0,8},{8,0},{16,24},{24,16},{1,9},{9,1},{17,25},{25,17},{2,10},{10... | collective-permute-start | bytes 1544 | tf_op jit(solution)/shard_map/ppermute | solution.py:331
  33.4 3.8 %collective-permute-start.4 = (s32[4,32]{1,0:T(4,128)}, s32[4,32]{1,0:T(4,128)S(1)}, u32[]{:S(2)}, u32[]{:S(2)}) collective-permute-start(s32[4,32]{1,0:T(4,128)} %refs_4_.1), channel_id=1, source_target_pairs={{0,16},{8,24},{16,0},{24,8},{1,17},{9,25},{17,1},{25,9},{2,18},{10... | collective-permute-start | bytes 1544 | tf_op jit(solution)/shard_map/ppermute | solution.py:331
  37.2 4.7 %collective-permute-start.5 = (s32[4,32]{1,0:T(4,128)}, s32[4,32]{1,0:T(4,128)S(1)}, u32[]{:S(2)}, u32[]{:S(2)}) collective-permute-start(s32[4,32]{1,0:T(4,128)} %refs_4_.1), channel_id=1, source_target_pairs={{0,24},{8,16},{16,8},{24,0},{1,25},{9,17},{17,9},{25,1},{2,26},{10... | collective-permute-start | bytes 1544 | tf_op jit(solution)/shard_map/ppermute | solution.py:331
  41.9 0.7 copy-start.2
  42.6 0.7 copy-start.3
  43.3 1.2 collective-permute-start.6
  44.5 40.2 %collective-permute-start.11 = (bf16[256,2048]{1,0:T(8,128)(2,1)}, bf16[256,2048]{1,0:T(8,128)(2,1)S(1)}, u32[]{:S(2)}, u32[]{:S(2)}) collective-permute-start(bf16[256,2048]{1,0:T(8,128)(2,1)} %refs_0_.1), channel_id=1, source_target_pairs={{0,1},{1,0},{2,3},{3,2},{4,5},{5,4},{6,7},{7,6},{8,9},{9,8},{10,11... | collective-permute-start | bytes 3145736 | tf_op jit(solution)/shard_map/ppermute | solution.py:327
  44.7 11.0 %collective-permute-start.18 = (bf16[64,2048]{1,0:T(8,128)(2,1)S(1)}, bf16[64,2048]{1,0:T(8,128)(2,1)S(1)}, u32[]{:S(2)}, u32[]{:S(2)}) collective-permute-start(bf16[64,2048]{1,0:T(8,128)(2,1)S(1)} %collective-permute-done.16.x_up), channel_id=1, source_target_pairs={{0,2},{1,3},{2,4},{3,5},{4,6},{5,7},{6,0},{7,1},{8,10},{9,11},{10,... | collective-permute-start | bytes 786440 | tf_op jit(solution)/shard_map/ppermute | solution.py:323
  44.7 14.2 %collective-permute-start.19 = (bf16[64,2048]{1,0:T(8,128)(2,1)S(1)}, bf16[64,2048]{1,0:T(8,128)(2,1)S(1)}, u32[]{:S(2)}, u32[]{:S(2)}) collective-permute-start(bf16[64,2048]{1,0:T(8,128)(2,1)S(1)} %collective-permute-done.17.x_down), channel_id=1, source_target_pairs={{0,6},{1,7},{2,0},{3,1},{4,2},{5,3},{6,4},{7,5},{8,14},{9,15},{10,... | collective-permute-start | bytes 786440 | tf_op jit(solution)/shard_map/ppermute | solution.py:323
  55.7 13.9 %collective-permute-start.20 = (bf16[64,2048]{1,0:T(8,128)(2,1)S(1)}, bf16[64,2048]{1,0:T(8,128)(2,1)S(1)}, u32[]{:S(2)}, u32[]{:S(2)}) collective-permute-start(bf16[64,2048]{1,0:T(8,128)(2,1)S(1)} %collective-permute-done.18.x_up), channel_id=1, source_target_pairs={{0,2},{1,3},{2,4},{3,5},{4,6},{5,7},{6,0},{7,1},{8,10},{9,11},{10,... | collective-permute-start | bytes 786440 | tf_op jit(solution)/shard_map/ppermute | solution.py:323
  58.9 14.5 %collective-permute-start.21 = (bf16[64,2048]{1,0:T(8,128)(2,1)S(1)}, bf16[64,2048]{1,0:T(8,128)(2,1)S(1)}, u32[]{:S(2)}, u32[]{:S(2)}) collective-permute-start(bf16[64,2048]{1,0:T(8,128)(2,1)S(1)} %collective-permute-done.19.x_down), channel_id=1, source_target_pairs={{0,6},{1,7},{2,0},{3,1},{4,2},{5,3},{6,4},{7,5},{8,14},{9,15},{10,... | collective-permute-start | bytes 786440 | tf_op jit(solution)/shard_map/ppermute | solution.py:323
  62.4 26.3 %collective-permute-start.9 = (bf16[256,2048]{1,0:T(8,128)(2,1)S(1)}, bf16[256,2048]{1,0:T(8,128)(2,1)S(1)}, u32[]{:S(2)}, u32[]{:S(2)}) collective-permute-start(bf16[256,2048]{1,0:T(8,128)(2,1)S(1)} %collective-permute-done.7.refs_0_), channel_id=1, source_target_pairs={{0,1},{1,0},{2,3},{3,2},{4,5},{5,4},{6,7},{7,6},{8,9},{9,8},{10,11... | collective-permute-start | bytes 3145736 | tf_op jit(solution)/shard_map/ppermute | solution.py:327
  62.5 26.2 %collective-permute-start.10 = (bf16[256,2048]{1,0:T(8,128)(2,1)S(1)}, bf16[256,2048]{1,0:T(8,128)(2,1)S(1)}, u32[]{:S(2)}, u32[]{:S(2)}) collective-permute-start(bf16[256,2048]{1,0:T(8,128)(2,1)S(1)} %collective-permute-done.8.refs_1_), channel_id=1, source_target_pairs={{0,1},{1,0},{2,3},{3,2},{4,5},{5,4},{6,7},{7,6},{8,9},{9,8},{10,11... | collective-permute-start | bytes 3145736 | tf_op jit(solution)/shard_map/ppermute | solution.py:327
  69.6 15.2 %collective-permute-start.12 = (bf16[128,2048]{1,0:T(8,128)(2,1)S(1)}, bf16[128,2048]{1,0:T(8,128)(2,1)S(1)}, u32[]{:S(2)}, u32[]{:S(2)}) collective-permute-start(bf16[128,2048]{1,0:T(8,128)(2,1)S(1)} %slice.16), channel_id=1, source_target_pairs={{0,8},{8,0},{16,24},{24,16},{1,9},{9,1},{17,25},{25,17},{2,10},{10... | collective-permute-start | bytes 1572872 | tf_op jit(solution)/shard_map/ppermute | solution.py:331
  73.4 13.3 %collective-permute-start.13 = (bf16[128,2048]{1,0:T(8,128)(2,1)S(1)}, bf16[128,2048]{1,0:T(8,128)(2,1)S(1)}, u32[]{:S(2)}, u32[]{:S(2)}) collective-permute-start(bf16[128,2048]{1,0:T(8,128)(2,1)S(1)} %slice.17), channel_id=1, source_target_pairs={{0,16},{8,24},{16,0},{24,8},{1,17},{9,25},{17,1},{25,9},{2,18},{10... | collective-permute-start | bytes 1572872 | tf_op jit(solution)/shard_map/ppermute | solution.py:331
  73.9 3.4 %copy-start = (bf16[2048,2048]{1,0:T(8,128)(2,1)S(1)}, bf16[2048,2048]{1,0:T(8,128)(2,1)}, u32[]{:S(2)}) copy-start(bf16[2048,2048]{1,0:T(8,128)(2,1)} %w_ref.9) | copy-start | bytes 25165828
  77.3 3.4 %copy-start.1 = (bf16[2048,2048]{1,0:T(8,128)(2,1)S(1)}, bf16[2048,2048]{1,0:T(8,128)(2,1)}, u32[]{:S(2)}) copy-start(bf16[2048,2048]{1,0:T(8,128)(2,1)} %w_ref.9) | copy-start | bytes 25165828
  84.6 2.2 %copy-start.4 = (bf16[256,2048]{1,0:T(8,128)(2,1)S(1)}, bf16[256,2048]{1,0:T(8,128)(2,1)}, u32[]{:S(2)}) copy-start(bf16[256,2048]{1,0:T(8,128)(2,1)} %refs_0_.1) | copy-start | bytes 3145732
  84.7 37.2 %collective-permute-start.33 = (bf16[512,2048]{1,0:T(8,128)(2,1)S(1)}, bf16[512,2048]{1,0:T(8,128)(2,1)S(1)}, u32[]{:S(2)}, u32[]{:S(2)}) collective-permute-start(bf16[512,2048]{1,0:T(8,128)(2,1)S(1)} %shard_map.80.refs_3_), channel_id=1, source_target_pairs={{0,1},{1,0},{2,3},{3,2},{4,5},{5,4},{6,7},{7,6},{8,9},{9,8},{10,11... | collective-permute-start | bytes 6291464 | tf_op jit(solution)/shard_map/ppermute | solution.py:327
  84.8 7.3 %collective-permute-start.14 = (bf16[128,2048]{1,0:T(8,128)(2,1)S(1)}, bf16[128,2048]{1,0:T(8,128)(2,1)S(1)}, u32[]{:S(2)}, u32[]{:S(2)}) collective-permute-start(bf16[128,2048]{1,0:T(8,128)(2,1)S(1)} %collective-permute-done.12.refs_2_), channel_id=1, source_target_pairs={{0,1},{1,0},{2,3},{3,2},{4,5},{5,4},{6,7},{7,6},{8,9},{9,8},{10,11... | collective-permute-start | bytes 1572872 | tf_op jit(solution)/shard_map/ppermute | solution.py:327
  86.7 5.4 %collective-permute-start.15 = (bf16[128,2048]{1,0:T(8,128)(2,1)S(1)}, bf16[128,2048]{1,0:T(8,128)(2,1)S(1)}, u32[]{:S(2)}, u32[]{:S(2)}) collective-permute-start(bf16[128,2048]{1,0:T(8,128)(2,1)S(1)} %collective-permute-done.13.refs_3_), channel_id=1, source_target_pairs={{0,1},{1,0},{2,3},{3,2},{4,5},{5,4},{6,7},{7,6},{8,9},{9,8},{10,11... | collective-permute-start | bytes 1572872 | tf_op jit(solution)/shard_map/ppermute | solution.py:327
  96.7 5.5 %collective-permute-start.22 = (f32[2,512]{1,0:T(2,128)S(1)}, f32[2,512]{1,0:T(2,128)S(1)}, u32[]{:S(2)}, u32[]{:S(2)}) collective-permute-start(f32[2,512]{1,0:T(2,128)S(1)} %get-tuple-element.50.refs_4_.refs_0_), channel_id=1, source_target_pairs={{0,2},{1,3},{2,4},{3,5},{4,6},{5,7},{6,0},{7,1},{8,10},{9,11},{10,... | collective-permute-start | bytes 12296 | tf_op jit(solution)/shard_map/ppermute | solution.py:323
  98.4 4.5 %collective-permute-start.23 = (f32[2,512]{1,0:T(2,128)S(1)}, f32[2,512]{1,0:T(2,128)S(1)}, u32[]{:S(2)}, u32[]{:S(2)}) collective-permute-start(f32[2,512]{1,0:T(2,128)S(1)} %get-tuple-element.50.refs_4_.refs_0_), channel_id=1, source_target_pairs={{0,4},{1,5},{2,6},{3,7},{4,0},{5,1},{6,2},{7,3},{8,12},{9,13},{10,... | collective-permute-start | bytes 12296 | tf_op jit(solution)/shard_map/ppermute | solution.py:323
  99.3 3.7 %collective-permute-start.24 = (f32[2,512]{1,0:T(2,128)S(1)}, f32[2,512]{1,0:T(2,128)S(1)}, u32[]{:S(2)}, u32[]{:S(2)}) collective-permute-start(f32[2,512]{1,0:T(2,128)S(1)} %get-tuple-element.50.refs_4_.refs_0_), channel_id=1, source_target_pairs={{0,6},{1,7},{2,0},{3,1},{4,2},{5,3},{6,4},{7,5},{8,14},{9,15},{10,... | collective-permute-start | bytes 12296 | tf_op jit(solution)/shard_map/ppermute | solution.py:323
  103.3 11.0 %collective-permute-start.25 = (bf16[64,2048]{1,0:T(8,128)(2,1)S(1)}, bf16[64,2048]{1,0:T(8,128)(2,1)S(1)}, u32[]{:S(2)}, u32[]{:S(2)}) collective-permute-start(bf16[64,2048]{1,0:T(8,128)(2,1)S(1)} %get-tuple-element.55), channel_id=1, source_target_pairs={{0,2},{1,3},{2,4},{3,5},{4,6},{5,7},{6,0},{7,1},{8,10},{9,11},{10,... | collective-permute-start | bytes 786440 | tf_op jit(solution)/shard_map/ppermute | solution.py:323
  105.2 13.1 %collective-permute-start.28 = (bf16[64,2048]{1,0:T(8,128)(2,1)S(1)}, bf16[64,2048]{1,0:T(8,128)(2,1)S(1)}, u32[]{:S(2)}, u32[]{:S(2)}) collective-permute-start(bf16[64,2048]{1,0:T(8,128)(2,1)S(1)} %get-tuple-element.59), channel_id=1, source_target_pairs={{0,6},{1,7},{2,0},{3,1},{4,2},{5,3},{6,4},{7,5},{8,14},{9,15},{10,... | collective-permute-start | bytes 786440 | tf_op jit(solution)/shard_map/ppermute | solution.py:323
  108.1 13.8 %collective-permute-start.31 = (bf16[128,512]{1,0:T(8,128)(2,1)S(1)}, bf16[128,512]{1,0:T(8,128)(2,1)S(1)}, u32[]{:S(2)}, u32[]{:S(2)}) collective-permute-start(bf16[128,512]{1,0:T(8,128)(2,1)S(1)} %get-tuple-element.63), channel_id=1, source_target_pairs={{0,1},{1,0},{2,3},{3,2},{4,5},{5,4},{6,7},{7,6},{8,9},{9,8},{10,11... | collective-permute-start | bytes 393224 | tf_op jit(solution)/shard_map/ppermute | solution.py:327
  108.2 13.7 %collective-permute-start.32 = (f32[1,512]{1,0:T(1,128)S(1)}, f32[1,512]{1,0:T(1,128)S(1)}, u32[]{:S(2)}, u32[]{:S(2)}) collective-permute-start(f32[1,512]{1,0:T(1,128)S(1)} %get-tuple-element.62.refs_2_), channel_id=1, source_target_pairs={{0,1},{1,0},{2,3},{3,2},{4,5},{5,4},{6,7},{7,6},{8,9},{9,8},{10,11... | collective-permute-start | bytes 6152 | tf_op jit(solution)/shard_map/ppermute | solution.py:327
  114.4 11.3 %collective-permute-start.26 = (bf16[64,2048]{1,0:T(8,128)(2,1)S(1)}, bf16[64,2048]{1,0:T(8,128)(2,1)S(1)}, u32[]{:S(2)}, u32[]{:S(2)}) collective-permute-start(bf16[64,2048]{1,0:T(8,128)(2,1)S(1)} %add_convert_fusion.5), channel_id=1, source_target_pairs={{0,2},{1,3},{2,4},{3,5},{4,6},{5,7},{6,0},{7,1},{8,10},{9,11},{10,... | collective-permute-start | bytes 786440 | tf_op jit(solution)/shard_map/ppermute | solution.py:323
  118.3 33.6 %collective-permute-start.29 = (bf16[64,2048]{1,0:T(8,128)(2,1)S(1)}, bf16[64,2048]{1,0:T(8,128)(2,1)S(1)}, u32[]{:S(2)}, u32[]{:S(2)}) collective-permute-start(bf16[64,2048]{1,0:T(8,128)(2,1)S(1)} %add_convert_fusion.3), channel_id=1, source_target_pairs={{0,6},{1,7},{2,0},{3,1},{4,2},{5,3},{6,4},{7,5},{8,14},{9,15},{10,... | collective-permute-start | bytes 786440 | tf_op jit(solution)/shard_map/ppermute | solution.py:323
  123.5 12.2 %collective-permute-start.35 = (bf16[128,2048]{1,0:T(8,128)(2,1)S(1)}, bf16[128,2048]{1,0:T(8,128)(2,1)S(1)}, u32[]{:S(2)}, u32[]{:S(2)}) collective-permute-start(bf16[128,2048]{1,0:T(8,128)(2,1)S(1)} %get-tuple-element.66), channel_id=1, source_target_pairs={{0,16},{8,24},{16,0},{24,8},{1,17},{9,25},{17,1},{25,9},{2,18},{10... | collective-permute-start | bytes 1572872 | tf_op jit(solution)/shard_map/ppermute | solution.py:331
  125.8 27.4 %collective-permute-start.27 = (bf16[64,2048]{1,0:T(8,128)(2,1)S(1)}, bf16[64,2048]{1,0:T(8,128)(2,1)S(1)}, u32[]{:S(2)}, u32[]{:S(2)}) collective-permute-start(bf16[64,2048]{1,0:T(8,128)(2,1)S(1)} %add_convert_fusion.4), channel_id=1, source_target_pairs={{0,2},{1,3},{2,4},{3,5},{4,6},{5,7},{6,0},{7,1},{8,10},{9,11},{10,... | collective-permute-start | bytes 786440 | tf_op jit(solution)/shard_map/ppermute | solution.py:323
  127.4 38.0 %collective-permute-start.34 = (bf16[128,2048]{1,0:T(8,128)(2,1)S(1)}, bf16[128,2048]{1,0:T(8,128)(2,1)S(1)}, u32[]{:S(2)}, u32[]{:S(2)}) collective-permute-start(bf16[128,2048]{1,0:T(8,128)(2,1)S(1)} %get-tuple-element.64), channel_id=1, source_target_pairs={{0,8},{8,0},{16,24},{24,16},{1,9},{9,1},{17,25},{25,17},{2,10},{10... | collective-permute-start | bytes 1572872 | tf_op jit(solution)/shard_map/ppermute | solution.py:331
  128.8 22.0 %collective-permute-start.37 = (bf16[128,2048]{1,0:T(8,128)(2,1)S(1)}, bf16[128,2048]{1,0:T(8,128)(2,1)S(1)}, u32[]{:S(2)}, u32[]{:S(2)}) collective-permute-start(bf16[128,2048]{1,0:T(8,128)(2,1)S(1)} %get-tuple-element.68), channel_id=1, source_target_pairs={{0,8},{8,0},{16,24},{24,16},{1,9},{9,1},{17,25},{25,17},{2,10},{10... | collective-permute-start | bytes 1572872 | tf_op jit(solution)/shard_map/ppermute | solution.py:331
  135.6 29.7 %collective-permute-start.39 = (bf16[128,2048]{1,0:T(8,128)(2,1)S(1)}, bf16[128,2048]{1,0:T(8,128)(2,1)S(1)}, u32[]{:S(2)}, u32[]{:S(2)}) collective-permute-start(bf16[128,2048]{1,0:T(8,128)(2,1)S(1)} %get-tuple-element.69), channel_id=1, source_target_pairs={{0,16},{8,24},{16,0},{24,8},{1,17},{9,25},{17,1},{25,9},{2,18},{10... | collective-permute-start | bytes 1572872 | tf_op jit(solution)/shard_map/ppermute | solution.py:331
  150.8 14.6 %collective-permute-start.36 = (bf16[128,2048]{1,0:T(8,128)(2,1)S(1)}, bf16[128,2048]{1,0:T(8,128)(2,1)S(1)}, u32[]{:S(2)}, u32[]{:S(2)}) collective-permute-start(bf16[128,2048]{1,0:T(8,128)(2,1)S(1)} %add_convert_fusion.1), channel_id=1, source_target_pairs={{0,8},{8,0},{16,24},{24,16},{1,9},{9,1},{17,25},{25,17},{2,10},{10... | collective-permute-start | bytes 1572872 | tf_op jit(solution)/shard_map/ppermute | solution.py:331
  151.9 13.5 %collective-permute-start.38 = (bf16[128,2048]{1,0:T(8,128)(2,1)S(1)}, bf16[128,2048]{1,0:T(8,128)(2,1)S(1)}, u32[]{:S(2)}, u32[]{:S(2)}) collective-permute-start(bf16[128,2048]{1,0:T(8,128)(2,1)S(1)} %add_convert_fusion), channel_id=1, source_target_pairs={{0,16},{8,24},{16,0},{24,8},{1,17},{9,25},{17,1},{25,9},{2,18},{10... | collective-permute-start | bytes 1572872 | tf_op jit(solution)/shard_map/ppermute | solution.py:331
  153.2 8.5 %collective-permute-start.30 = (bf16[64,2048]{1,0:T(8,128)(2,1)S(1)}, bf16[64,2048]{1,0:T(8,128)(2,1)S(1)}, u32[]{:S(2)}, u32[]{:S(2)}) collective-permute-start(bf16[64,2048]{1,0:T(8,128)(2,1)S(1)} %add_convert_fusion.2), channel_id=1, source_target_pairs={{0,6},{1,7},{2,0},{3,1},{4,2},{5,3},{6,4},{7,5},{8,14},{9,15},{10,... | collective-permute-start | bytes 786440 | tf_op jit(solution)/shard_map/ppermute | solution.py:323

commit v2 on v1

--- a/solution.py
+++ b/solution.py
@@ -96,11 +96,29 @@
     return ((ids - first) == lane).astype(BF16)
 
 
-def pick_kernel(plan, own_rows, each, own_ref, other_ref, *refs):
+def pick_kernel(plan, own_rows, each, slots, scale, own_ref, other_ref, *refs):
     n = len(plan)
-    blocks = refs[:n]
-    base_ref = refs[n] if len(refs) > n + 2 else None
-    pick_rows(plan, own_rows, each, own_ref, other_ref, blocks, base_ref, [refs[-2]], refs[-1], 0)
+    blocks, refs = refs[:n], refs[n:]
+    base_ref = None
+    if slots is not None:
+        base_ref, refs = refs[0], refs[1:]
+    if not slots:
+        pos_ref, row_ref = refs
+        pick_rows(plan, own_rows, each, own_ref, other_ref, blocks, base_ref, [pos_ref], row_ref, 0)
+        return
+    before, zs = refs[0], refs[1 : 1 + slots]
+    pos_ref, row_ref, logit_ref = refs[1 + slots :]
+    at = before.shape[0]
+    row_ref[:at] = before[...]
+    pick_rows(plan, own_rows, each, own_ref, other_ref, blocks, base_ref, [pos_ref], row_ref, at)
+    logits = 0.0
+    width = row_ref.shape[1]
+    step = chunk_of(width)
+    for c in range(0, width, step):
+        cols = slice(c, c + step)
+        z = jnp.concatenate([z[:, cols] for z in zs], axis=0)
+        logits = logits + dot(row_ref[:, cols], z, 1, 1)
+    logit_ref[...] = scale * logits
 
 
 def pick_rows(plan, own_rows, each, own_ref, other_ref, blocks, base_ref, pos_refs, row_ref, at):
@@ -132,22 +150,25 @@
             row_ref[at + o * each : at + (o + 1) * each, cols] = got.astype(BF16)
 
 
-def scores(scale, z_of, neg_ref, pos_refs, here, logit_ref, pos_out):
+def scores(scale, z_of, neg_ref, done, pos_refs, here, logit_ref, pos_out):
     width = neg_ref.shape[1]
     step = chunk_of(width)
     lanes = min(width, 128)
     slot = pos_refs[0].shape[0]
+    skip = 0 if done is None else done.shape[0]
     logits = 0.0
     pos = [jnp.zeros((slot, lanes), F32) for _ in pos_refs]
     for c in range(0, width, step):
         cols = slice(c, c + step)
         z = z_of(cols)
-        logits = logits + dot(neg_ref[:, cols], z, 1, 1)
+        logits = logits + dot(neg_ref[skip:, cols], z, 1, 1)
         for k, ref in enumerate(pos_refs):
             prod = z[k * slot : (k + 1) * slot].astype(F32) * ref[:, cols].astype(F32)
             for d in range(0, step, lanes):
                 pos[k] = pos[k] + prod[:, d : d + lanes]
     logits = logits * scale
+    if done is not None:
+        logits = jnp.concatenate([done[...], logits], axis=0)
     pos = [scale * jnp.sum(jnp.transpose(p), axis=0, keepdims=True) for p in pos]
     pos = pos[0] if len(pos) == 1 else jnp.concatenate(pos, axis=1)
     top = jnp.max(logits, axis=0, keepdims=True)
@@ -161,10 +182,10 @@
 
 def main_kernel(plan, own_rows, each, slots, scale, own_ref, other_ref, base_ref, *refs):
     n = len(plan)
-    early = refs[:2]
-    blocks = refs[2 : 2 + n]
-    zs = refs[2 + n : 2 + n + slots]
-    rest = refs[2 + n + slots :]
+    early, done = refs[:2], refs[2]
+    blocks = refs[3 : 3 + n]
+    zs = refs[3 + n : 3 + n + slots]
+    rest = refs[3 + n + slots :]
     pos_refs, (neg_out, logit_ref, pos_out, stat_ref) = rest[: slots + 1], rest[slots + 1 :]
     at = 0
     for e in early:
@@ -177,7 +198,7 @@
 
     users = slots * pos_refs[0].shape[0]
     here = is_here(own_ref[0:1, :users], own_rows)
-    top, total = scores(scale, z_of, neg_out, pos_refs[:slots], here, logit_ref, pos_out)
+    top, total = scores(scale, z_of, neg_out, done, pos_refs[:slots], here, logit_ref, pos_out)
     stat_ref[0:1] = top
     stat_ref[1:2] = total
 
@@ -191,7 +212,7 @@
     slot = pos_ref.shape[0]
     users = own_ref.shape[1]
     here = is_here(own_ref[0:1, users - slot :], own_rows)
-    top, total = scores(scale, z_of, neg_ref, [pos_ref], here, logit_ref, pos_out)
+    top, total = scores(scale, z_of, neg_ref, None, [pos_ref], here, logit_ref, pos_out)
     stat_ref[:, : users - slot] = stat_in[...]
     stat_ref[0:1, users - slot :] = top
     stat_ref[1:2, users - slot :] = total
@@ -241,25 +262,12 @@
         down_ref[:, cols] = grad[half:].astype(down_ref.dtype)
 
 
-def lead_kernel(chips, own_rows, scale, own_ref, logit_ref, pos_ref, neg_ref, rows_ref, *refs):
-    stats, (up_ref, down_ref) = refs[:chips], refs[chips:]
+def lead_kernel(chips, own_rows, scale, order, each, own_in, logit_ref, pos_ref, *refs):
+    logit_t, pos_t, neg_ref, rows_ref = refs[:4]
+    stats, refs = refs[4 : 4 + chips], refs[4 + chips :]
+    up_ref, down_ref, own_ref, other_ref, weight_ref, all_ref = refs
     slot = rows_ref.shape[0]
-    lanes = slice(slot, 2 * slot)
-    here = is_here(own_ref[0:1, lanes], own_rows)
-    prob, weight = slot_weights(
-        stats, chips, 1, slot, logit_ref[:, lanes], pos_ref[:, lanes], here
-    )
-    slot_grad(scale, prob, weight, neg_ref, rows_ref, up_ref, down_ref)
-
-
-def rest_kernel(chips, own_rows, scale, order, each, own_in, logit_ref, pos_ref, logit_t, pos_t, *refs):
-    neg_ref, refs = refs[0], refs[1:]
-    rows, refs = refs[: chips - 1], refs[chips - 1 :]
-    stats, refs = refs[:chips], refs[chips:]
-    own_ref, other_ref, weight_ref = refs[:3]
-    parts = refs[3:]
-    slot = rows[0].shape[0]
-    at = 0
+    mine = own_ref.shape[0]
     for k in range(chips):
         lanes = slice(k * slot, (k + 1) * slot)
         last = k == chips - 1
@@ -268,34 +276,47 @@
         here = is_here(own_in[0:1, lanes], own_rows)
         prob, weight = slot_weights(stats, chips, k, slot, logit, pos, here)
         weight_ref[:, lanes] = weight
+        all_ref[:, lanes] = prob
+        other_ref[mine:, lanes] = jnp.broadcast_to(weight, (16, slot)).astype(BF16)
         for n, (side, owner) in enumerate(order):
             to = other_ref if side else own_ref
             to[owner * each : (owner + 1) * each, lanes] = prob[n * each : (n + 1) * each]
-        if k != 1:
-            slot_grad(scale, prob, weight, neg_ref, rows[at], parts[2 * at], parts[2 * at + 1])
-            at += 1
-
-
-def item_kernel(scale, k, each, *refs):
-    sides = [refs[4 * s : 4 * s + 4] for s in range(2)]
-    outs = refs[8:]
+        if k == 1:
+            slot_grad(scale, prob, weight, neg_ref, rows_ref, up_ref, down_ref)
+
+
+def rest_kernel(chips, scale, all_ref, weight_ref, neg_ref, *refs):
+    rows, parts = refs[: chips - 1], refs[chips - 1 :]
+    slot = rows[0].shape[0]
+    others = [k for k in range(chips) if k != 1]
+    for at, k in enumerate(others):
+        lanes = slice(k * slot, (k + 1) * slot)
+        prob, weight = all_ref[:, lanes], weight_ref[:, lanes]
+        slot_grad(scale, prob, weight, neg_ref, rows[at], parts[2 * at], parts[2 * at + 1])
+
+
+def item_kernel(scale, k, each, own_in, prob_own, weight_own, z_own, other_in, prob_other, z_other, *outs):
     own_rows = sum(o.shape[0] for o in outs)
     width = outs[0].shape[1]
     first = first_of(k, 0, own_rows)
     owner = slice(k * each, (k + 1) * each)
-    neg = sides[0][0][1:2, owner] - first
+    neg = own_in[1:2, owner] - first
     pick = lax.broadcasted_iota(jnp.int32, (own_rows, each), 0) == neg
     pick = pick.astype(F32).astype(BF16)
+    mine = prob_own.shape[0]
     weights = []
-    for ids_ref, prob_ref, weight_ref, _ in sides:
+    for ids_ref, prob_ref, weight in (
+        (own_in, prob_own, weight_own[...]),
+        (other_in, prob_other, prob_other[mine : mine + 1].astype(F32)),
+    ):
         ids = ids_ref[0:1] - first
         row = lax.broadcasted_iota(jnp.int32, (own_rows, ids.shape[1]), 0)
-        w = dot(pick, prob_ref[owner]) + jnp.where(row == ids, weight_ref[...], 0.0)
+        w = dot(pick, prob_ref[owner]) + jnp.where(row == ids, weight, 0.0)
         weights.append(w.astype(BF16))
     step = chunk_of(width)
     for c in range(0, width, step):
         cols = slice(c, c + step)
-        grad = scale * sum(dot(w, side[3][:, cols]) for w, side in zip(weights, sides))
+        grad = scale * sum(dot(w, z[:, cols]) for w, z in zip(weights, (z_own, z_other)))
         at = 0
         for o in outs:
             o[:, cols] = grad[at : at + o.shape[0]].astype(o.dtype)
@@ -311,7 +332,13 @@
     step = chunk_of(w_ref.shape[0])
     for c in range(0, w_ref.shape[0], step):
         cols = slice(c, c + step)
-        out_ref[:, cols] = dot(grad, w_ref[cols], 1, 1).astype(BF16)
+        out_ref[:, cols] = dot(grad, w_ref[:, cols]).astype(BF16)
+
+
+def flip_kernel(w_ref, out_ref):
+    step = chunk_of(w_ref.shape[0])
+    for r in range(0, w_ref.shape[0], step):
+        out_ref[:, r : r + step] = jnp.transpose(w_ref[r : r + step])
 
 
 def ring_shift(x, step, chips):
@@ -392,36 +419,51 @@
                     rows.append(core_swap(piece, members) if side else piece)
         return tuple(plan), rows
 
-    order = []
     slots = chips - 1
-    base, early = [], []
-    for ks in ([0], single):
-        plan, rows = stage(ks)
-        order += [(side, k) for side, k, _ in plan]
-        pos_base, got_rows = call(
-            functools.partial(pick_kernel, plan, own_rows, neg_rows),
-            [((users, width), BF16), ((len(plan) * neg_rows, width), BF16)],
+    lanes = slots * rows_here
+    negs = 2 * groups * neg_rows
+
+    def pick(plan, rows, extra, slots, more):
+        return call(
+            functools.partial(pick_kernel, plan, own_rows, neg_rows, slots, scale),
+            [((users, width), BF16)] + more,
             0,
-            [own, other] + rows + base,
+            [own, other] + rows + extra,
             2 * users * width * own_rows * len(rows),
         )
-        base = [pos_base]
-        early.append(got_rows)
+
+    plan, rows = stage([0])
+    order = [(side, k) for side, k, _ in plan]
+    base, neg_first = pick(plan, rows, [], None, [((len(order) * neg_rows, width), BF16)])
+    plan, rows = stage(single)
+    order += [(side, k) for side, k, _ in plan]
+    early = len(order) * neg_rows
+    base, neg_early, logits_early = pick(
+        plan,
+        rows,
+        [base, neg_first] + z_slots[:slots],
+        slots,
+        [((early, width), BF16), ((early, lanes), F32)],
+    )
     plan, rows = stage(double)
-    order += list(dict.fromkeys((side, k) for side, k, _ in plan))
-    negs = 2 * groups * neg_rows
+    cut = len(plan) // 2
+    late = list(dict.fromkeys((side, k) for side, k, _ in plan))
+    order += late
+    base, neg_late = pick(
+        plan[:cut], rows[:cut], [base], 0, [((len(late) // 2 * neg_rows, width), BF16)]
+    )
     out = call(
-        functools.partial(main_kernel, plan, own_rows, neg_rows, slots, scale),
+        functools.partial(main_kernel, plan[cut:], own_rows, neg_rows, slots, scale),
         [((rows_here, width), BF16)] * chips
         + [
             ((negs, width), BF16),
-            ((negs, slots * rows_here), F32),
-            ((1, slots * rows_here), F32),
-            ((2, slots * rows_here), F32),
+            ((negs, lanes), F32),
+            ((1, lanes), F32),
+            ((2, lanes), F32),
         ],
         0,
-        [own, other] + base + early + rows + z_slots[:slots],
-        2 * users * width * mid * len(rows) + 2 * users * negs * width,
+        [own, other, base, neg_early, neg_late, logits_early] + rows[cut:] + z_slots[:slots],
+        2 * users * width * mid * cut + 2 * users * negs * width,
     )
     pos_rows, (neg_all, logits, pos, stat) = out[:chips], out[chips:]
     logits_t, pos_t, stat = call(
@@ -436,34 +478,39 @@
     z_other = core_swap(z_all, members)
     mine = groups * neg_rows
     part = [None] * chips
-    part[1] = call(
-        functools.partial(lead_kernel, chips, own_rows, scale),
-        [((half, width), BF16)] * 2,
+    out = call(
+        functools.partial(lead_kernel, chips, own_rows, scale, tuple(order), neg_rows),
+        [((half, width), BF16)] * 2
+        + [
+            ((mine, users), BF16),
+            ((mine + 16, users), BF16),
+            ((1, users), F32),
+            ((negs, users), BF16),
+        ],
         0,
-        [own, logits, pos, neg_all, pos_rows[1]] + stats,
+        [own, logits, pos, logits_t, pos_t, neg_all, pos_rows[1]] + stats,
         2 * rows_here * negs * width,
     )
+    part[1] = out[:2]
+    prob, prob_out, weight, prob_all = out[2:]
+    prob_in = core_swap(prob_out, members)
     others = [k for k in range(chips) if k != 1]
     out = call(
-        functools.partial(rest_kernel, chips, own_rows, scale, tuple(order), neg_rows),
-        [((mine, users), BF16), ((mine, users), BF16), ((1, users), F32)]
-        + [((half, width), BF16 if k else F32) for k in others for _ in range(2)],
+        functools.partial(rest_kernel, chips, scale),
+        [((half, width), BF16 if k else F32) for k in others for _ in range(2)],
         0,
-        [own, logits, pos, logits_t, pos_t, neg_all] + [pos_rows[k] for k in others] + stats,
+        [prob_all, weight, neg_all] + [pos_rows[k] for k in others],
         2 * users * negs * width,
     )
-    prob, prob_out, weight = out[:3]
     for n, k in enumerate(others):
-        part[k] = out[3 + 2 * n : 5 + 2 * n]
-    prob_in = core_swap(prob_out, members)
-    weight_in = core_swap(weight, members)
+        part[k] = out[2 * n : 2 * n + 2]
 
     def item_part(k, kinds):
         return call(
             functools.partial(item_kernel, scale, k, neg_rows),
             [((n, width), t) for n, t in kinds],
             0,
-            [own, prob, weight, z_all, other, prob_in, weight_in, z_other],
+            [own, prob, weight, z_all, other, prob_in, z_other],
             4 * own_rows * users * width,
         )
 
@@ -492,11 +539,12 @@
     for k in single:
         got[k] = [group_swap(piece, k, groups) for piece in sums[k]]
     item_grad = total + sum(jnp.concatenate(got[k]).astype(F32) for k in single)
+    (flipped,) = call(flip_kernel, [((width, width), BF16)], 0, [projection], width)
     (user_grad,) = call(
         finish_kernel,
         [((rows_here, width), BF16)],
         0,
-        [part[0][0], up_in, part[0][1], down_in, hidden, projection],
+        [part[0][0], up_in, part[0][1], down_in, hidden, flipped],
         2 * rows_here * width * width,
     )
     return (user_grad, item_grad)

time: 167 us -> 169 us (1.012)
  local copies, waits for them, and re-layouts: 7.95 us -> 5.87 us
  Pallas kernels: 26.4 us -> 28.1 us
    ppermute x13, waiting for transfers between devices: 31.2 us -> 38.4 us  [group_swap(): return lax.ppermute(x, 'grp', [(g, g ^ bits) for g in range(groups)])]
    ppermute x18, waiting for transfers between devices: 52.6 us -> 46.4 us  [ring_shift(): return lax.ppermute(x, 'mem', perm)]
    ppermute x18, starting transfers between devices: 30.2 us -> 32.9 us  [ring_shift(): return lax.ppermute(x, 'mem', perm)]
    unnamed x10, local copies, waits for them, and re-layouts: 6.8 us -> 4.73 us
    pallas_call x17 -> x19, Pallas kernels: 26.4 us -> 28.1 us  [call(): pl.pallas_call(kernel, out_shape=[jax.ShapeDtypeStruct(s, t) for s, t in...]
  transfers between devices with their start and end apart: 40 -> 39, of which waited for: 20 -> 20; matrix products, arithmetic and copies ran while one was open for 1% -> 1% of each run, Pallas kernels for 16% -> 17%
where the time goes in v2:
time: 169 us
  waiting for transfers between devices  86 us (51%)
  starting transfers between devices  45.6 us (27%)
  Pallas kernels  28.1 us (17%)
  local copies, waits for them, and re-layouts  5.87 us (3%)
  other arithmetic  2.33 us (1%)
    ppermute x18, waiting for transfers between devices, ring_shift(): return lax.ppermute(x, 'mem', perm)  46.4 us
    ppermute x13, waiting for transfers between devices, group_swap(): return lax.ppermute(x, 'grp', [(g, g ^ bits) for g in range(groups)])  38.4 us
    ppermute x18, starting transfers between devices, ring_shift(): return lax.ppermute(x, 'mem', perm)  32.9 us
    pallas_call x19, Pallas kernels, call(): pl.pallas_call(kernel, out_shape=[jax.ShapeDtypeStruct(s, t) for s, t in...  28.1 us
    ppermute x13, starting transfers between devices, group_swap(): return lax.ppermute(x, 'grp', [(g, g ^ bits) for g in range(groups)])  11.4 us
    unnamed x10, local copies, waits for them, and re-layouts  4.73 us
  transfers between devices with their start and end apart: 39, of which 20 were waited for; matrix products, arithmetic and copies ran while one was open for 1% of the time, Pallas kernels for 17%

profile of v2, /device:TPU:0, one launch (start us, length us, event | category | flops | bytes accessed | tf_op | source)
XLA Modules:
  0.0 168.8 jit_solution(7981926821356395290)
XLA Ops:
  0.6 3.0 %collective-permute-start.9 = (bf16[256,2048]{1,0:T(8,128)(2,1)}, bf16[256,2048]{1,0:T(8,128)(2,1)S(1)}, u32[]{:S(2)}, u32[]{:S(2)}) collective-permute-start(bf16[256,2048]{1,0:T(8,128)(2,1)} %refs_0_.1), channel_id=1, source_target_pairs={{0,8},{8,0},{16,24},{24,16},{1,9},{9,1},{17,25},{25,17},{2,10},{10... | collective-permute-start | bytes 3145736 | tf_op jit(solution)/shard_map/ppermute | solution.py:358
  3.7 1.5 collective-permute-start.7
  6.3 1.6 collective-permute-start.14
  7.9 2.2 %collective-permute-start.15 = (bf16[64,2048]{1,0:T(8,128)(2,1)S(1)}, bf16[64,2048]{1,0:T(8,128)(2,1)S(1)}, u32[]{:S(2)}, u32[]{:S(2)}) collective-permute-start(bf16[64,2048]{1,0:T(8,128)(2,1)S(1)} %get-tuple-element.78.x_down), channel_id=1, source_target_pairs={{0,6},{1,7},{2,0},{3,1},{4,2},{5,3},{6,4},{7,5},{8,14},{9,15},{10,... | collective-permute-start | bytes 786440 | tf_op jit(solution)/shard_map/ppermute | solution.py:350
  10.1 11.2 %collective-permute-done.refs_1_ = s32[1,128]{1,0:T(1,128)S(1)} collective-permute-done((s32[1,128]{1,0:T(1,128)}, s32[1,128]{1,0:T(1,128)S(1)}, u32[]{:S(2)}, u32[]{:S(2)}) %collective-permute-start) | collective-permute-done | bytes 544 | tf_op jit(solution)/shard_map/ppermute | solution.py:350
  22.1 3.8 %collective-permute-done.1.refs_2_ = s32[1,128]{1,0:T(1,128)S(1)} collective-permute-done((s32[1,128]{1,0:T(1,128)}, s32[1,128]{1,0:T(1,128)S(1)}, u32[]{:S(2)}, u32[]{:S(2)}) %collective-permute-start.1) | collective-permute-done | bytes 544 | tf_op jit(solution)/shard_map/ppermute | solution.py:350
  25.9 1.8 %collective-permute-start.2 = (s32[1,128]{1,0:T(1,128)}, s32[1,128]{1,0:T(1,128)S(1)}, u32[]{:S(2)}, u32[]{:S(2)}) collective-permute-start(s32[1,128]{1,0:T(1,128)} %bitcast.3), channel_id=1, source_target_pairs={{0,6},{1,7},{2,0},{3,1},{4,2},{5,3},{6,4},{7,5},{8,14},{9,15},{10,... | collective-permute-start | bytes 1544 | tf_op jit(solution)/shard_map/ppermute | solution.py:350
  27.7 1.9 %collective-permute-done.2.refs_3_ = s32[1,128]{1,0:T(1,128)S(1)} collective-permute-done((s32[1,128]{1,0:T(1,128)}, s32[1,128]{1,0:T(1,128)S(1)}, u32[]{:S(2)}, u32[]{:S(2)}) %collective-permute-start.2) | collective-permute-done | bytes 544 | tf_op jit(solution)/shard_map/ppermute | solution.py:350
  30.2 3.3 %collective-permute-done.3.refs_5_ = s32[4,32]{1,0:T(4,128)S(1)} collective-permute-done((s32[4,32]{1,0:T(4,128)}, s32[4,32]{1,0:T(4,128)S(1)}, u32[]{:S(2)}, u32[]{:S(2)}) %collective-permute-start.3) | collective-permute-done | bytes 544 | tf_op jit(solution)/shard_map/ppermute | solution.py:358
  33.9 3.3 %collective-permute-done.4.refs_6_ = s32[4,32]{1,0:T(4,128)S(1)} collective-permute-done((s32[4,32]{1,0:T(4,128)}, s32[4,32]{1,0:T(4,128)S(1)}, u32[]{:S(2)}, u32[]{:S(2)}) %collective-permute-start.4) | collective-permute-done | bytes 544 | tf_op jit(solution)/shard_map/ppermute | solution.py:358
  37.7 4.2 %collective-permute-done.5.refs_7_ = s32[4,32]{1,0:T(4,128)S(1)} collective-permute-done((s32[4,32]{1,0:T(4,128)}, s32[4,32]{1,0:T(4,128)S(1)}, u32[]{:S(2)}, u32[]{:S(2)}) %collective-permute-start.5) | collective-permute-done | bytes 544 | tf_op jit(solution)/shard_map/ppermute | solution.py:358
  43.4 1.2 collective-permute-done.6.other_ref.other_in
  44.7 3.8 %collective-permute-start.17 = (bf16[64,2048]{1,0:T(8,128)(2,1)S(1)}, bf16[64,2048]{1,0:T(8,128)(2,1)S(1)}, u32[]{:S(2)}, u32[]{:S(2)}) collective-permute-start(bf16[64,2048]{1,0:T(8,128)(2,1)S(1)} %collective-permute-done.15.x_down), channel_id=1, source_target_pairs={{0,6},{1,7},{2,0},{3,1},{4,2},{5,3},{6,4},{7,5},{8,14},{9,15},{10,... | collective-permute-start | bytes 786440 | tf_op jit(solution)/shard_map/ppermute | solution.py:350
  49.0 6.7 %collective-permute-done.16.x_up = bf16[64,2048]{1,0:T(8,128)(2,1)S(1)} collective-permute-done((bf16[64,2048]{1,0:T(8,128)(2,1)S(1)}, bf16[64,2048]{1,0:T(8,128)(2,1)S(1)}, u32[]{:S(2)}, u32[]{:S(2)}) %collective-permute-start.16) | collective-permute-done | bytes 262176 | tf_op jit(solution)/shard_map/ppermute | solution.py:350
  55.7 3.2 %collective-permute-done.17.x_down = bf16[64,2048]{1,0:T(8,128)(2,1)S(1)} collective-permute-done((bf16[64,2048]{1,0:T(8,128)(2,1)S(1)}, bf16[64,2048]{1,0:T(8,128)(2,1)S(1)}, u32[]{:S(2)}, u32[]{:S(2)}) %collective-permute-start.17) | collective-permute-done | bytes 262176 | tf_op jit(solution)/shard_map/ppermute | solution.py:350
  58.9 3.5 %collective-permute-start.21 = (bf16[64,2048]{1,0:T(8,128)(2,1)S(1)}, bf16[64,2048]{1,0:T(8,128)(2,1)S(1)}, u32[]{:S(2)}, u32[]{:S(2)}) collective-permute-start(bf16[64,2048]{1,0:T(8,128)(2,1)S(1)} %collective-permute-done.17.x_down), channel_id=1, source_target_pairs={{0,6},{1,7},{2,0},{3,1},{4,2},{5,3},{6,4},{7,5},{8,14},{9,15},{10,... | collective-permute-start | bytes 786440 | tf_op jit(solution)/shard_map/ppermute | solution.py:350
  62.4 3.4 %copy-done = bf16[2048,2048]{1,0:T(8,128)(2,1)S(1)} copy-done((bf16[2048,2048]{1,0:T(8,128)(2,1)S(1)}, bf16[2048,2048]{1,0:T(8,128)(2,1)}, u32[]{:S(2)}) %copy-start) | copy-done | bytes 8388632
  65.8 1.3 shard_map.70
  67.2 2.4 %collective-permute-done.20.x_up = bf16[64,2048]{1,0:T(8,128)(2,1)S(1)} collective-permute-done((bf16[64,2048]{1,0:T(8,128)(2,1)S(1)}, bf16[64,2048]{1,0:T(8,128)(2,1)S(1)}, u32[]{:S(2)}, u32[]{:S(2)}) %collective-permute-start.20) | collective-permute-done | bytes 262176 | tf_op jit(solution)/shard_map/ppermute | solution.py:350
  70.1 3.3 %collective-permute-done.21.x_down = bf16[64,2048]{1,0:T(8,128)(2,1)S(1)} collective-permute-done((bf16[64,2048]{1,0:T(8,128)(2,1)S(1)}, bf16[64,2048]{1,0:T(8,128)(2,1)S(1)}, u32[]{:S(2)}, u32[]{:S(2)}) %collective-permute-start.21) | collective-permute-done | bytes 262176 | tf_op jit(solution)/shard_map/ppermute | solution.py:350
  73.9 1.3 shard_map.71.refs_7_.refs_6_.refs_1_
  75.3 1.3 shard_map.72.refs_8_.refs_7_.refs_2_
  76.6 1.3 shard_map.76.z_ref.refs_3_
  78.1 8.6 %collective-permute-done.8.refs_0_ = bf16[128,2048]{1,0:T(8,128)(2,1)S(1)} collective-permute-done((bf16[128,2048]{1,0:T(8,128)(2,1)S(1)}, bf16[128,2048]{1,0:T(8,128)(2,1)S(1)}, u32[]{:S(2)}, u32[]{:S(2)}) %collective-permute-start.8) | collective-permute-done | bytes 524320 | tf_op jit(solution)/shard_map/ppermute | solution.py:358
  87.2 2.0 %shard_map.69 = (bf16[512,2048]{1,0:T(8,128)(2,1)S(1)}, bf16[64,2048]{1,0:T(8,128)(2,1)S(1)}) custom-call(s32[2,512]{1,0:T(2,128)S(1)} %shard_map.68.own_ref.own_in, s32[2,512]{1,0:T(2,128)S(1)} %collective-permute-done.6.other_ref.other_in, bf16[256,2048]{1,0:T(8,128)(2,1)S(1)} %copy-done.4, bf16[256,2048]{1,0:T(8,128)(2,1)S(1)} %collective-permute-done.13.refs_1_), custom_call_target="tpu_custom_call" | custom-call | flops 1073741824 | bytes 4464640 | tf_op jit(solution)/shard_map/pallas_call | solution.py:39
  89.2 3.7 %shard_map.73 = (bf16[512,2048]{1,0:T(8,128)(2,1)S(1)}, bf16[192,2048]{1,0:T(8,128)(2,1)S(1)}, f32[192,384]{1,0:T(8,128)S(1)}) custom-call(s32[2,512]{1,0:T(2,128)S(1)} %shard_map.68.own_ref.own_in, s32[2,512]{1,0:T(2,128)S(1)} %collective-permute-done.6.other_ref.other_in, bf16[256,2048]{1,0:T(8,128)(2,1)S(1)} %collective-permute-done.9.refs_0_, ...), custom_call_target="tpu_custom_call" | custom-call | flops 2147483648 | bytes 11313152 | tf_op jit(solution)/shard_map/pallas_call | solution.py:39
  92.9 1.8 %shard_map.74 = (bf16[512,2048]{1,0:T(8,128)(2,1)S(1)}, bf16[32,2048]{1,0:T(8,128)(2,1)S(1)}) custom-call(s32[2,512]{1,0:T(2,128)S(1)} %shard_map.68.own_ref.own_in, s32[2,512]{1,0:T(2,128)S(1)} %collective-permute-done.6.other_ref.other_in, bf16[128,2048]{1,0:T(8,128)(2,1)S(1)} %collective-permute-done.8.refs_0_, ...), custom_call_target="tpu_custom_call" | custom-call | flops 1073741824 | bytes 5382144 | tf_op jit(solution)/shard_map/pallas_call | solution.py:39
  94.8 2.5 %shard_map.75 = (bf16[128,2048]{1,0:T(8,128)(2,1)S(1)}, bf16[128,2048]{1,0:T(8,128)(2,1)S(1)}, bf16[128,2048]{1,0:T(8,128)(2,1)S(1)}, bf16[128,2048]{1,0:T(8,128...) custom-call(s32[2,512]{1,0:T(2,128)S(1)} %shard_map.68.own_ref.own_i, ...), custom_call_target="tpu_custom_call" | custom-call | flops 1073741824 | bytes 9482752 | tf_op jit(solution)/shard_map/pallas_call | solution.py:39
  97.8 1.8 %collective-permute-start.22 = (f32[2,512]{1,0:T(2,128)S(1)}, f32[2,512]{1,0:T(2,128)S(1)}, u32[]{:S(2)}, u32[]{:S(2)}) collective-permute-start(f32[2,512]{1,0:T(2,128)S(1)} %get-tuple-element.56.refs_4_), channel_id=1, source_target_pairs={{0,2},{1,3},{2,4},{3,5},{4,6},{5,7},{6,0},{7,1},{8,10},{9,11},{10,... | collective-permute-start | bytes 12296 | tf_op jit(solution)/shard_map/ppermute | solution.py:350
  100.2 1.9 %collective-permute-start.24 = (f32[2,512]{1,0:T(2,128)S(1)}, f32[2,512]{1,0:T(2,128)S(1)}, u32[]{:S(2)}, u32[]{:S(2)}) collective-permute-start(f32[2,512]{1,0:T(2,128)S(1)} %get-tuple-element.56.refs_4_), channel_id=1, source_target_pairs={{0,6},{1,7},{2,0},{3,1},{4,2},{5,3},{6,4},{7,5},{8,14},{9,15},{10,... | collective-permute-start | bytes 12296 | tf_op jit(solution)/shard_map/ppermute | solution.py:350
  102.0 1.3 collective-permute-done.22.refs_5_
  104.5 3.4 %collective-permute-start.28 = (bf16[64,2048]{1,0:T(8,128)(2,1)S(1)}, bf16[64,2048]{1,0:T(8,128)(2,1)S(1)}, u32[]{:S(2)}, u32[]{:S(2)}) collective-permute-start(bf16[64,2048]{1,0:T(8,128)(2,1)S(1)} %get-tuple-element.68), channel_id=1, source_target_pairs={{0,6},{1,7},{2,0},{3,1},{4,2},{5,3},{6,4},{7,5},{8,14},{9,15},{10,... | collective-permute-start | bytes 786440 | tf_op jit(solution)/shard_map/ppermute | solution.py:350
  108.8 5.9 %collective-permute-done.28 = bf16[64,2048]{1,0:T(8,128)(2,1)S(1)} collective-permute-done((bf16[64,2048]{1,0:T(8,128)(2,1)S(1)}, bf16[64,2048]{1,0:T(8,128)(2,1)S(1)}, u32[]{:S(2)}, u32[]{:S(2)}) %collective-permute-start.28) | collective-permute-done | bytes 262176 | tf_op jit(solution)/shard_map/ppermute | solution.py:350
  114.7 4.3 %collective-permute-start.29 = (bf16[64,2048]{1,0:T(8,128)(2,1)S(1)}, bf16[64,2048]{1,0:T(8,128)(2,1)S(1)}, u32[]{:S(2)}, u32[]{:S(2)}) collective-permute-start(bf16[64,2048]{1,0:T(8,128)(2,1)S(1)} %add_convert_fusion.3), channel_id=1, source_target_pairs={{0,6},{1,7},{2,0},{3,1},{4,2},{5,3},{6,4},{7,5},{8,14},{9,15},{10,... | collective-permute-start | bytes 786440 | tf_op jit(solution)/shard_map/ppermute | solution.py:350
  119.0 1.2 collective-permute-done.25
  120.3 2.5 %collective-permute-start.26 = (bf16[64,2048]{1,0:T(8,128)(2,1)S(1)}, bf16[64,2048]{1,0:T(8,128)(2,1)S(1)}, u32[]{:S(2)}, u32[]{:S(2)}) collective-permute-start(bf16[64,2048]{1,0:T(8,128)(2,1)S(1)} %add_convert_fusion.5), channel_id=1, source_target_pairs={{0,2},{1,3},{2,4},{3,5},{4,6},{5,7},{6,0},{7,1},{8,10},{9,11},{10,... | collective-permute-start | bytes 786440 | tf_op jit(solution)/shard_map/ppermute | solution.py:350
  122.9 1.5 shard_map.85
  125.6 4.3 %collective-permute-start.30 = (bf16[64,2048]{1,0:T(8,128)(2,1)S(1)}, bf16[64,2048]{1,0:T(8,128)(2,1)S(1)}, u32[]{:S(2)}, u32[]{:S(2)}) collective-permute-start(bf16[64,2048]{1,0:T(8,128)(2,1)S(1)} %add_convert_fusion.2), channel_id=1, source_target_pairs={{0,6},{1,7},{2,0},{3,1},{4,2},{5,3},{6,4},{7,5},{8,14},{9,15},{10,... | collective-permute-start | bytes 786440 | tf_op jit(solution)/shard_map/ppermute | solution.py:350
  129.9 1.5 shard_map.86
  132.1 1.5 collective-permute-start.34
  133.6 1.5 shard_map.84
  135.1 1.4 collective-permute-done.36
  137.2 17.6 %collective-permute-done.34 = bf16[128,2048]{1,0:T(8,128)(2,1)S(1)} collective-permute-done((bf16[128,2048]{1,0:T(8,128)(2,1)S(1)}, bf16[128,2048]{1,0:T(8,128)(2,1)S(1)}, u32[]{:S(2)}, u32[]{:S(2)}) %collective-permute-start.34) | collective-permute-done | bytes 524320 | tf_op jit(solution)/shard_map/ppermute | solution.py:358
  156.5 2.4 %shard_map.80.w_ref = bf16[2048,2048]{1,0:T(8,128)(2,1)S(1)} custom-call(bf16[2048,2048]{1,0:T(8,128)(2,1)S(1)} %copy-done.1), custom_call_target="tpu_custom_call" | custom-call | flops 2048 | bytes 16777216 | tf_op jit(solution)/shard_map/pallas_call | solution.py:39
  158.9 1.5 shard_map.83
  160.4 4.2 %collective-permute-done.27.up_in_ref = bf16[64,2048]{1,0:T(8,128)(2,1)S(1)} collective-permute-done((bf16[64,2048]{1,0:T(8,128)(2,1)S(1)}, bf16[64,2048]{1,0:T(8,128)(2,1)S(1)}, u32[]{:S(2)}, u32[]{:S(2)}) %collective-permute-start.27) | collective-permute-done | bytes 262176 | tf_op jit(solution)/shard_map/ppermute | solution.py:350
  164.7 2.3 %shard_map.81 = bf16[128,2048]{1,0:T(8,128)(2,1)} custom-call(f32[64,2048]{1,0:T(8,128)S(1)} %get-tuple-element.61.up_ref, bf16[64,2048]{1,0:T(8,128)(2,1)S(1)} %collective-permute-done.27.up_in_ref, f32[64,2048]{1,0:T(8,128)S(1)} %get-tuple-element.65.down_ref, bf16[64,2048]{1,0:T(8,128)(2,1)S(1)} %collective-permute-done.30.down_in_ref, ...), custom_call_target="tpu_custom_call" | custom-call | flops 1073741824 | bytes 11534336 | tf_op jit(solution)/shard_map/pallas_call | solution.py:39
  167.0 1.8 %add_add_fusion = f32[256,2048]{1,0:T(8,128)} fusion(f32[256,2048]{1,0:T(8,128)S(1)} %shard_map.83, bf16[128,2048]{1,0:T(8,128)(2,1)S(1)} %collective-permute-done.35, bf16[128,2048]{1,0:T(8,128)(2,1)S(1)} %collective-permute-done.33, bf16[128,2048]{1,0:T(8,128)(2,1)S(1)} %collective-permute-done.38, bf16[128,2048]{1,0:T(8,128)(2,1)S(1)} %collective-permute-done.37), kind=kLoop, calls=%fused_computation | loop fusion | flops 5242880 | bytes 6291456 | tf_op jit(solution)/shard_map/add | solution.py:541
  (69 shorter events, 14.7 us)
Async XLA Ops:
  0.6 47.9 %collective-permute-start.9 = (bf16[256,2048]{1,0:T(8,128)(2,1)}, bf16[256,2048]{1,0:T(8,128)(2,1)S(1)}, u32[]{:S(2)}, u32[]{:S(2)}) collective-permute-start(bf16[256,2048]{1,0:T(8,128)(2,1)} %refs_0_.1), channel_id=1, source_target_pairs={{0,8},{8,0},{16,24},{24,16},{1,9},{9,1},{17,25},{25,17},{2,10},{10... | collective-permute-start | bytes 3145736 | tf_op jit(solution)/shard_map/ppermute | solution.py:358
  3.7 44.9 %collective-permute-start.7 = (bf16[256,2048]{1,0:T(8,128)(2,1)}, bf16[256,2048]{1,0:T(8,128)(2,1)S(1)}, u32[]{:S(2)}, u32[]{:S(2)}) collective-permute-start(bf16[256,2048]{1,0:T(8,128)(2,1)} %refs_0_.1), channel_id=1, source_target_pairs={{0,16},{8,24},{16,0},{24,8},{1,17},{9,25},{17,1},{25,9},{2,18},{10... | collective-permute-start | bytes 3145736 | tf_op jit(solution)/shard_map/ppermute | solution.py:358
  6.3 38.4 %collective-permute-start.14 = (bf16[64,2048]{1,0:T(8,128)(2,1)S(1)}, bf16[64,2048]{1,0:T(8,128)(2,1)S(1)}, u32[]{:S(2)}, u32[]{:S(2)}) collective-permute-start(bf16[64,2048]{1,0:T(8,128)(2,1)S(1)} %get-tuple-element.79.x_up), channel_id=1, source_target_pairs={{0,2},{1,3},{2,4},{3,5},{4,6},{5,7},{6,0},{7,1},{8,10},{9,11},{10,... | collective-permute-start | bytes 786440 | tf_op jit(solution)/shard_map/ppermute | solution.py:350
  7.9 36.8 %collective-permute-start.15 = (bf16[64,2048]{1,0:T(8,128)(2,1)S(1)}, bf16[64,2048]{1,0:T(8,128)(2,1)S(1)}, u32[]{:S(2)}, u32[]{:S(2)}) collective-permute-start(bf16[64,2048]{1,0:T(8,128)(2,1)S(1)} %get-tuple-element.78.x_down), channel_id=1, source_target_pairs={{0,6},{1,7},{2,0},{3,1},{4,2},{5,3},{6,4},{7,5},{8,14},{9,15},{10,... | collective-permute-start | bytes 786440 | tf_op jit(solution)/shard_map/ppermute | solution.py:350
  10.1 11.2 %collective-permute-start = (s32[1,128]{1,0:T(1,128)}, s32[1,128]{1,0:T(1,128)S(1)}, u32[]{:S(2)}, u32[]{:S(2)}) collective-permute-start(s32[1,128]{1,0:T(1,128)} %bitcast.1), channel_id=1, source_target_pairs={{0,2},{1,3},{2,4},{3,5},{4,6},{5,7},{6,0},{7,1},{8,10},{9,11},{10,... | collective-permute-start | bytes 1544 | tf_op jit(solution)/shard_map/ppermute | solution.py:350
  21.3 4.6 %collective-permute-start.1 = (s32[1,128]{1,0:T(1,128)}, s32[1,128]{1,0:T(1,128)S(1)}, u32[]{:S(2)}, u32[]{:S(2)}) collective-permute-start(s32[1,128]{1,0:T(1,128)} %bitcast.2), channel_id=1, source_target_pairs={{0,4},{1,5},{2,6},{3,7},{4,0},{5,1},{6,2},{7,3},{8,12},{9,13},{10,... | collective-permute-start | bytes 1544 | tf_op jit(solution)/shard_map/ppermute | solution.py:350
  25.9 3.7 %collective-permute-start.2 = (s32[1,128]{1,0:T(1,128)}, s32[1,128]{1,0:T(1,128)S(1)}, u32[]{:S(2)}, u32[]{:S(2)}) collective-permute-start(s32[1,128]{1,0:T(1,128)} %bitcast.3), channel_id=1, source_target_pairs={{0,6},{1,7},{2,0},{3,1},{4,2},{5,3},{6,4},{7,5},{8,14},{9,15},{10,... | collective-permute-start | bytes 1544 | tf_op jit(solution)/shard_map/ppermute | solution.py:350
  29.6 3.8 %collective-permute-start.3 = (s32[4,32]{1,0:T(4,128)}, s32[4,32]{1,0:T(4,128)S(1)}, u32[]{:S(2)}, u32[]{:S(2)}) collective-permute-start(s32[4,32]{1,0:T(4,128)} %refs_4_.1), channel_id=1, source_target_pairs={{0,8},{8,0},{16,24},{24,16},{1,9},{9,1},{17,25},{25,17},{2,10},{10... | collective-permute-start | bytes 1544 | tf_op jit(solution)/shard_map/ppermute | solution.py:358
  33.4 3.8 %collective-permute-start.4 = (s32[4,32]{1,0:T(4,128)}, s32[4,32]{1,0:T(4,128)S(1)}, u32[]{:S(2)}, u32[]{:S(2)}) collective-permute-start(s32[4,32]{1,0:T(4,128)} %refs_4_.1), channel_id=1, source_target_pairs={{0,16},{8,24},{16,0},{24,8},{1,17},{9,25},{17,1},{25,9},{2,18},{10... | collective-permute-start | bytes 1544 | tf_op jit(solution)/shard_map/ppermute | solution.py:358
  37.2 4.7 %collective-permute-start.5 = (s32[4,32]{1,0:T(4,128)}, s32[4,32]{1,0:T(4,128)S(1)}, u32[]{:S(2)}, u32[]{:S(2)}) collective-permute-start(s32[4,32]{1,0:T(4,128)} %refs_4_.1), channel_id=1, source_target_pairs={{0,24},{8,16},{16,8},{24,0},{1,25},{9,17},{17,9},{25,1},{2,26},{10... | collective-permute-start | bytes 1544 | tf_op jit(solution)/shard_map/ppermute | solution.py:358
  41.9 0.7 copy-start.2
  42.6 0.7 copy-start.3
  43.3 1.2 collective-permute-start.6
  44.5 33.5 %collective-permute-start.13 = (bf16[256,2048]{1,0:T(8,128)(2,1)}, bf16[256,2048]{1,0:T(8,128)(2,1)S(1)}, u32[]{:S(2)}, u32[]{:S(2)}) collective-permute-start(bf16[256,2048]{1,0:T(8,128)(2,1)} %refs_0_.1), channel_id=1, source_target_pairs={{0,1},{1,0},{2,3},{3,2},{4,5},{5,4},{6,7},{7,6},{8,9},{9,8},{10,11... | collective-permute-start | bytes 3145736 | tf_op jit(solution)/shard_map/ppermute | solution.py:354
  44.7 11.0 %collective-permute-start.16 = (bf16[64,2048]{1,0:T(8,128)(2,1)S(1)}, bf16[64,2048]{1,0:T(8,128)(2,1)S(1)}, u32[]{:S(2)}, u32[]{:S(2)}) collective-permute-start(bf16[64,2048]{1,0:T(8,128)(2,1)S(1)} %collective-permute-done.14.x_up), channel_id=1, source_target_pairs={{0,2},{1,3},{2,4},{3,5},{4,6},{5,7},{6,0},{7,1},{8,10},{9,11},{10,... | collective-permute-start | bytes 786440 | tf_op jit(solution)/shard_map/ppermute | solution.py:350
  44.7 14.2 %collective-permute-start.17 = (bf16[64,2048]{1,0:T(8,128)(2,1)S(1)}, bf16[64,2048]{1,0:T(8,128)(2,1)S(1)}, u32[]{:S(2)}, u32[]{:S(2)}) collective-permute-start(bf16[64,2048]{1,0:T(8,128)(2,1)S(1)} %collective-permute-done.15.x_down), channel_id=1, source_target_pairs={{0,6},{1,7},{2,0},{3,1},{4,2},{5,3},{6,4},{7,5},{8,14},{9,15},{10,... | collective-permute-start | bytes 786440 | tf_op jit(solution)/shard_map/ppermute | solution.py:350
  48.5 40.7 %collective-permute-start.11 = (bf16[256,2048]{1,0:T(8,128)(2,1)S(1)}, bf16[256,2048]{1,0:T(8,128)(2,1)S(1)}, u32[]{:S(2)}, u32[]{:S(2)}) collective-permute-start(bf16[256,2048]{1,0:T(8,128)(2,1)S(1)} %collective-permute-done.9.refs_0_), channel_id=1, source_target_pairs={{0,1},{1,0},{2,3},{3,2},{4,5},{5,4},{6,7},{7,6},{8,9},{9,8},{10,11... | collective-permute-start | bytes 3145736 | tf_op jit(solution)/shard_map/ppermute | solution.py:354
  48.5 40.7 %collective-permute-start.12 = (bf16[256,2048]{1,0:T(8,128)(2,1)S(1)}, bf16[256,2048]{1,0:T(8,128)(2,1)S(1)}, u32[]{:S(2)}, u32[]{:S(2)}) collective-permute-start(bf16[256,2048]{1,0:T(8,128)(2,1)S(1)} %collective-permute-done.7.refs_1_), channel_id=1, source_target_pairs={{0,1},{1,0},{2,3},{3,2},{4,5},{5,4},{6,7},{7,6},{8,9},{9,8},{10,11... | collective-permute-start | bytes 3145736 | tf_op jit(solution)/shard_map/ppermute | solution.py:354
  55.7 13.9 %collective-permute-start.20 = (bf16[64,2048]{1,0:T(8,128)(2,1)S(1)}, bf16[64,2048]{1,0:T(8,128)(2,1)S(1)}, u32[]{:S(2)}, u32[]{:S(2)}) collective-permute-start(bf16[64,2048]{1,0:T(8,128)(2,1)S(1)} %collective-permute-done.16.x_up), channel_id=1, source_target_pairs={{0,2},{1,3},{2,4},{3,5},{4,6},{5,7},{6,0},{7,1},{8,10},{9,11},{10,... | collective-permute-start | bytes 786440 | tf_op jit(solution)/shard_map/ppermute | solution.py:350
  58.9 14.5 %collective-permute-start.21 = (bf16[64,2048]{1,0:T(8,128)(2,1)S(1)}, bf16[64,2048]{1,0:T(8,128)(2,1)S(1)}, u32[]{:S(2)}, u32[]{:S(2)}) collective-permute-start(bf16[64,2048]{1,0:T(8,128)(2,1)S(1)} %collective-permute-done.17.x_down), channel_id=1, source_target_pairs={{0,6},{1,7},{2,0},{3,1},{4,2},{5,3},{6,4},{7,5},{8,14},{9,15},{10,... | collective-permute-start | bytes 786440 | tf_op jit(solution)/shard_map/ppermute | solution.py:350
  62.4 3.4 %copy-start = (bf16[2048,2048]{1,0:T(8,128)(2,1)S(1)}, bf16[2048,2048]{1,0:T(8,128)(2,1)}, u32[]{:S(2)}) copy-start(bf16[2048,2048]{1,0:T(8,128)(2,1)} %w_ref.9) | copy-start | bytes 25165828
  65.8 8.1 %copy-start.1 = (bf16[2048,2048]{1,0:T(8,128)(2,1)S(1)}, bf16[2048,2048]{1,0:T(8,128)(2,1)}, u32[]{:S(2)}) copy-start(bf16[2048,2048]{1,0:T(8,128)(2,1)} %w_ref.9) | copy-start | bytes 25165828
  69.6 17.1 %collective-permute-start.10 = (bf16[128,2048]{1,0:T(8,128)(2,1)S(1)}, bf16[128,2048]{1,0:T(8,128)(2,1)S(1)}, u32[]{:S(2)}, u32[]{:S(2)}) collective-permute-start(bf16[128,2048]{1,0:T(8,128)(2,1)S(1)} %slice.17), channel_id=1, source_target_pairs={{0,16},{8,24},{16,0},{24,8},{1,17},{9,25},{17,1},{25,9},{2,18},{10... | collective-permute-start | bytes 1572872 | tf_op jit(solution)/shard_map/ppermute | solution.py:358
  73.4 13.3 %collective-permute-start.8 = (bf16[128,2048]{1,0:T(8,128)(2,1)S(1)}, bf16[128,2048]{1,0:T(8,128)(2,1)S(1)}, u32[]{:S(2)}, u32[]{:S(2)}) collective-permute-start(bf16[128,2048]{1,0:T(8,128)(2,1)S(1)} %slice.16), channel_id=1, source_target_pairs={{0,8},{8,0},{16,24},{24,16},{1,9},{9,1},{17,25},{25,17},{2,10},{10... | collective-permute-start | bytes 1572872 | tf_op jit(solution)/shard_map/ppermute | solution.py:358
  77.9 9.3 %copy-start.4 = (bf16[256,2048]{1,0:T(8,128)(2,1)S(1)}, bf16[256,2048]{1,0:T(8,128)(2,1)}, u32[]{:S(2)}) copy-start(bf16[256,2048]{1,0:T(8,128)(2,1)} %refs_0_.1) | copy-start | bytes 3145732
  78.1 44.8 %collective-permute-start.32 = (bf16[512,2048]{1,0:T(8,128)(2,1)S(1)}, bf16[512,2048]{1,0:T(8,128)(2,1)S(1)}, u32[]{:S(2)}, u32[]{:S(2)}) collective-permute-start(bf16[512,2048]{1,0:T(8,128)(2,1)S(1)} %shard_map.82.z_own), channel_id=1, source_target_pairs={{0,1},{1,0},{2,3},{3,2},{4,5},{5,4},{6,7},{7,6},{8,9},{9,8},{10,11... | collective-permute-start | bytes 6291464 | tf_op jit(solution)/shard_map/ppermute | solution.py:354
  86.7 8.0 %collective-permute-start.18 = (bf16[128,2048]{1,0:T(8,128)(2,1)S(1)}, bf16[128,2048]{1,0:T(8,128)(2,1)S(1)}, u32[]{:S(2)}, u32[]{:S(2)}) collective-permute-start(bf16[128,2048]{1,0:T(8,128)(2,1)S(1)} %collective-permute-done.8.refs_0_), channel_id=1, source_target_pairs={{0,1},{1,0},{2,3},{3,2},{4,5},{5,4},{6,7},{7,6},{8,9},{9,8},{10,11... | collective-permute-start | bytes 1572872 | tf_op jit(solution)/shard_map/ppermute | solution.py:354
  86.7 8.0 %collective-permute-start.19 = (bf16[128,2048]{1,0:T(8,128)(2,1)S(1)}, bf16[128,2048]{1,0:T(8,128)(2,1)S(1)}, u32[]{:S(2)}, u32[]{:S(2)}) collective-permute-start(bf16[128,2048]{1,0:T(8,128)(2,1)S(1)} %collective-permute-done.10.refs_1_), channel_id=1, source_target_pairs={{0,1},{1,0},{2,3},{3,2},{4,5},{5,4},{6,7},{7,6},{8,9},{9,8},{10,11... | collective-permute-start | bytes 1572872 | tf_op jit(solution)/shard_map/ppermute | solution.py:354
  97.8 5.5 %collective-permute-start.22 = (f32[2,512]{1,0:T(2,128)S(1)}, f32[2,512]{1,0:T(2,128)S(1)}, u32[]{:S(2)}, u32[]{:S(2)}) collective-permute-start(f32[2,512]{1,0:T(2,128)S(1)} %get-tuple-element.56.refs_4_), channel_id=1, source_target_pairs={{0,2},{1,3},{2,4},{3,5},{4,6},{5,7},{6,0},{7,1},{8,10},{9,11},{10,... | collective-permute-start | bytes 12296 | tf_op jit(solution)/shard_map/ppermute | solution.py:350
  99.6 4.5 %collective-permute-start.23 = (f32[2,512]{1,0:T(2,128)S(1)}, f32[2,512]{1,0:T(2,128)S(1)}, u32[]{:S(2)}, u32[]{:S(2)}) collective-permute-start(f32[2,512]{1,0:T(2,128)S(1)} %get-tuple-element.56.refs_4_), channel_id=1, source_target_pairs={{0,4},{1,5},{2,6},{3,7},{4,0},{5,1},{6,2},{7,3},{8,12},{9,13},{10,... | collective-permute-start | bytes 12296 | tf_op jit(solution)/shard_map/ppermute | solution.py:350
  100.2 3.9 %collective-permute-start.24 = (f32[2,512]{1,0:T(2,128)S(1)}, f32[2,512]{1,0:T(2,128)S(1)}, u32[]{:S(2)}, u32[]{:S(2)}) collective-permute-start(f32[2,512]{1,0:T(2,128)S(1)} %get-tuple-element.56.refs_4_), channel_id=1, source_target_pairs={{0,6},{1,7},{2,0},{3,1},{4,2},{5,3},{6,4},{7,5},{8,14},{9,15},{10,... | collective-permute-start | bytes 12296 | tf_op jit(solution)/shard_map/ppermute | solution.py:350
  104.5 10.1 %collective-permute-start.28 = (bf16[64,2048]{1,0:T(8,128)(2,1)S(1)}, bf16[64,2048]{1,0:T(8,128)(2,1)S(1)}, u32[]{:S(2)}, u32[]{:S(2)}) collective-permute-start(bf16[64,2048]{1,0:T(8,128)(2,1)S(1)} %get-tuple-element.68), channel_id=1, source_target_pairs={{0,6},{1,7},{2,0},{3,1},{4,2},{5,3},{6,4},{7,5},{8,14},{9,15},{10,... | collective-permute-start | bytes 786440 | tf_op jit(solution)/shard_map/ppermute | solution.py:350
  107.9 15.0 %collective-permute-start.31 = (bf16[144,512]{1,0:T(8,128)(2,1)S(1)}, bf16[144,512]{1,0:T(8,128)(2,1)S(1)}, u32[]{:S(2)}, u32[]{:S(2)}) collective-permute-start(bf16[144,512]{1,0:T(8,128)(2,1)S(1)} %get-tuple-element.71), channel_id=1, source_target_pairs={{0,1},{1,0},{2,3},{3,2},{4,5},{5,4},{6,7},{7,6},{8,9},{9,8},{10,11... | collective-permute-start | bytes 442376 | tf_op jit(solution)/shard_map/ppermute | solution.py:354
  107.9 12.4 %collective-permute-start.25 = (bf16[64,2048]{1,0:T(8,128)(2,1)S(1)}, bf16[64,2048]{1,0:T(8,128)(2,1)S(1)}, u32[]{:S(2)}, u32[]{:S(2)}) collective-permute-start(bf16[64,2048]{1,0:T(8,128)(2,1)S(1)} %get-tuple-element.64), channel_id=1, source_target_pairs={{0,2},{1,3},{2,4},{3,5},{4,6},{5,7},{6,0},{7,1},{8,10},{9,11},{10,... | collective-permute-start | bytes 786440 | tf_op jit(solution)/shard_map/ppermute | solution.py:350
  114.7 10.8 %collective-permute-start.29 = (bf16[64,2048]{1,0:T(8,128)(2,1)S(1)}, bf16[64,2048]{1,0:T(8,128)(2,1)S(1)}, u32[]{:S(2)}, u32[]{:S(2)}) collective-permute-start(bf16[64,2048]{1,0:T(8,128)(2,1)S(1)} %add_convert_fusion.3), channel_id=1, source_target_pairs={{0,6},{1,7},{2,0},{3,1},{4,2},{5,3},{6,4},{7,5},{8,14},{9,15},{10,... | collective-permute-start | bytes 786440 | tf_op jit(solution)/shard_map/ppermute | solution.py:350
  120.3 35.2 %collective-permute-start.26 = (bf16[64,2048]{1,0:T(8,128)(2,1)S(1)}, bf16[64,2048]{1,0:T(8,128)(2,1)S(1)}, u32[]{:S(2)}, u32[]{:S(2)}) collective-permute-start(bf16[64,2048]{1,0:T(8,128)(2,1)S(1)} %add_convert_fusion.5), channel_id=1, source_target_pairs={{0,2},{1,3},{2,4},{3,5},{4,6},{5,7},{6,0},{7,1},{8,10},{9,11},{10,... | collective-permute-start | bytes 786440 | tf_op jit(solution)/shard_map/ppermute | solution.py:350
  124.4 12.2 %collective-permute-start.36 = (bf16[128,2048]{1,0:T(8,128)(2,1)S(1)}, bf16[128,2048]{1,0:T(8,128)(2,1)S(1)}, u32[]{:S(2)}, u32[]{:S(2)}) collective-permute-start(bf16[128,2048]{1,0:T(8,128)(2,1)S(1)} %get-tuple-element.76), channel_id=1, source_target_pairs={{0,8},{8,0},{16,24},{24,16},{1,9},{9,1},{17,25},{25,17},{2,10},{10... | collective-permute-start | bytes 1572872 | tf_op jit(solution)/shard_map/ppermute | solution.py:358
  125.6 30.6 %collective-permute-start.30 = (bf16[64,2048]{1,0:T(8,128)(2,1)S(1)}, bf16[64,2048]{1,0:T(8,128)(2,1)S(1)}, u32[]{:S(2)}, u32[]{:S(2)}) collective-permute-start(bf16[64,2048]{1,0:T(8,128)(2,1)S(1)} %add_convert_fusion.2), channel_id=1, source_target_pairs={{0,6},{1,7},{2,0},{3,1},{4,2},{5,3},{6,4},{7,5},{8,14},{9,15},{10,... | collective-permute-start | bytes 786440 | tf_op jit(solution)/shard_map/ppermute | solution.py:350
  131.5 35.5 %collective-permute-start.38 = (bf16[128,2048]{1,0:T(8,128)(2,1)S(1)}, bf16[128,2048]{1,0:T(8,128)(2,1)S(1)}, u32[]{:S(2)}, u32[]{:S(2)}) collective-permute-start(bf16[128,2048]{1,0:T(8,128)(2,1)S(1)} %get-tuple-element.77), channel_id=1, source_target_pairs={{0,16},{8,24},{16,0},{24,8},{1,17},{9,25},{17,1},{25,9},{2,18},{10... | collective-permute-start | bytes 1572872 | tf_op jit(solution)/shard_map/ppermute | solution.py:358
  132.1 22.8 %collective-permute-start.34 = (bf16[128,2048]{1,0:T(8,128)(2,1)S(1)}, bf16[128,2048]{1,0:T(8,128)(2,1)S(1)}, u32[]{:S(2)}, u32[]{:S(2)}) collective-permute-start(bf16[128,2048]{1,0:T(8,128)(2,1)S(1)} %get-tuple-element.74), channel_id=1, source_target_pairs={{0,16},{8,24},{16,0},{24,8},{1,17},{9,25},{17,1},{25,9},{2,18},{10... | collective-permute-start | bytes 1572872 | tf_op jit(solution)/shard_map/ppermute | solution.py:358
  136.6 30.4 %collective-permute-start.33 = (bf16[128,2048]{1,0:T(8,128)(2,1)S(1)}, bf16[128,2048]{1,0:T(8,128)(2,1)S(1)}, u32[]{:S(2)}, u32[]{:S(2)}) collective-permute-start(bf16[128,2048]{1,0:T(8,128)(2,1)S(1)} %get-tuple-element.72), channel_id=1, source_target_pairs={{0,8},{8,0},{16,24},{24,16},{1,9},{9,1},{17,25},{25,17},{2,10},{10... | collective-permute-start | bytes 1572872 | tf_op jit(solution)/shard_map/ppermute | solution.py:358
  154.9 12.1 %collective-permute-start.37 = (bf16[128,2048]{1,0:T(8,128)(2,1)S(1)}, bf16[128,2048]{1,0:T(8,128)(2,1)S(1)}, u32[]{:S(2)}, u32[]{:S(2)}) collective-permute-start(bf16[128,2048]{1,0:T(8,128)(2,1)S(1)} %add_convert_fusion), channel_id=1, source_target_pairs={{0,16},{8,24},{16,0},{24,8},{1,17},{9,25},{17,1},{25,9},{2,18},{10... | collective-permute-start | bytes 1572872 | tf_op jit(solution)/shard_map/ppermute | solution.py:358
  155.6 11.4 %collective-permute-start.35 = (bf16[128,2048]{1,0:T(8,128)(2,1)S(1)}, bf16[128,2048]{1,0:T(8,128)(2,1)S(1)}, u32[]{:S(2)}, u32[]{:S(2)}) collective-permute-start(bf16[128,2048]{1,0:T(8,128)(2,1)S(1)} %add_convert_fusion.1), channel_id=1, source_target_pairs={{0,8},{8,0},{16,24},{24,16},{1,9},{9,1},{17,25},{25,17},{2,10},{10... | collective-permute-start | bytes 1572872 | tf_op jit(solution)/shard_map/ppermute | solution.py:358
  156.2 8.4 %collective-permute-start.27 = (bf16[64,2048]{1,0:T(8,128)(2,1)S(1)}, bf16[64,2048]{1,0:T(8,128)(2,1)S(1)}, u32[]{:S(2)}, u32[]{:S(2)}) collective-permute-start(bf16[64,2048]{1,0:T(8,128)(2,1)S(1)} %add_convert_fusion.4), channel_id=1, source_target_pairs={{0,2},{1,3},{2,4},{3,5},{4,6},{5,7},{6,0},{7,1},{8,10},{9,11},{10,... | collective-permute-start | bytes 786440 | tf_op jit(solution)/shard_map/ppermute | solution.py:350

commit v3 on v2

--- a/solution.py
+++ b/solution.py
@@ -22,7 +22,7 @@
 
 
 def chunk_of(width):
-    return width if width < 512 else 512
+    return width if width < 256 else 256
 
 
 def cost(flops, nbytes):
@@ -295,7 +295,9 @@
         slot_grad(scale, prob, weight, neg_ref, rows[at], parts[2 * at], parts[2 * at + 1])
 
 
-def item_kernel(scale, k, each, own_in, prob_own, weight_own, z_own, other_in, prob_other, z_other, *outs):
+def item_kernel(scale, k, each, more, own_in, prob_own, weight_own, z_own, *refs):
+    other_in, prob_other, z_other = refs[:3]
+    adds, outs = refs[3 : 3 + more], refs[3 + more :]
     own_rows = sum(o.shape[0] for o in outs)
     width = outs[0].shape[1]
     first = first_of(k, 0, own_rows)
@@ -317,6 +319,8 @@
     for c in range(0, width, step):
         cols = slice(c, c + step)
         grad = scale * sum(dot(w, z[:, cols]) for w, z in zip(weights, (z_own, z_other)))
+        if more:
+            grad = grad + jnp.concatenate([a[:, cols].astype(F32) for a in adds], axis=0)
         at = 0
         for o in outs:
             o[:, cols] = grad[at : at + o.shape[0]].astype(o.dtype)
@@ -505,12 +509,12 @@
     for n, k in enumerate(others):
         part[k] = out[2 * n : 2 * n + 2]
 
-    def item_part(k, kinds):
+    def item_part(k, kinds, adds=()):
         return call(
-            functools.partial(item_kernel, scale, k, neg_rows),
+            functools.partial(item_kernel, scale, k, neg_rows, len(adds)),
             [((n, width), t) for n, t in kinds],
             0,
-            [own, prob, weight, z_all, other, prob_in, z_other],
+            [own, prob, weight, z_all, other, prob_in, z_other] + list(adds),
             4 * own_rows * users * width,
         )
 
@@ -527,7 +531,8 @@
     sums = {}
     for k in double + single:
         sums[k] = item_part(k, [(mid, BF16), (mid, BF16)])
-    (total,) = item_part(0, [(own_rows, F32)])
+    got = {(k, n): None for k in single for n in range(2)}
+    forwarded = set()
     for k in double:
         low = low_bit(k)
         rest = k ^ low
@@ -535,10 +540,13 @@
         b = group_swap(sums[k][1], rest, groups)
         sums[rest] = [(sums[rest][0].astype(F32) + a.astype(F32)).astype(BF16), sums[rest][1]]
         sums[low] = [sums[low][0], (sums[low][1].astype(F32) + b.astype(F32)).astype(BF16)]
-    got = {}
-    for k in single:
-        got[k] = [group_swap(piece, k, groups) for piece in sums[k]]
-    item_grad = total + sum(jnp.concatenate(got[k]).astype(F32) for k in single)
+        forwarded |= {(rest, 0), (low, 1)}
+    for k, n in got:
+        got[k, n] = group_swap(sums[k][n], k, groups)
+    soon = [[got[k, n] for k in single if (k, n) not in forwarded] for n in range(2)]
+    last = [[got[k, n] for k in single if (k, n) in forwarded] for n in range(2)]
+    (total,) = item_part(0, [(own_rows, F32)], [sum(s[1:], s[0]) for s in soon])
+    item_grad = total + jnp.concatenate([sum(x.astype(F32) for x in s) for s in last])
     (flipped,) = call(flip_kernel, [((width, width), BF16)], 0, [projection], width)
     (user_grad,) = call(
         finish_kernel,

time: 169 us -> 164 us (0.970)
  waiting for transfers between devices: 86 us -> 81.9 us
    ppermute x13, waiting for transfers between devices: 38.4 us -> 32.8 us  [group_swap(): return lax.ppermute(x, 'grp', [(g, g ^ bits) for g in range(groups)])]
  transfers between devices with their start and end apart: 39 -> 39, of which waited for: 20 -> 21; matrix products, arithmetic and copies ran while one was open for 1% -> 1% of each run, Pallas kernels for 17% -> 17%
where the time goes in v3:
time: 164 us
  waiting for transfers between devices  81.9 us (50%)
  starting transfers between devices  45.5 us (28%)
  Pallas kernels  27.9 us (17%)
  local copies, waits for them, and re-layouts  5.88 us (4%)
  other arithmetic  2.11 us (1%)
    ppermute x18, waiting for transfers between devices, ring_shift(): return lax.ppermute(x, 'mem', perm)  47.9 us
    ppermute x18, starting transfers between devices, ring_shift(): return lax.ppermute(x, 'mem', perm)  32.9 us
    ppermute x13, waiting for transfers between devices, group_swap(): return lax.ppermute(x, 'grp', [(g, g ^ bits) for g in range(groups)])  32.8 us
    pallas_call x19, Pallas kernels, call(): pl.pallas_call(kernel, out_shape=[jax.ShapeDtypeStruct(s, t) for s, t in...  27.9 us
    ppermute x13, starting transfers between devices, group_swap(): return lax.ppermute(x, 'grp', [(g, g ^ bits) for g in range(groups)])  11.4 us
    unnamed x10, local copies, waits for them, and re-layouts  4.73 us
  transfers between devices with their start and end apart: 39, of which 21 were waited for; matrix products, arithmetic and copies ran while one was open for 1% of the time, Pallas kernels for 17%

profile of v3, /device:TPU:0, one launch (start us, length us, event | category | flops | bytes accessed | tf_op | source)
XLA Modules:
  0.0 164.2 jit_solution(9036333864041747480)
XLA Ops:
  0.6 3.0 %collective-permute-start.9 = (bf16[256,2048]{1,0:T(8,128)(2,1)}, bf16[256,2048]{1,0:T(8,128)(2,1)S(1)}, u32[]{:S(2)}, u32[]{:S(2)}) collective-permute-start(bf16[256,2048]{1,0:T(8,128)(2,1)} %refs_0_.1), channel_id=1, source_target_pairs={{0,8},{8,0},{16,24},{24,16},{1,9},{9,1},{17,25},{25,17},{2,10},{10... | collective-permute-start | bytes 3145736 | tf_op jit(solution)/shard_map/ppermute | solution.py:362
  3.7 1.5 collective-permute-start.7
  6.3 1.6 collective-permute-start.14
  7.9 2.2 %collective-permute-start.15 = (bf16[64,2048]{1,0:T(8,128)(2,1)S(1)}, bf16[64,2048]{1,0:T(8,128)(2,1)S(1)}, u32[]{:S(2)}, u32[]{:S(2)}) collective-permute-start(bf16[64,2048]{1,0:T(8,128)(2,1)S(1)} %get-tuple-element.78.x_down), channel_id=1, source_target_pairs={{0,6},{1,7},{2,0},{3,1},{4,2},{5,3},{6,4},{7,5},{8,14},{9,15},{10,... | collective-permute-start | bytes 786440 | tf_op jit(solution)/shard_map/ppermute | solution.py:354
  10.1 11.2 %collective-permute-done.refs_1_ = s32[1,128]{1,0:T(1,128)S(1)} collective-permute-done((s32[1,128]{1,0:T(1,128)}, s32[1,128]{1,0:T(1,128)S(1)}, u32[]{:S(2)}, u32[]{:S(2)}) %collective-permute-start) | collective-permute-done | bytes 544 | tf_op jit(solution)/shard_map/ppermute | solution.py:354
  22.1 3.8 %collective-permute-done.1.refs_2_ = s32[1,128]{1,0:T(1,128)S(1)} collective-permute-done((s32[1,128]{1,0:T(1,128)}, s32[1,128]{1,0:T(1,128)S(1)}, u32[]{:S(2)}, u32[]{:S(2)}) %collective-permute-start.1) | collective-permute-done | bytes 544 | tf_op jit(solution)/shard_map/ppermute | solution.py:354
  25.9 1.8 %collective-permute-start.2 = (s32[1,128]{1,0:T(1,128)}, s32[1,128]{1,0:T(1,128)S(1)}, u32[]{:S(2)}, u32[]{:S(2)}) collective-permute-start(s32[1,128]{1,0:T(1,128)} %bitcast.3), channel_id=1, source_target_pairs={{0,6},{1,7},{2,0},{3,1},{4,2},{5,3},{6,4},{7,5},{8,14},{9,15},{10,... | collective-permute-start | bytes 1544 | tf_op jit(solution)/shard_map/ppermute | solution.py:354
  27.7 1.9 %collective-permute-done.2.refs_3_ = s32[1,128]{1,0:T(1,128)S(1)} collective-permute-done((s32[1,128]{1,0:T(1,128)}, s32[1,128]{1,0:T(1,128)S(1)}, u32[]{:S(2)}, u32[]{:S(2)}) %collective-permute-start.2) | collective-permute-done | bytes 544 | tf_op jit(solution)/shard_map/ppermute | solution.py:354
  30.2 3.3 %collective-permute-done.3.refs_5_ = s32[4,32]{1,0:T(4,128)S(1)} collective-permute-done((s32[4,32]{1,0:T(4,128)}, s32[4,32]{1,0:T(4,128)S(1)}, u32[]{:S(2)}, u32[]{:S(2)}) %collective-permute-start.3) | collective-permute-done | bytes 544 | tf_op jit(solution)/shard_map/ppermute | solution.py:362
  33.9 3.3 %collective-permute-done.4.refs_6_ = s32[4,32]{1,0:T(4,128)S(1)} collective-permute-done((s32[4,32]{1,0:T(4,128)}, s32[4,32]{1,0:T(4,128)S(1)}, u32[]{:S(2)}, u32[]{:S(2)}) %collective-permute-start.4) | collective-permute-done | bytes 544 | tf_op jit(solution)/shard_map/ppermute | solution.py:362
  37.7 4.2 %collective-permute-done.5.refs_7_ = s32[4,32]{1,0:T(4,128)S(1)} collective-permute-done((s32[4,32]{1,0:T(4,128)}, s32[4,32]{1,0:T(4,128)S(1)}, u32[]{:S(2)}, u32[]{:S(2)}) %collective-permute-start.5) | collective-permute-done | bytes 544 | tf_op jit(solution)/shard_map/ppermute | solution.py:362
  44.7 3.8 %collective-permute-start.17 = (bf16[64,2048]{1,0:T(8,128)(2,1)S(1)}, bf16[64,2048]{1,0:T(8,128)(2,1)S(1)}, u32[]{:S(2)}, u32[]{:S(2)}) collective-permute-start(bf16[64,2048]{1,0:T(8,128)(2,1)S(1)} %collective-permute-done.15.x_down), channel_id=1, source_target_pairs={{0,6},{1,7},{2,0},{3,1},{4,2},{5,3},{6,4},{7,5},{8,14},{9,15},{10,... | collective-permute-start | bytes 786440 | tf_op jit(solution)/shard_map/ppermute | solution.py:354
  49.0 6.7 %collective-permute-done.16.x_up = bf16[64,2048]{1,0:T(8,128)(2,1)S(1)} collective-permute-done((bf16[64,2048]{1,0:T(8,128)(2,1)S(1)}, bf16[64,2048]{1,0:T(8,128)(2,1)S(1)}, u32[]{:S(2)}, u32[]{:S(2)}) %collective-permute-start.16) | collective-permute-done | bytes 262176 | tf_op jit(solution)/shard_map/ppermute | solution.py:354
  55.7 3.2 %collective-permute-done.17.x_down = bf16[64,2048]{1,0:T(8,128)(2,1)S(1)} collective-permute-done((bf16[64,2048]{1,0:T(8,128)(2,1)S(1)}, bf16[64,2048]{1,0:T(8,128)(2,1)S(1)}, u32[]{:S(2)}, u32[]{:S(2)}) %collective-permute-start.17) | collective-permute-done | bytes 262176 | tf_op jit(solution)/shard_map/ppermute | solution.py:354
  58.9 3.5 %collective-permute-start.21 = (bf16[64,2048]{1,0:T(8,128)(2,1)S(1)}, bf16[64,2048]{1,0:T(8,128)(2,1)S(1)}, u32[]{:S(2)}, u32[]{:S(2)}) collective-permute-start(bf16[64,2048]{1,0:T(8,128)(2,1)S(1)} %collective-permute-done.17.x_down), channel_id=1, source_target_pairs={{0,6},{1,7},{2,0},{3,1},{4,2},{5,3},{6,4},{7,5},{8,14},{9,15},{10,... | collective-permute-start | bytes 786440 | tf_op jit(solution)/shard_map/ppermute | solution.py:354
  62.4 3.4 %copy-done = bf16[2048,2048]{1,0:T(8,128)(2,1)S(1)} copy-done((bf16[2048,2048]{1,0:T(8,128)(2,1)S(1)}, bf16[2048,2048]{1,0:T(8,128)(2,1)}, u32[]{:S(2)}) %copy-start) | copy-done | bytes 8388632
  65.8 1.3 shard_map.70
  67.2 2.4 %collective-permute-done.20.x_up = bf16[64,2048]{1,0:T(8,128)(2,1)S(1)} collective-permute-done((bf16[64,2048]{1,0:T(8,128)(2,1)S(1)}, bf16[64,2048]{1,0:T(8,128)(2,1)S(1)}, u32[]{:S(2)}, u32[]{:S(2)}) %collective-permute-start.20) | collective-permute-done | bytes 262176 | tf_op jit(solution)/shard_map/ppermute | solution.py:354
  70.1 3.3 %collective-permute-done.21.x_down = bf16[64,2048]{1,0:T(8,128)(2,1)S(1)} collective-permute-done((bf16[64,2048]{1,0:T(8,128)(2,1)S(1)}, bf16[64,2048]{1,0:T(8,128)(2,1)S(1)}, u32[]{:S(2)}, u32[]{:S(2)}) %collective-permute-start.21) | collective-permute-done | bytes 262176 | tf_op jit(solution)/shard_map/ppermute | solution.py:354
  73.9 1.3 shard_map.71.refs_7_.refs_6_.refs_1_
  75.2 1.3 shard_map.72.refs_8_.refs_7_.refs_2_
  76.5 1.3 shard_map.76.z_ref.refs_3_
  78.1 8.6 %collective-permute-done.8.refs_0_ = bf16[128,2048]{1,0:T(8,128)(2,1)S(1)} collective-permute-done((bf16[128,2048]{1,0:T(8,128)(2,1)S(1)}, bf16[128,2048]{1,0:T(8,128)(2,1)S(1)}, u32[]{:S(2)}, u32[]{:S(2)}) %collective-permute-start.8) | collective-permute-done | bytes 524320 | tf_op jit(solution)/shard_map/ppermute | solution.py:362
  87.2 1.9 %shard_map.69 = (bf16[512,2048]{1,0:T(8,128)(2,1)S(1)}, bf16[64,2048]{1,0:T(8,128)(2,1)S(1)}) custom-call(s32[2,512]{1,0:T(2,128)S(1)} %shard_map.68.own_ref.own_in, s32[2,512]{1,0:T(2,128)S(1)} %collective-permute-done.6.other_ref.refs_0_, bf16[256,2048]{1,0:T(8,128)(2,1)S(1)} %copy-done.4, bf16[256,2048]{1,0:T(8,128)(2,1)S(1)} %collective-permute-done.13.refs_1_), custom_call_target="tpu_custom_call" | custom-call | flops 1073741824 | bytes 4464640 | tf_op jit(solution)/shard_map/pallas_call | solution.py:39
  89.2 3.8 %shard_map.73 = (bf16[512,2048]{1,0:T(8,128)(2,1)S(1)}, bf16[192,2048]{1,0:T(8,128)(2,1)S(1)}, f32[192,384]{1,0:T(8,128)S(1)}) custom-call(s32[2,512]{1,0:T(2,128)S(1)} %shard_map.68.own_ref.own_in, s32[2,512]{1,0:T(2,128)S(1)} %collective-permute-done.6.other_ref.refs_0_, bf16[256,2048]{1,0:T(8,128)(2,1)S(1)} %collective-permute-done.9.refs_0_, ...), custom_call_target="tpu_custom_call" | custom-call | flops 2147483648 | bytes 11313152 | tf_op jit(solution)/shard_map/pallas_call | solution.py:39
  93.0 1.7 %shard_map.74 = (bf16[512,2048]{1,0:T(8,128)(2,1)S(1)}, bf16[32,2048]{1,0:T(8,128)(2,1)S(1)}) custom-call(s32[2,512]{1,0:T(2,128)S(1)} %shard_map.68.own_ref.own_in, s32[2,512]{1,0:T(2,128)S(1)} %collective-permute-done.6.other_ref.refs_0_, bf16[128,2048]{1,0:T(8,128)(2,1)S(1)} %collective-permute-done.8.refs_0_, ...), custom_call_target="tpu_custom_call" | custom-call | flops 1073741824 | bytes 5382144 | tf_op jit(solution)/shard_map/pallas_call | solution.py:39
  94.7 2.5 %shard_map.75 = (bf16[128,2048]{1,0:T(8,128)(2,1)S(1)}, bf16[128,2048]{1,0:T(8,128)(2,1)S(1)}, bf16[128,2048]{1,0:T(8,128)(2,1)S(1)}, bf16[128,2048]{1,0:T(8,128...) custom-call(s32[2,512]{1,0:T(2,128)S(1)} %shard_map.68.own_ref.own_i, ...), custom_call_target="tpu_custom_call" | custom-call | flops 1073741824 | bytes 9482752 | tf_op jit(solution)/shard_map/pallas_call | solution.py:39
  97.8 1.8 %collective-permute-start.22 = (f32[2,512]{1,0:T(2,128)S(1)}, f32[2,512]{1,0:T(2,128)S(1)}, u32[]{:S(2)}, u32[]{:S(2)}) collective-permute-start(f32[2,512]{1,0:T(2,128)S(1)} %get-tuple-element.56.refs_4_), channel_id=1, source_target_pairs={{0,2},{1,3},{2,4},{3,5},{4,6},{5,7},{6,0},{7,1},{8,10},{9,11},{10,... | collective-permute-start | bytes 12296 | tf_op jit(solution)/shard_map/ppermute | solution.py:354
  100.1 1.9 %collective-permute-start.24 = (f32[2,512]{1,0:T(2,128)S(1)}, f32[2,512]{1,0:T(2,128)S(1)}, u32[]{:S(2)}, u32[]{:S(2)}) collective-permute-start(f32[2,512]{1,0:T(2,128)S(1)} %get-tuple-element.56.refs_4_), channel_id=1, source_target_pairs={{0,6},{1,7},{2,0},{3,1},{4,2},{5,3},{6,4},{7,5},{8,14},{9,15},{10,... | collective-permute-start | bytes 12296 | tf_op jit(solution)/shard_map/ppermute | solution.py:354
  102.0 1.3 collective-permute-done.22.refs_5_
  104.5 3.4 %collective-permute-start.28 = (bf16[64,2048]{1,0:T(8,128)(2,1)S(1)}, bf16[64,2048]{1,0:T(8,128)(2,1)S(1)}, u32[]{:S(2)}, u32[]{:S(2)}) collective-permute-start(bf16[64,2048]{1,0:T(8,128)(2,1)S(1)} %get-tuple-element.68), channel_id=1, source_target_pairs={{0,6},{1,7},{2,0},{3,1},{4,2},{5,3},{6,4},{7,5},{8,14},{9,15},{10,... | collective-permute-start | bytes 786440 | tf_op jit(solution)/shard_map/ppermute | solution.py:354
  108.7 5.9 %collective-permute-done.28 = bf16[64,2048]{1,0:T(8,128)(2,1)S(1)} collective-permute-done((bf16[64,2048]{1,0:T(8,128)(2,1)S(1)}, bf16[64,2048]{1,0:T(8,128)(2,1)S(1)}, u32[]{:S(2)}, u32[]{:S(2)}) %collective-permute-start.28) | collective-permute-done | bytes 262176 | tf_op jit(solution)/shard_map/ppermute | solution.py:354
  114.7 4.3 %collective-permute-start.29 = (bf16[64,2048]{1,0:T(8,128)(2,1)S(1)}, bf16[64,2048]{1,0:T(8,128)(2,1)S(1)}, u32[]{:S(2)}, u32[]{:S(2)}) collective-permute-start(bf16[64,2048]{1,0:T(8,128)(2,1)S(1)} %add_convert_fusion.3), channel_id=1, source_target_pairs={{0,6},{1,7},{2,0},{3,1},{4,2},{5,3},{6,4},{7,5},{8,14},{9,15},{10,... | collective-permute-start | bytes 786440 | tf_op jit(solution)/shard_map/ppermute | solution.py:354
  119.0 1.2 collective-permute-done.25
  120.3 2.5 %collective-permute-start.26 = (bf16[64,2048]{1,0:T(8,128)(2,1)S(1)}, bf16[64,2048]{1,0:T(8,128)(2,1)S(1)}, u32[]{:S(2)}, u32[]{:S(2)}) collective-permute-start(bf16[64,2048]{1,0:T(8,128)(2,1)S(1)} %add_convert_fusion.5), channel_id=1, source_target_pairs={{0,2},{1,3},{2,4},{3,5},{4,6},{5,7},{6,0},{7,1},{8,10},{9,11},{10,... | collective-permute-start | bytes 786440 | tf_op jit(solution)/shard_map/ppermute | solution.py:354
  122.8 1.5 shard_map.86
  125.6 4.3 %collective-permute-start.30 = (bf16[64,2048]{1,0:T(8,128)(2,1)S(1)}, bf16[64,2048]{1,0:T(8,128)(2,1)S(1)}, u32[]{:S(2)}, u32[]{:S(2)}) collective-permute-start(bf16[64,2048]{1,0:T(8,128)(2,1)S(1)} %add_convert_fusion.2), channel_id=1, source_target_pairs={{0,6},{1,7},{2,0},{3,1},{4,2},{5,3},{6,4},{7,5},{8,14},{9,15},{10,... | collective-permute-start | bytes 786440 | tf_op jit(solution)/shard_map/ppermute | solution.py:354
  130.4 1.5 shard_map.84
  132.0 1.6 collective-permute-start.34
  133.5 1.5 shard_map.83
  135.1 1.5 collective-permute-done.35
  137.2 7.5 %collective-permute-done.37 = bf16[128,2048]{1,0:T(8,128)(2,1)S(1)} collective-permute-done((bf16[128,2048]{1,0:T(8,128)(2,1)S(1)}, bf16[128,2048]{1,0:T(8,128)(2,1)S(1)}, u32[]{:S(2)}, u32[]{:S(2)}) %collective-permute-start.37) | collective-permute-done | bytes 524320 | tf_op jit(solution)/shard_map/ppermute | solution.py:362
  146.3 2.4 %shard_map.80.w_ref = bf16[2048,2048]{1,0:T(8,128)(2,1)S(1)} custom-call(bf16[2048,2048]{1,0:T(8,128)(2,1)S(1)} %copy-done.1), custom_call_target="tpu_custom_call" | custom-call | flops 2048 | bytes 16777216 | tf_op jit(solution)/shard_map/pallas_call | solution.py:39
  148.8 5.7 %collective-permute-done.27.up_in_ref = bf16[64,2048]{1,0:T(8,128)(2,1)S(1)} collective-permute-done((bf16[64,2048]{1,0:T(8,128)(2,1)S(1)}, bf16[64,2048]{1,0:T(8,128)(2,1)S(1)}, u32[]{:S(2)}, u32[]{:S(2)}) %collective-permute-start.27) | collective-permute-done | bytes 262176 | tf_op jit(solution)/shard_map/ppermute | solution.py:354
  154.5 2.2 %shard_map.81 = bf16[128,2048]{1,0:T(8,128)(2,1)} custom-call(f32[64,2048]{1,0:T(8,128)S(1)} %get-tuple-element.61.up_ref, bf16[64,2048]{1,0:T(8,128)(2,1)S(1)} %collective-permute-done.27.up_in_ref, f32[64,2048]{1,0:T(8,128)S(1)} %get-tuple-element.65.down_ref, bf16[64,2048]{1,0:T(8,128)(2,1)S(1)} %collective-permute-done.30.down_in_ref, ...), custom_call_target="tpu_custom_call" | custom-call | flops 1073741824 | bytes 11534336 | tf_op jit(solution)/shard_map/pallas_call | solution.py:39
  156.7 1.5 shard_map.85
  158.2 4.4 %collective-permute-done.36 = bf16[128,2048]{1,0:T(8,128)(2,1)S(1)} collective-permute-done((bf16[128,2048]{1,0:T(8,128)(2,1)S(1)}, bf16[128,2048]{1,0:T(8,128)(2,1)S(1)}, u32[]{:S(2)}, u32[]{:S(2)}) %collective-permute-start.36) | collective-permute-done | bytes 524320 | tf_op jit(solution)/shard_map/ppermute | solution.py:362
  162.6 1.6 convert_add_fusion
  (69 shorter events, 15.8 us)
Async XLA Ops:
  0.6 47.9 %collective-permute-start.9 = (bf16[256,2048]{1,0:T(8,128)(2,1)}, bf16[256,2048]{1,0:T(8,128)(2,1)S(1)}, u32[]{:S(2)}, u32[]{:S(2)}) collective-permute-start(bf16[256,2048]{1,0:T(8,128)(2,1)} %refs_0_.1), channel_id=1, source_target_pairs={{0,8},{8,0},{16,24},{24,16},{1,9},{9,1},{17,25},{25,17},{2,10},{10... | collective-permute-start | bytes 3145736 | tf_op jit(solution)/shard_map/ppermute | solution.py:362
  3.7 44.9 %collective-permute-start.7 = (bf16[256,2048]{1,0:T(8,128)(2,1)}, bf16[256,2048]{1,0:T(8,128)(2,1)S(1)}, u32[]{:S(2)}, u32[]{:S(2)}) collective-permute-start(bf16[256,2048]{1,0:T(8,128)(2,1)} %refs_0_.1), channel_id=1, source_target_pairs={{0,16},{8,24},{16,0},{24,8},{1,17},{9,25},{17,1},{25,9},{2,18},{10... | collective-permute-start | bytes 3145736 | tf_op jit(solution)/shard_map/ppermute | solution.py:362
  6.3 38.4 %collective-permute-start.14 = (bf16[64,2048]{1,0:T(8,128)(2,1)S(1)}, bf16[64,2048]{1,0:T(8,128)(2,1)S(1)}, u32[]{:S(2)}, u32[]{:S(2)}) collective-permute-start(bf16[64,2048]{1,0:T(8,128)(2,1)S(1)} %get-tuple-element.79.x_up), channel_id=1, source_target_pairs={{0,2},{1,3},{2,4},{3,5},{4,6},{5,7},{6,0},{7,1},{8,10},{9,11},{10,... | collective-permute-start | bytes 786440 | tf_op jit(solution)/shard_map/ppermute | solution.py:354
  7.9 36.8 %collective-permute-start.15 = (bf16[64,2048]{1,0:T(8,128)(2,1)S(1)}, bf16[64,2048]{1,0:T(8,128)(2,1)S(1)}, u32[]{:S(2)}, u32[]{:S(2)}) collective-permute-start(bf16[64,2048]{1,0:T(8,128)(2,1)S(1)} %get-tuple-element.78.x_down), channel_id=1, source_target_pairs={{0,6},{1,7},{2,0},{3,1},{4,2},{5,3},{6,4},{7,5},{8,14},{9,15},{10,... | collective-permute-start | bytes 786440 | tf_op jit(solution)/shard_map/ppermute | solution.py:354
  10.1 11.2 %collective-permute-start = (s32[1,128]{1,0:T(1,128)}, s32[1,128]{1,0:T(1,128)S(1)}, u32[]{:S(2)}, u32[]{:S(2)}) collective-permute-start(s32[1,128]{1,0:T(1,128)} %bitcast.1), channel_id=1, source_target_pairs={{0,2},{1,3},{2,4},{3,5},{4,6},{5,7},{6,0},{7,1},{8,10},{9,11},{10,... | collective-permute-start | bytes 1544 | tf_op jit(solution)/shard_map/ppermute | solution.py:354
  21.3 4.6 %collective-permute-start.1 = (s32[1,128]{1,0:T(1,128)}, s32[1,128]{1,0:T(1,128)S(1)}, u32[]{:S(2)}, u32[]{:S(2)}) collective-permute-start(s32[1,128]{1,0:T(1,128)} %bitcast.2), channel_id=1, source_target_pairs={{0,4},{1,5},{2,6},{3,7},{4,0},{5,1},{6,2},{7,3},{8,12},{9,13},{10,... | collective-permute-start | bytes 1544 | tf_op jit(solution)/shard_map/ppermute | solution.py:354
  25.9 3.7 %collective-permute-start.2 = (s32[1,128]{1,0:T(1,128)}, s32[1,128]{1,0:T(1,128)S(1)}, u32[]{:S(2)}, u32[]{:S(2)}) collective-permute-start(s32[1,128]{1,0:T(1,128)} %bitcast.3), channel_id=1, source_target_pairs={{0,6},{1,7},{2,0},{3,1},{4,2},{5,3},{6,4},{7,5},{8,14},{9,15},{10,... | collective-permute-start | bytes 1544 | tf_op jit(solution)/shard_map/ppermute | solution.py:354
  29.6 3.8 %collective-permute-start.3 = (s32[4,32]{1,0:T(4,128)}, s32[4,32]{1,0:T(4,128)S(1)}, u32[]{:S(2)}, u32[]{:S(2)}) collective-permute-start(s32[4,32]{1,0:T(4,128)} %refs_4_.1), channel_id=1, source_target_pairs={{0,8},{8,0},{16,24},{24,16},{1,9},{9,1},{17,25},{25,17},{2,10},{10... | collective-permute-start | bytes 1544 | tf_op jit(solution)/shard_map/ppermute | solution.py:362
  33.4 3.8 %collective-permute-start.4 = (s32[4,32]{1,0:T(4,128)}, s32[4,32]{1,0:T(4,128)S(1)}, u32[]{:S(2)}, u32[]{:S(2)}) collective-permute-start(s32[4,32]{1,0:T(4,128)} %refs_4_.1), channel_id=1, source_target_pairs={{0,16},{8,24},{16,0},{24,8},{1,17},{9,25},{17,1},{25,9},{2,18},{10... | collective-permute-start | bytes 1544 | tf_op jit(solution)/shard_map/ppermute | solution.py:362
  37.2 4.7 %collective-permute-start.5 = (s32[4,32]{1,0:T(4,128)}, s32[4,32]{1,0:T(4,128)S(1)}, u32[]{:S(2)}, u32[]{:S(2)}) collective-permute-start(s32[4,32]{1,0:T(4,128)} %refs_4_.1), channel_id=1, source_target_pairs={{0,24},{8,16},{16,8},{24,0},{1,25},{9,17},{17,9},{25,1},{2,26},{10... | collective-permute-start | bytes 1544 | tf_op jit(solution)/shard_map/ppermute | solution.py:362
  41.9 0.7 copy-start.2
  42.6 0.7 copy-start.3
  43.3 1.2 collective-permute-start.6
  44.5 33.5 %collective-permute-start.13 = (bf16[256,2048]{1,0:T(8,128)(2,1)}, bf16[256,2048]{1,0:T(8,128)(2,1)S(1)}, u32[]{:S(2)}, u32[]{:S(2)}) collective-permute-start(bf16[256,2048]{1,0:T(8,128)(2,1)} %refs_0_.1), channel_id=1, source_target_pairs={{0,1},{1,0},{2,3},{3,2},{4,5},{5,4},{6,7},{7,6},{8,9},{9,8},{10,11... | collective-permute-start | bytes 3145736 | tf_op jit(solution)/shard_map/ppermute | solution.py:358
  44.7 11.0 %collective-permute-start.16 = (bf16[64,2048]{1,0:T(8,128)(2,1)S(1)}, bf16[64,2048]{1,0:T(8,128)(2,1)S(1)}, u32[]{:S(2)}, u32[]{:S(2)}) collective-permute-start(bf16[64,2048]{1,0:T(8,128)(2,1)S(1)} %collective-permute-done.14.x_up), channel_id=1, source_target_pairs={{0,2},{1,3},{2,4},{3,5},{4,6},{5,7},{6,0},{7,1},{8,10},{9,11},{10,... | collective-permute-start | bytes 786440 | tf_op jit(solution)/shard_map/ppermute | solution.py:354
  44.7 14.2 %collective-permute-start.17 = (bf16[64,2048]{1,0:T(8,128)(2,1)S(1)}, bf16[64,2048]{1,0:T(8,128)(2,1)S(1)}, u32[]{:S(2)}, u32[]{:S(2)}) collective-permute-start(bf16[64,2048]{1,0:T(8,128)(2,1)S(1)} %collective-permute-done.15.x_down), channel_id=1, source_target_pairs={{0,6},{1,7},{2,0},{3,1},{4,2},{5,3},{6,4},{7,5},{8,14},{9,15},{10,... | collective-permute-start | bytes 786440 | tf_op jit(solution)/shard_map/ppermute | solution.py:354
  48.5 40.6 %collective-permute-start.11 = (bf16[256,2048]{1,0:T(8,128)(2,1)S(1)}, bf16[256,2048]{1,0:T(8,128)(2,1)S(1)}, u32[]{:S(2)}, u32[]{:S(2)}) collective-permute-start(bf16[256,2048]{1,0:T(8,128)(2,1)S(1)} %collective-permute-done.9.refs_0_), channel_id=1, source_target_pairs={{0,1},{1,0},{2,3},{3,2},{4,5},{5,4},{6,7},{7,6},{8,9},{9,8},{10,11... | collective-permute-start | bytes 3145736 | tf_op jit(solution)/shard_map/ppermute | solution.py:358
  48.5 40.6 %collective-permute-start.12 = (bf16[256,2048]{1,0:T(8,128)(2,1)S(1)}, bf16[256,2048]{1,0:T(8,128)(2,1)S(1)}, u32[]{:S(2)}, u32[]{:S(2)}) collective-permute-start(bf16[256,2048]{1,0:T(8,128)(2,1)S(1)} %collective-permute-done.7.refs_1_), channel_id=1, source_target_pairs={{0,1},{1,0},{2,3},{3,2},{4,5},{5,4},{6,7},{7,6},{8,9},{9,8},{10,11... | collective-permute-start | bytes 3145736 | tf_op jit(solution)/shard_map/ppermute | solution.py:358
  55.7 13.9 %collective-permute-start.20 = (bf16[64,2048]{1,0:T(8,128)(2,1)S(1)}, bf16[64,2048]{1,0:T(8,128)(2,1)S(1)}, u32[]{:S(2)}, u32[]{:S(2)}) collective-permute-start(bf16[64,2048]{1,0:T(8,128)(2,1)S(1)} %collective-permute-done.16.x_up), channel_id=1, source_target_pairs={{0,2},{1,3},{2,4},{3,5},{4,6},{5,7},{6,0},{7,1},{8,10},{9,11},{10,... | collective-permute-start | bytes 786440 | tf_op jit(solution)/shard_map/ppermute | solution.py:354
  58.9 14.5 %collective-permute-start.21 = (bf16[64,2048]{1,0:T(8,128)(2,1)S(1)}, bf16[64,2048]{1,0:T(8,128)(2,1)S(1)}, u32[]{:S(2)}, u32[]{:S(2)}) collective-permute-start(bf16[64,2048]{1,0:T(8,128)(2,1)S(1)} %collective-permute-done.17.x_down), channel_id=1, source_target_pairs={{0,6},{1,7},{2,0},{3,1},{4,2},{5,3},{6,4},{7,5},{8,14},{9,15},{10,... | collective-permute-start | bytes 786440 | tf_op jit(solution)/shard_map/ppermute | solution.py:354
  62.4 3.4 %copy-start = (bf16[2048,2048]{1,0:T(8,128)(2,1)S(1)}, bf16[2048,2048]{1,0:T(8,128)(2,1)}, u32[]{:S(2)}) copy-start(bf16[2048,2048]{1,0:T(8,128)(2,1)} %w_ref.9) | copy-start | bytes 25165828
  65.8 8.1 %copy-start.1 = (bf16[2048,2048]{1,0:T(8,128)(2,1)S(1)}, bf16[2048,2048]{1,0:T(8,128)(2,1)}, u32[]{:S(2)}) copy-start(bf16[2048,2048]{1,0:T(8,128)(2,1)} %w_ref.9) | copy-start | bytes 25165828
  69.6 17.1 %collective-permute-start.10 = (bf16[128,2048]{1,0:T(8,128)(2,1)S(1)}, bf16[128,2048]{1,0:T(8,128)(2,1)S(1)}, u32[]{:S(2)}, u32[]{:S(2)}) collective-permute-start(bf16[128,2048]{1,0:T(8,128)(2,1)S(1)} %slice.17), channel_id=1, source_target_pairs={{0,16},{8,24},{16,0},{24,8},{1,17},{9,25},{17,1},{25,9},{2,18},{10... | collective-permute-start | bytes 1572872 | tf_op jit(solution)/shard_map/ppermute | solution.py:362
  73.4 13.3 %collective-permute-start.8 = (bf16[128,2048]{1,0:T(8,128)(2,1)S(1)}, bf16[128,2048]{1,0:T(8,128)(2,1)S(1)}, u32[]{:S(2)}, u32[]{:S(2)}) collective-permute-start(bf16[128,2048]{1,0:T(8,128)(2,1)S(1)} %slice.16), channel_id=1, source_target_pairs={{0,8},{8,0},{16,24},{24,16},{1,9},{9,1},{17,25},{25,17},{2,10},{10... | collective-permute-start | bytes 1572872 | tf_op jit(solution)/shard_map/ppermute | solution.py:362
  77.8 9.4 %copy-start.4 = (bf16[256,2048]{1,0:T(8,128)(2,1)S(1)}, bf16[256,2048]{1,0:T(8,128)(2,1)}, u32[]{:S(2)}) copy-start(bf16[256,2048]{1,0:T(8,128)(2,1)} %refs_0_.1) | copy-start | bytes 3145732
  78.0 44.8 %collective-permute-start.32 = (bf16[512,2048]{1,0:T(8,128)(2,1)S(1)}, bf16[512,2048]{1,0:T(8,128)(2,1)S(1)}, u32[]{:S(2)}, u32[]{:S(2)}) collective-permute-start(bf16[512,2048]{1,0:T(8,128)(2,1)S(1)} %shard_map.82.z_own), channel_id=1, source_target_pairs={{0,1},{1,0},{2,3},{3,2},{4,5},{5,4},{6,7},{7,6},{8,9},{9,8},{10,11... | collective-permute-start | bytes 6291464 | tf_op jit(solution)/shard_map/ppermute | solution.py:358
  86.7 8.0 %collective-permute-start.18 = (bf16[128,2048]{1,0:T(8,128)(2,1)S(1)}, bf16[128,2048]{1,0:T(8,128)(2,1)S(1)}, u32[]{:S(2)}, u32[]{:S(2)}) collective-permute-start(bf16[128,2048]{1,0:T(8,128)(2,1)S(1)} %collective-permute-done.8.refs_0_), channel_id=1, source_target_pairs={{0,1},{1,0},{2,3},{3,2},{4,5},{5,4},{6,7},{7,6},{8,9},{9,8},{10,11... | collective-permute-start | bytes 1572872 | tf_op jit(solution)/shard_map/ppermute | solution.py:358
  86.7 8.0 %collective-permute-start.19 = (bf16[128,2048]{1,0:T(8,128)(2,1)S(1)}, bf16[128,2048]{1,0:T(8,128)(2,1)S(1)}, u32[]{:S(2)}, u32[]{:S(2)}) collective-permute-start(bf16[128,2048]{1,0:T(8,128)(2,1)S(1)} %collective-permute-done.10.refs_1_), channel_id=1, source_target_pairs={{0,1},{1,0},{2,3},{3,2},{4,5},{5,4},{6,7},{7,6},{8,9},{9,8},{10,11... | collective-permute-start | bytes 1572872 | tf_op jit(solution)/shard_map/ppermute | solution.py:358
  97.8 5.5 %collective-permute-start.22 = (f32[2,512]{1,0:T(2,128)S(1)}, f32[2,512]{1,0:T(2,128)S(1)}, u32[]{:S(2)}, u32[]{:S(2)}) collective-permute-start(f32[2,512]{1,0:T(2,128)S(1)} %get-tuple-element.56.refs_4_), channel_id=1, source_target_pairs={{0,2},{1,3},{2,4},{3,5},{4,6},{5,7},{6,0},{7,1},{8,10},{9,11},{10,... | collective-permute-start | bytes 12296 | tf_op jit(solution)/shard_map/ppermute | solution.py:354
  99.5 4.5 %collective-permute-start.23 = (f32[2,512]{1,0:T(2,128)S(1)}, f32[2,512]{1,0:T(2,128)S(1)}, u32[]{:S(2)}, u32[]{:S(2)}) collective-permute-start(f32[2,512]{1,0:T(2,128)S(1)} %get-tuple-element.56.refs_4_), channel_id=1, source_target_pairs={{0,4},{1,5},{2,6},{3,7},{4,0},{5,1},{6,2},{7,3},{8,12},{9,13},{10,... | collective-permute-start | bytes 12296 | tf_op jit(solution)/shard_map/ppermute | solution.py:354
  100.1 3.9 %collective-permute-start.24 = (f32[2,512]{1,0:T(2,128)S(1)}, f32[2,512]{1,0:T(2,128)S(1)}, u32[]{:S(2)}, u32[]{:S(2)}) collective-permute-start(f32[2,512]{1,0:T(2,128)S(1)} %get-tuple-element.56.refs_4_), channel_id=1, source_target_pairs={{0,6},{1,7},{2,0},{3,1},{4,2},{5,3},{6,4},{7,5},{8,14},{9,15},{10,... | collective-permute-start | bytes 12296 | tf_op jit(solution)/shard_map/ppermute | solution.py:354
  104.5 10.1 %collective-permute-start.28 = (bf16[64,2048]{1,0:T(8,128)(2,1)S(1)}, bf16[64,2048]{1,0:T(8,128)(2,1)S(1)}, u32[]{:S(2)}, u32[]{:S(2)}) collective-permute-start(bf16[64,2048]{1,0:T(8,128)(2,1)S(1)} %get-tuple-element.68), channel_id=1, source_target_pairs={{0,6},{1,7},{2,0},{3,1},{4,2},{5,3},{6,4},{7,5},{8,14},{9,15},{10,... | collective-permute-start | bytes 786440 | tf_op jit(solution)/shard_map/ppermute | solution.py:354
  107.9 15.0 %collective-permute-start.31 = (bf16[144,512]{1,0:T(8,128)(2,1)S(1)}, bf16[144,512]{1,0:T(8,128)(2,1)S(1)}, u32[]{:S(2)}, u32[]{:S(2)}) collective-permute-start(bf16[144,512]{1,0:T(8,128)(2,1)S(1)} %get-tuple-element.71), channel_id=1, source_target_pairs={{0,1},{1,0},{2,3},{3,2},{4,5},{5,4},{6,7},{7,6},{8,9},{9,8},{10,11... | collective-permute-start | bytes 442376 | tf_op jit(solution)/shard_map/ppermute | solution.py:358
  107.9 12.4 %collective-permute-start.25 = (bf16[64,2048]{1,0:T(8,128)(2,1)S(1)}, bf16[64,2048]{1,0:T(8,128)(2,1)S(1)}, u32[]{:S(2)}, u32[]{:S(2)}) collective-permute-start(bf16[64,2048]{1,0:T(8,128)(2,1)S(1)} %get-tuple-element.64), channel_id=1, source_target_pairs={{0,2},{1,3},{2,4},{3,5},{4,6},{5,7},{6,0},{7,1},{8,10},{9,11},{10,... | collective-permute-start | bytes 786440 | tf_op jit(solution)/shard_map/ppermute | solution.py:354
  114.7 10.8 %collective-permute-start.29 = (bf16[64,2048]{1,0:T(8,128)(2,1)S(1)}, bf16[64,2048]{1,0:T(8,128)(2,1)S(1)}, u32[]{:S(2)}, u32[]{:S(2)}) collective-permute-start(bf16[64,2048]{1,0:T(8,128)(2,1)S(1)} %add_convert_fusion.3), channel_id=1, source_target_pairs={{0,6},{1,7},{2,0},{3,1},{4,2},{5,3},{6,4},{7,5},{8,14},{9,15},{10,... | collective-permute-start | bytes 786440 | tf_op jit(solution)/shard_map/ppermute | solution.py:354
  120.3 25.1 %collective-permute-start.26 = (bf16[64,2048]{1,0:T(8,128)(2,1)S(1)}, bf16[64,2048]{1,0:T(8,128)(2,1)S(1)}, u32[]{:S(2)}, u32[]{:S(2)}) collective-permute-start(bf16[64,2048]{1,0:T(8,128)(2,1)S(1)} %add_convert_fusion.5), channel_id=1, source_target_pairs={{0,2},{1,3},{2,4},{3,5},{4,6},{5,7},{6,0},{7,1},{8,10},{9,11},{10,... | collective-permute-start | bytes 786440 | tf_op jit(solution)/shard_map/ppermute | solution.py:354
  124.4 12.2 %collective-permute-start.35 = (bf16[128,2048]{1,0:T(8,128)(2,1)S(1)}, bf16[128,2048]{1,0:T(8,128)(2,1)S(1)}, u32[]{:S(2)}, u32[]{:S(2)}) collective-permute-start(bf16[128,2048]{1,0:T(8,128)(2,1)S(1)} %get-tuple-element.75), channel_id=1, source_target_pairs={{0,8},{8,0},{16,24},{24,16},{1,9},{9,1},{17,25},{25,17},{2,10},{10... | collective-permute-start | bytes 1572872 | tf_op jit(solution)/shard_map/ppermute | solution.py:362
  125.6 20.5 %collective-permute-start.30 = (bf16[64,2048]{1,0:T(8,128)(2,1)S(1)}, bf16[64,2048]{1,0:T(8,128)(2,1)S(1)}, u32[]{:S(2)}, u32[]{:S(2)}) collective-permute-start(bf16[64,2048]{1,0:T(8,128)(2,1)S(1)} %add_convert_fusion.2), channel_id=1, source_target_pairs={{0,6},{1,7},{2,0},{3,1},{4,2},{5,3},{6,4},{7,5},{8,14},{9,15},{10,... | collective-permute-start | bytes 786440 | tf_op jit(solution)/shard_map/ppermute | solution.py:354
  129.9 14.8 %collective-permute-start.37 = (bf16[128,2048]{1,0:T(8,128)(2,1)S(1)}, bf16[128,2048]{1,0:T(8,128)(2,1)S(1)}, u32[]{:S(2)}, u32[]{:S(2)}) collective-permute-start(bf16[128,2048]{1,0:T(8,128)(2,1)S(1)} %get-tuple-element.77), channel_id=1, source_target_pairs={{0,16},{8,24},{16,0},{24,8},{1,17},{9,25},{17,1},{25,9},{2,18},{10... | collective-permute-start | bytes 1572872 | tf_op jit(solution)/shard_map/ppermute | solution.py:362
  132.0 24.7 %collective-permute-start.34 = (bf16[128,2048]{1,0:T(8,128)(2,1)S(1)}, bf16[128,2048]{1,0:T(8,128)(2,1)S(1)}, u32[]{:S(2)}, u32[]{:S(2)}) collective-permute-start(bf16[128,2048]{1,0:T(8,128)(2,1)S(1)} %get-tuple-element.73), channel_id=1, source_target_pairs={{0,16},{8,24},{16,0},{24,8},{1,17},{9,25},{17,1},{25,9},{2,18},{10... | collective-permute-start | bytes 1572872 | tf_op jit(solution)/shard_map/ppermute | solution.py:362
  136.5 20.2 %collective-permute-start.33 = (bf16[128,2048]{1,0:T(8,128)(2,1)S(1)}, bf16[128,2048]{1,0:T(8,128)(2,1)S(1)}, u32[]{:S(2)}, u32[]{:S(2)}) collective-permute-start(bf16[128,2048]{1,0:T(8,128)(2,1)S(1)} %get-tuple-element.72), channel_id=1, source_target_pairs={{0,8},{8,0},{16,24},{24,16},{1,9},{9,1},{17,25},{25,17},{2,10},{10... | collective-permute-start | bytes 1572872 | tf_op jit(solution)/shard_map/ppermute | solution.py:362
  144.7 17.9 %collective-permute-start.36 = (bf16[128,2048]{1,0:T(8,128)(2,1)S(1)}, bf16[128,2048]{1,0:T(8,128)(2,1)S(1)}, u32[]{:S(2)}, u32[]{:S(2)}) collective-permute-start(bf16[128,2048]{1,0:T(8,128)(2,1)S(1)} %add_convert_fusion.1), channel_id=1, source_target_pairs={{0,16},{8,24},{16,0},{24,8},{1,17},{9,25},{17,1},{25,9},{2,18},{10... | collective-permute-start | bytes 1572872 | tf_op jit(solution)/shard_map/ppermute | solution.py:362
  145.4 17.2 %collective-permute-start.38 = (bf16[128,2048]{1,0:T(8,128)(2,1)S(1)}, bf16[128,2048]{1,0:T(8,128)(2,1)S(1)}, u32[]{:S(2)}, u32[]{:S(2)}) collective-permute-start(bf16[128,2048]{1,0:T(8,128)(2,1)S(1)} %add_convert_fusion), channel_id=1, source_target_pairs={{0,8},{8,0},{16,24},{24,16},{1,9},{9,1},{17,25},{25,17},{2,10},{10... | collective-permute-start | bytes 1572872 | tf_op jit(solution)/shard_map/ppermute | solution.py:362
  146.0 8.4 %collective-permute-start.27 = (bf16[64,2048]{1,0:T(8,128)(2,1)S(1)}, bf16[64,2048]{1,0:T(8,128)(2,1)S(1)}, u32[]{:S(2)}, u32[]{:S(2)}) collective-permute-start(bf16[64,2048]{1,0:T(8,128)(2,1)S(1)} %add_convert_fusion.4), channel_id=1, source_target_pairs={{0,2},{1,3},{2,4},{3,5},{4,6},{5,7},{6,0},{7,1},{8,10},{9,11},{10,... | collective-permute-start | bytes 786440 | tf_op jit(solution)/shard_map/ppermute | solution.py:354
